TPU v7x, 128 devices: a whole 4x4x4 slice. The times are simulated.
128 devices in a mesh: gx: 8 (over z, x_hi), gy: 16 (over x_lo, y, core).
Axes of the slice: x: 4 (x_hi: 2, x_lo: 2; x = x_hi * 2 + x_lo), y: 4, z: 4, core: 2. Of those that a mesh axis runs over, the one named last changes fastest.
Arguments:
- source_planes: float32 [384, 384, 384], P(('gx', 'gy')), may hold values from -6 to 6
- weight_x: float32 [64, 384], replicated, may hold values from -0.3125 to 0.3125
- weight_y: float32 [96, 384], replicated, may hold values from -0.3125 to 0.3125
- weight_z: float32 [96, 384], replicated, may hold values from -0.3125 to 0.3125
- box_anchor: int32 [3], replicated, may hold values from 0 to 416, as said below
- velocity: float32 [3, 192, 512, 320], P(None, 'gx', 'gy'), may hold values from -6 to 6
- stress: float32 [6, 192, 512, 320], P(None, 'gx', 'gy'), may hold values from -6 to 6
- lame_lambda: float32 [192, 512, 320], P('gx', 'gy'), may hold values from 0.2 to 1
- lame_mu: float32 [192, 512, 320], P('gx', 'gy'), may hold values from 0.2 to 1
- buoyancy: float32 [192, 512, 320], P('gx', 'gy'), may hold values from 0.5 to 1.5
- attenuation: float32 [192, 512, 320], P('gx', 'gy'), may hold values from 0.05 to 3
Outputs:
- velocity_out: float32 [3, 192, 512, 320], P(None, 'gx', 'gy')
- stress_out: float32 [6, 192, 512, 320], P(None, 'gx', 'gy')
Inputs may be any that keep to these rules, and one draw needn't show every extreme that they name: The box of 64 x 96 x 96 cells that starts at box_anchor lies inside the thorax grid; along the dimension with the most room it ends at the grid's far side, along one of the other two it starts at cell 0.
All inputs are finite; a program needn't handle non-finite values.
Results may differ from a plain program's by a relative error of at most 0.00005.
Values sent between devices are 32-bit elements; how exact they have to be, the bound alone decides.
No kernel may reach another device: no remote copies, remote signals or barrier semaphores. Data moves between devices by JAX's collectives and lax.ppermute only.
A program may use at most 128 MiB of HBM per device.

v0:
```python
import jax
import jax.numpy as jnp
from jax import lax
from jax.sharding import PartitionSpec as P

STEPS = 2


time_step = 0.2
precise = lax.Precision.HIGHEST


def from_behind(value, axis, by):
    size = lax.axis_size(axis)
    pairs = [(i, i + by) for i in range(size) if 0 <= i + by < size]
    return lax.ppermute(value, axis, pairs)


def back_diff(values, dimension, beside):
    count = values.shape[dimension]
    return values - jnp.concatenate(
        [beside, lax.slice_in_dim(values, 0, count - 1, axis=dimension)], dimension
    )


def ahead_diff(values, dimension, beside):
    count = values.shape[dimension]
    return (
        jnp.concatenate([lax.slice_in_dim(values, 1, count, axis=dimension), beside], dimension)
        - values
    )


def one_hot(anchor, amount, box_start, extent):
    positions = anchor + lax.iota(jnp.int32, amount) - box_start
    return (positions[:, None] == lax.iota(jnp.int32, extent)[None, :]).astype(jnp.float32)


def shards(
    source_planes,
    weight_x,
    weight_y,
    weight_z,
    box_anchor,
    velocity,
    stress,
    lame_lambda,
    lame_mu,
    buoyancy,
    attenuation,
):
    rows_x = velocity.shape[1]
    rows_y = velocity.shape[2]
    cells_z = velocity.shape[3]
    box_x = weight_x.shape[0]
    box_y = weight_y.shape[0]
    box_z = weight_z.shape[0]
    reduced = jnp.einsum("abc,zc->abz", source_planes, weight_z, precision=precise)
    reduced = jnp.einsum("abz,yb->ayz", reduced, weight_y, precision=precise)
    own_planes = reduced.shape[0]
    own_start = lax.axis_index(("gx", "gy")) * own_planes
    weight_own = lax.dynamic_slice_in_dim(weight_x, own_start, own_planes, 1)
    partial_box = jnp.einsum("xa,ayz->xyz", weight_own, reduced, precision=precise)
    whole_box = lax.psum(partial_box, ("gx", "gy"))
    place_x = one_hot(lax.axis_index("gx") * rows_x, rows_x, box_anchor[0], box_x)
    box_rows = jnp.einsum("Xx,xyz->Xyz", place_x, whole_box, precision=precise)
    place_y = one_hot(lax.axis_index("gy") * rows_y, rows_y, box_anchor[1], box_y)
    place_z = one_hot(0, cells_z, box_anchor[2], box_z)
    pressure = jnp.einsum("xyz,Yy->xYz", box_rows, place_y, precision=precise)
    pressure = jnp.einsum("xYz,Zz->xYZ", pressure, place_z, precision=precise)
    decay = jnp.exp(-time_step * attenuation)
    zero_z = jnp.zeros((rows_x, rows_y, 1), jnp.float32)
    speed_x, speed_y, speed_z = (velocity[0], velocity[1], velocity[2])
    stress_xx, stress_yy, stress_zz = (stress[0], stress[1], stress[2])
    stress_xy, stress_xz, stress_yz = (stress[3], stress[4], stress[5])
    for stepping in range(STEPS):
        lower_x = from_behind(jnp.stack([stress_xx[-1], stress_xy[-1], stress_xz[-1]]), "gx", 1)
        lower_y = from_behind(
            jnp.stack([stress_xy[:, -1], stress_yy[:, -1], stress_yz[:, -1]]), "gy", 1
        )
        speed_x = speed_x + time_step * buoyancy * (
            back_diff(stress_xx, 0, lower_x[0][None])
            + back_diff(stress_xy, 1, lower_y[0][:, None])
            + back_diff(stress_xz, 2, zero_z)
        )
        speed_y = speed_y + time_step * buoyancy * (
            back_diff(stress_xy, 0, lower_x[1][None])
            + back_diff(stress_yy, 1, lower_y[1][:, None])
            + back_diff(stress_yz, 2, zero_z)
        )
        speed_z = speed_z + time_step * buoyancy * (
            back_diff(stress_xz, 0, lower_x[2][None])
            + back_diff(stress_yz, 1, lower_y[2][:, None])
            + back_diff(stress_zz, 2, zero_z)
        )
        upper_x = from_behind(jnp.stack([speed_x[0], speed_y[0], speed_z[0]]), "gx", -1)
        upper_y = from_behind(jnp.stack([speed_x[:, 0], speed_y[:, 0], speed_z[:, 0]]), "gy", -1)
        strain_xx = ahead_diff(speed_x, 0, upper_x[0][None])
        strain_yy = ahead_diff(speed_y, 1, upper_y[1][:, None])
        strain_zz = ahead_diff(speed_z, 2, zero_z)
        trace = strain_xx + strain_yy + strain_zz
        shear_xy = ahead_diff(speed_x, 1, upper_y[0][:, None]) + ahead_diff(
            speed_y, 0, upper_x[1][None]
        )
        shear_xz = ahead_diff(speed_x, 2, zero_z) + ahead_diff(speed_z, 0, upper_x[2][None])
        shear_yz = ahead_diff(speed_y, 2, zero_z) + ahead_diff(speed_z, 1, upper_y[2][:, None])
        stress_xx = decay * (
            stress_xx
            + time_step * (lame_lambda * trace + 2.0 * lame_mu * strain_xx)
            - time_step * pressure
        )
        stress_yy = decay * (
            stress_yy
            + time_step * (lame_lambda * trace + 2.0 * lame_mu * strain_yy)
            - time_step * pressure
        )
        stress_zz = decay * (
            stress_zz
            + time_step * (lame_lambda * trace + 2.0 * lame_mu * strain_zz)
            - time_step * pressure
        )
        stress_xy = decay * (stress_xy + time_step * lame_mu * shear_xy)
        stress_xz = decay * (stress_xz + time_step * lame_mu * shear_xz)
        stress_yz = decay * (stress_yz + time_step * lame_mu * shear_yz)
    velocity_out = jnp.stack([speed_x, speed_y, speed_z])
    stress_out = jnp.stack([stress_xx, stress_yy, stress_zz, stress_xy, stress_xz, stress_yz])
    return (velocity_out, stress_out)


def solution(mesh):
    in_specs = (
        P(("gx", "gy"), None, None),
        P(),
        P(),
        P(),
        P(),
        P(None, "gx", "gy", None),
        P(None, "gx", "gy", None),
        P("gx", "gy", None),
        P("gx", "gy", None),
        P("gx", "gy", None),
        P("gx", "gy", None),
    )
    out_specs = (P(None, "gx", "gy", None), P(None, "gx", "gy", None))
    return jax.shard_map(shards, mesh=mesh, in_specs=in_specs, out_specs=out_specs, check_vma=False)
```

profile of v0, /device:TPU:57, one launch (start us, length us, event | category | flops | bytes accessed | tf_op | source)
XLA Modules:
  0.0 257.5 jit_solution(14584826044277785940)
XLA Ops:
  7.2 4.8 %slice_bitcast_fusion.1 = (f32[24,32,320]{2,1,0:T(8,128)}, f32[24,32,320]{2,1,0:T(8,128)S(1)}, f32[24,32,320]{2,1,0:T(8,128)S(1)}, f32[24,32,320]{2,1,0:T(8,128)S(1)}, f32[24,32,320]{2,1,0:T(8,128)}) fusion(f32[6,24,32,320]{3,2,1,0:T(8,128)} %param.17), kind=kLoop, calls=%fused_computation.98 | loop fusion | bytes 9830400 | tf_op jit(solution)/shard_map/squeeze | solution.py:75
  13.6 3.3 %collective-permute-start.1 = (f32[3,24,320]{2,0,1:T(4,128)S(1)}, f32[3,24,320]{2,0,1:T(4,128)}, u32[]{:S(2)}, u32[]{:S(2)}) collective-permute-start(f32[3,24,320]{2,0,1:T(4,128)S(1)} %pad_maximum_fusion.2), channel_id=1, source_target_pairs={{0,1},{1,2},{2,3},{3,4},{4,5},{5,6},{6,7},{7,8},{8,9},{9,10},{10,1... | collective-permute-start | bytes 276488 | tf_op jit(solution)/shard_map/ppermute | solution.py:16
  17.8 4.4 %collective-permute-start = (f32[3,32,320]{2,1,0:T(8,128)S(1)}, f32[3,32,320]{2,1,0:T(8,128)S(1)}, u32[]{:S(2)}, u32[]{:S(2)}) collective-permute-start(f32[3,32,320]{2,1,0:T(8,128)S(1)} %pad_maximum_fusion.1), channel_id=1, source_target_pairs={{0,16},{16,32},{32,48},{48,64},{64,80},{80,96},{96,112},{1,17},{17... | collective-permute-start | bytes 368648 | tf_op jit(solution)/shard_map/ppermute | solution.py:16
  22.2 1.6 fusion.60
  25.1 3.5 %fusion.65 = f32[64,96,96]{2,0,1:T(8,128)S(1)} fusion(f32[3,96,96]{2,0,1:T(4,128)S(1)} %copy.13, f32[64,384]{1,0:T(8,128)} %param.12, s32[]{:T(128)S(6)} %select_n.3), kind=kOutput, calls=%fused_computation.147 | convolution fusion | flops 21233664 | bytes 2502660 | tf_op jit(solution)/shard_map/xa,ayz->xyz/dot_general | solution.py:63
  28.6 3.5 %copy.14 = f32[64,96,96]{2,1,0:T(8,128)} copy(f32[64,96,96]{2,0,1:T(8,128)S(1)} %fusion.65) | data formatting | bytes 4718592 | tf_op jit(solution)/shard_map/xa,ayz->xyz/dot_general | solution.py:63
  32.1 3.9 %slice_bitcast_fusion.7 = (f32[23,32,320]{2,1,0:T(8,128)}, f32[23,32,320]{2,1,0:T(8,128)}, f32[23,32,320]{2,1,0:T(8,128)}) fusion(f32[6,24,32,320]{3,2,1,0:T(8,128)} %param.17), kind=kLoop, calls=%fused_computation.105 | loop fusion | bytes 5652480 | tf_op jit(solution)/shard_map/slice | solution.py:22
  40.0 6.5 %fusion.5 = (f32[24,32,320]{2,1,0:T(8,128)S(1)}, f32[24,32,320]{2,1,0:T(8,128)S(1)}) fusion(f32[23,32,320]{2,1,0:T(8,128)} %get-tuple-element.17, f32[1,32,320]{2,1,0:T(8,128)S(1)} %get-tuple-element.46, f32[24,31,320]{2,1,0:T(8,128)} %bitcast.189, f32[24,1,320]{2,1,0:T(1,128)S(1)} %get-tuple-element.43, f32[24,32,319]{2,1,0:T(8,128)} %bitcast.190, ...), kind=kLoop, calls=%fused_computation.9 | loop fusion | flops 4669440 | bytes 15722496 | tf_op jit(solution)/shard_map/add | solution.py:81
  49.0 2.4 fusion.9
  52.7 1.4 slice.439
  56.5 1.4 slice.454
  59.7 2.1 collective-permute-start.3
  61.8 3.4 %collective-permute-start.2 = (f32[3,32,320]{2,1,0:T(8,128)S(1)}, f32[3,32,320]{2,1,0:T(8,128)S(1)}, u32[]{:S(2)}, u32[]{:S(2)}) collective-permute-start(f32[3,32,320]{2,1,0:T(8,128)S(1)} %pad_maximum_fusion.3), channel_id=1, source_target_pairs={{16,0},{32,16},{48,32},{64,48},{80,64},{96,80},{112,96},{17,1},{33... | collective-permute-start | bytes 368648 | tf_op jit(solution)/shard_map/ppermute | solution.py:16
  65.2 4.6 %collective-permute-done.3 = f32[3,24,320]{2,0,1:T(4,128)S(1)} collective-permute-done((f32[3,24,320]{2,0,1:T(4,128)S(1)}, f32[3,24,320]{2,0,1:T(4,128)S(1)}, u32[]{:S(2)}, u32[]{:S(2)}) %collective-permute-start.3) | collective-permute-done | bytes 92192 | tf_op jit(solution)/shard_map/ppermute | solution.py:16
  73.0 111.7 %all-reduce.14.cloned.1.call-done = f32[64,96,96]{2,1,0:T(8,128)} async-done(((f32[64,96,96]{2,1,0:T(8,128)}), f32[64,96,96]{2,1,0:T(8,128)}) %all-reduce.14.cloned.1.call-update) | async-done | bytes 2359312 | tf_op jit(solution)/shard_map/psum | solution.py:64
  184.6 4.9 %fusion = f32[24,96,96]{2,0,1:T(8,128)S(1)} fusion(f32[64,96,96]{2,1,0:T(8,128)} %all-reduce.14.cloned.1.call-done, s32[24]{0:T(128)S(1)} %add_subtract_fusion), kind=kOutput, calls=%fused_computation.1 | convolution fusion | flops 169870848 | bytes 3244128 | tf_op jit(solution)/shard_map/Xx,xyz->Xyz/dot_general | solution.py:66
  190.8 5.2 %subtract_multiply_fusion = (f32[24,32,320]{2,1,0:T(8,128)}, f32[24,32,320]{2,1,0:T(8,128)S(1)}, f32[24,32,320]{2,1,0:T(8,128)S(1)}, f32[24,32,320]{2,1,0:T(8,128)S(1)}) fusion(f32[24,32,320]{2,1,0:T(8,128)S(1)} %copy-done.2, f32[24,32,320]{2,1,0:T(8,128)S(1)} %copy-done.8, f32[24,32,319]{2,1,0:T(8,128)} %slice.439, f32[6,24,32,320]{3,2,1,0:T(8,128)} %param.17, ...), kind=kOutput, calls=%fused_computation.92 | convolution fusion | flops 289290240 | bytes 17001728 | tf_op jit(solution)/shard_map/xYz,Zz->xYZ/dot_general | solution.py:70
  196.4 2.2 subtract_multiply_fusion.1
  200.9 3.3 %collective-permute-start.5 = (f32[3,24,320]{2,0,1:T(4,128)S(1)}, f32[3,24,320]{2,0,1:T(4,128)S(1)}, u32[]{:S(2)}, u32[]{:S(2)}) collective-permute-start(f32[3,24,320]{2,0,1:T(4,128)S(1)} %pad_maximum_fusion.6), channel_id=1, source_target_pairs={{0,1},{1,2},{2,3},{3,4},{4,5},{5,6},{6,7},{7,8},{8,9},{9,10},{10,1... | collective-permute-start | bytes 276488 | tf_op jit(solution)/shard_map/ppermute | solution.py:16
  204.3 4.8 %collective-permute-start.4 = (f32[3,32,320]{2,1,0:T(8,128)S(1)}, f32[3,32,320]{2,1,0:T(8,128)S(1)}, u32[]{:S(2)}, u32[]{:S(2)}) collective-permute-start(f32[3,32,320]{2,1,0:T(8,128)S(1)} %pad_maximum_fusion.5), channel_id=1, source_target_pairs={{0,16},{16,32},{32,48},{48,64},{64,80},{80,96},{96,112},{1,17},{17... | collective-permute-start | bytes 368648 | tf_op jit(solution)/shard_map/ppermute | solution.py:16
  209.2 4.5 %collective-permute-done.4 = f32[3,32,320]{2,1,0:T(8,128)S(1)} collective-permute-done((f32[3,32,320]{2,1,0:T(8,128)S(1)}, f32[3,32,320]{2,1,0:T(8,128)S(1)}, u32[]{:S(2)}, u32[]{:S(2)}) %collective-permute-start.4) | collective-permute-done | bytes 122912 | tf_op jit(solution)/shard_map/ppermute | solution.py:16
  215.0 5.1 %fusion.25 = (f32[24,32,320]{2,1,0:T(8,128)S(1)}, f32[24,32,320]{2,1,0:T(8,128)S(1)}) fusion(f32[24,32,320]{2,1,0:T(8,128)S(1)} %copy-done.6, f32[24,32,320]{2,1,0:T(8,128)} %copy-done.16, f32[23,32,320]{2,1,0:T(8,128)} %slice.451, f32[1,32,320]{2,1,0:T(8,128)S(1)} %get-tuple-element.34, f32[24,32,320]{2,1,0:T(8,128)S(1)} %get-tuple-element.8, ...), kind=kLoop, calls=%fused_computation.40 | loop fusion | flops 4669440 | bytes 15722496 | tf_op jit(solution)/shard_map/add | solution.py:81
  224.1 2.2 collective-permute-start.7
  226.4 2.1 pad_maximum_fusion
  228.5 4.6 %collective-permute-start.6 = (f32[3,32,320]{2,1,0:T(8,128)S(1)}, f32[3,32,320]{2,1,0:T(8,128)S(1)}, u32[]{:S(2)}, u32[]{:S(2)}) collective-permute-start(f32[3,32,320]{2,1,0:T(8,128)S(1)} %pad_maximum_fusion.7), channel_id=1, source_target_pairs={{16,0},{32,16},{48,32},{64,48},{80,64},{96,80},{112,96},{17,1},{33... | collective-permute-start | bytes 368648 | tf_op jit(solution)/shard_map/ppermute | solution.py:16
  233.2 3.7 %collective-permute-done.6 = f32[3,32,320]{2,1,0:T(8,128)S(1)} collective-permute-done((f32[3,32,320]{2,1,0:T(8,128)S(1)}, f32[3,32,320]{2,1,0:T(8,128)S(1)}, u32[]{:S(2)}, u32[]{:S(2)}) %collective-permute-start.6) | collective-permute-done | bytes 122912 | tf_op jit(solution)/shard_map/ppermute | solution.py:16
  236.9 3.8 %bitcast_dynamic-update-slice_fusion.2 = (f32[6,24,32,320]{3,2,1,0:T(8,128)}, f32[24,32,320]{2,1,0:T(8,128)S(1)}) fusion(f32[24,32,320]{2,1,0:T(8,128)S(1)} %get-tuple-element.52, f32[24,32,320]{2,1,0:T(8,128)S(1)} %copy-done.17, f32[24,32,320]{2,1,0:T(8,128)S(1)} %copy-done.2, f32[24,32,320]{2,1,0:T(8,128)S(1)} %get-tuple-element.23, ...), kind=kLoop, calls=%fused_computation.85 | loop fusion | flops 3932159 | bytes 12973056
  240.8 2.0 bitcast_dynamic-update-slice_fusion.1
  242.8 2.0 bitcast_dynamic-update-slice_fusion
  244.7 2.0 fusion.43
  246.7 2.0 fusion.49
  248.7 2.0 fusion.55
  (144 shorter events, 27.9 us)
Async XLA Ops:
  7.2 15.0 %copy-start = (f32[3,384,384]{2,1,0:T(8,128)S(1)}, f32[3,384,384]{2,1,0:T(8,128)}, u32[]{:S(2)}) copy-start(f32[3,384,384]{2,1,0:T(8,128)} %param.11) | copy-start | bytes 5308420
  7.2 177.5 %all-reduce.14.cloned.1.call-start = ((), (), s32[]{:S(2)}) async-start(), calls=%async_computation | async-start | bytes 6291456 | tf_op jit(solution)/shard_map/psum | solution.py:64
  12.0 10.1 %copy-start.27 = (f32[96,384]{1,0:T(8,128)S(1)}, f32[96,384]{1,0:T(8,128)}, u32[]{:S(2)}) copy-start(f32[96,384]{1,0:T(8,128)} %param.14) | copy-start | bytes 442372
  13.6 25.2 %collective-permute-start.1 = (f32[3,24,320]{2,0,1:T(4,128)S(1)}, f32[3,24,320]{2,0,1:T(4,128)}, u32[]{:S(2)}, u32[]{:S(2)}) collective-permute-start(f32[3,24,320]{2,0,1:T(4,128)S(1)} %pad_maximum_fusion.2), channel_id=1, source_target_pairs={{0,1},{1,2},{2,3},{3,4},{4,5},{5,6},{6,7},{7,8},{8,9},{9,10},{10,1... | collective-permute-start | bytes 276488 | tf_op jit(solution)/shard_map/ppermute | solution.py:16
  17.8 22.1 %collective-permute-start = (f32[3,32,320]{2,1,0:T(8,128)S(1)}, f32[3,32,320]{2,1,0:T(8,128)S(1)}, u32[]{:S(2)}, u32[]{:S(2)}) collective-permute-start(f32[3,32,320]{2,1,0:T(8,128)S(1)} %pad_maximum_fusion.1), channel_id=1, source_target_pairs={{0,16},{16,32},{32,48},{48,64},{64,80},{80,96},{96,112},{1,17},{17... | collective-permute-start | bytes 368648 | tf_op jit(solution)/shard_map/ppermute | solution.py:16
  32.1 7.9 %copy-start.13 = (f32[24,32,320]{2,1,0:T(8,128)S(1)}, f32[24,32,320]{2,1,0:T(8,128)}, u32[]{:S(2)}) copy-start(f32[24,32,320]{2,1,0:T(8,128)} %param.20) | copy-start | bytes 2949124
  40.0 6.7 %slice-start = ((s8[7077888]{0:T(1024)(128)(4,1)}), s8[4194304]{0:T(1024)(128)(4,1)S(1)}, s32[]{:S(2)}) async-start(s8[7077888]{0:T(1024)(128)(4,1)} %bitcast.175), calls=%async_computation.1 | async-start | bytes 8388608
  40.0 7.7 %slice-start.1 = ((s8[7077888]{0:T(1024)(128)(4,1)}), s8[2883584]{0:T(1024)(128)(4,1)S(1)}, s32[]{:S(2)}) async-start(s8[7077888]{0:T(1024)(128)(4,1)} %bitcast.175), calls=%async_computation.2 | async-start | bytes 5767168
  40.0 8.7 %copy-start.21 = (f32[24,32,320]{2,1,0:T(8,128)S(1)}, f32[24,32,320]{2,1,0:T(8,128)}, u32[]{:S(2)}) copy-start(f32[24,32,320]{2,1,0:T(8,128)} %copy-done.20) | copy-start | bytes 2949124
  40.0 9.0 %copy-start.25 = (f32[23,32,320]{2,1,0:T(8,128)S(1)}, f32[23,32,320]{2,1,0:T(8,128)}, u32[]{:S(2)}) copy-start(f32[23,32,320]{2,1,0:T(8,128)} %get-tuple-element.18) | copy-start | bytes 2826244
  46.5 23.4 %copy-start.5 = (f32[24,32,320]{2,1,0:T(8,128)}, f32[24,32,320]{2,1,0:T(8,128)S(1)}, u32[]{:S(2)}) copy-start(f32[24,32,320]{2,1,0:T(8,128)S(1)} %get-tuple-element.10) | copy-start | bytes 2949124
  46.5 23.4 %copy-start.7 = (f32[24,32,320]{2,1,0:T(8,128)}, f32[24,32,320]{2,1,0:T(8,128)S(1)}, u32[]{:S(2)}) copy-start(f32[24,32,320]{2,1,0:T(8,128)S(1)} %get-tuple-element.11) | copy-start | bytes 2949124
  51.4 7.6 %copy-start.9 = (f32[24,32,320]{2,1,0:T(8,128)}, f32[24,32,320]{2,1,0:T(8,128)S(1)}, u32[]{:S(2)}) copy-start(f32[24,32,320]{2,1,0:T(8,128)S(1)} %fusion.9) | copy-start | bytes 2949124
  59.4 10.5 %copy-start.2 = (f32[24,32,320]{2,1,0:T(8,128)S(1)}, f32[24,32,320]{2,1,0:T(8,128)}, u32[]{:S(2)}) copy-start(f32[24,32,320]{2,1,0:T(8,128)} %param.19) | copy-start | bytes 2949124
  59.5 10.5 %copy-start.3 = (f32[24,32,320]{2,1,0:T(8,128)S(1)}, f32[24,32,320]{2,1,0:T(8,128)}, u32[]{:S(2)}) copy-start(f32[24,32,320]{2,1,0:T(8,128)} %param.21) | copy-start | bytes 2949124
  59.7 10.1 %collective-permute-start.3 = (f32[3,24,320]{2,0,1:T(4,128)S(1)}, f32[3,24,320]{2,0,1:T(4,128)S(1)}, u32[]{:S(2)}, u32[]{:S(2)}) collective-permute-start(f32[3,24,320]{2,0,1:T(4,128)S(1)} %pad_maximum_fusion.4), channel_id=1, source_target_pairs={{1,0},{2,1},{3,2},{4,3},{5,4},{6,5},{7,6},{8,7},{9,8},{10,9},{11,1... | collective-permute-start | bytes 276488 | tf_op jit(solution)/shard_map/ppermute | solution.py:16
  61.8 8.1 %collective-permute-start.2 = (f32[3,32,320]{2,1,0:T(8,128)S(1)}, f32[3,32,320]{2,1,0:T(8,128)S(1)}, u32[]{:S(2)}, u32[]{:S(2)}) collective-permute-start(f32[3,32,320]{2,1,0:T(8,128)S(1)} %pad_maximum_fusion.3), channel_id=1, source_target_pairs={{16,0},{32,16},{48,32},{64,48},{80,64},{96,80},{112,96},{17,1},{33... | collective-permute-start | bytes 368648 | tf_op jit(solution)/shard_map/ppermute | solution.py:16
  184.6 5.6 %copy-start.8 = (f32[24,32,320]{2,1,0:T(8,128)S(1)}, f32[24,32,320]{2,1,0:T(8,128)}, u32[]{:S(2)}) copy-start(f32[24,32,320]{2,1,0:T(8,128)} %copy-done.7) | copy-start | bytes 2949124
  184.6 5.6 %copy-start.10 = (f32[24,32,320]{2,1,0:T(8,128)S(1)}, f32[24,32,320]{2,1,0:T(8,128)}, u32[]{:S(2)}) copy-start(f32[24,32,320]{2,1,0:T(8,128)} %copy-done.9) | copy-start | bytes 2949124
  184.6 5.6 %copy-start.18 = (f32[24,31,320]{2,1,0:T(8,128)S(1)}, f32[24,31,320]{2,1,0:T(8,128)}, u32[]{:S(2)}) copy-start(f32[24,31,320]{2,1,0:T(8,128)} %slice.434) | copy-start | bytes 2856964
  184.6 5.6 %copy-start.19 = (f32[23,32,320]{2,1,0:T(8,128)S(1)}, f32[23,32,320]{2,1,0:T(8,128)}, u32[]{:S(2)}) copy-start(f32[23,32,320]{2,1,0:T(8,128)} %slice.421) | copy-start | bytes 2826244
  190.2 5.8 %slice-start.2 = ((s8[7077888]{0:T(1024)(128)(4,1)}), s8[4194304]{0:T(1024)(128)(4,1)S(1)}, s32[]{:S(2)}) async-start(s8[7077888]{0:T(1024)(128)(4,1)} %bitcast.177), calls=%async_computation.3 | async-start | bytes 8388608
  190.8 5.2 %slice-start.3 = ((s8[7077888]{0:T(1024)(128)(4,1)}), s8[2883584]{0:T(1024)(128)(4,1)S(1)}, s32[]{:S(2)}) async-start(s8[7077888]{0:T(1024)(128)(4,1)} %bitcast.177), calls=%async_computation.4 | async-start | bytes 5767168
  190.8 5.2 %slice-start.5 = ((f32[24,32,320]{2,1,0:T(8,128)}), f32[23,32,320]{2,1,0:T(8,128)S(1)}, s32[]{:S(2)}) async-start(f32[24,32,320]{2,1,0:T(8,128)} %copy-done.9), calls=%async_computation.6 | async-start | bytes 2260992 | tf_op jit(solution)/shard_map/slice | solution.py:29
  190.8 5.6 %copy-start.24 = (f32[24,31,320]{2,1,0:T(8,128)S(1)}, f32[24,31,320]{2,1,0:T(8,128)}, u32[]{:S(2)}) copy-start(f32[24,31,320]{2,1,0:T(8,128)} %slice.441) | copy-start | bytes 2856964
  199.6 14.1 %copy-start.14 = (f32[24,32,320]{2,1,0:T(8,128)S(1)}, f32[24,32,320]{2,1,0:T(8,128)}, u32[]{:S(2)}) copy-start(f32[24,32,320]{2,1,0:T(8,128)} %param.20) | copy-start | bytes 2949124
  200.9 8.2 %collective-permute-start.5 = (f32[3,24,320]{2,0,1:T(4,128)S(1)}, f32[3,24,320]{2,0,1:T(4,128)S(1)}, u32[]{:S(2)}, u32[]{:S(2)}) collective-permute-start(f32[3,24,320]{2,0,1:T(4,128)S(1)} %pad_maximum_fusion.6), channel_id=1, source_target_pairs={{0,1},{1,2},{2,3},{3,4},{4,5},{5,6},{6,7},{7,8},{8,9},{9,10},{10,1... | collective-permute-start | bytes 276488 | tf_op jit(solution)/shard_map/ppermute | solution.py:16
  204.3 9.4 %collective-permute-start.4 = (f32[3,32,320]{2,1,0:T(8,128)S(1)}, f32[3,32,320]{2,1,0:T(8,128)S(1)}, u32[]{:S(2)}, u32[]{:S(2)}) collective-permute-start(f32[3,32,320]{2,1,0:T(8,128)S(1)} %pad_maximum_fusion.5), channel_id=1, source_target_pairs={{0,16},{16,32},{32,48},{48,64},{64,80},{80,96},{96,112},{1,17},{17... | collective-permute-start | bytes 368648 | tf_op jit(solution)/shard_map/ppermute | solution.py:16
  224.1 9.0 %collective-permute-start.7 = (f32[3,24,320]{2,0,1:T(4,128)S(1)}, f32[3,24,320]{2,0,1:T(4,128)S(1)}, u32[]{:S(2)}, u32[]{:S(2)}) collective-permute-start(f32[3,24,320]{2,0,1:T(4,128)S(1)} %pad_maximum_fusion.8), channel_id=1, source_target_pairs={{1,0},{2,1},{3,2},{4,3},{5,4},{6,5},{7,6},{8,7},{9,8},{10,9},{11,1... | collective-permute-start | bytes 276488 | tf_op jit(solution)/shard_map/ppermute | solution.py:16
  226.4 10.6 %copy-start.17 = (f32[24,32,320]{2,1,0:T(8,128)S(1)}, f32[24,32,320]{2,1,0:T(8,128)}, u32[]{:S(2)}) copy-start(f32[24,32,320]{2,1,0:T(8,128)} %copy-done.16) | copy-start | bytes 2949124
  226.4 10.6 %copy-start.23 = (f32[24,32,320]{2,1,0:T(8,128)S(1)}, f32[24,32,320]{2,1,0:T(8,128)}, u32[]{:S(2)}) copy-start(f32[24,32,320]{2,1,0:T(8,128)} %param.18) | copy-start | bytes 2949124
  228.5 8.4 %collective-permute-start.6 = (f32[3,32,320]{2,1,0:T(8,128)S(1)}, f32[3,32,320]{2,1,0:T(8,128)S(1)}, u32[]{:S(2)}, u32[]{:S(2)}) collective-permute-start(f32[3,32,320]{2,1,0:T(8,128)S(1)} %pad_maximum_fusion.7), channel_id=1, source_target_pairs={{16,0},{32,16},{48,32},{64,48},{80,64},{96,80},{112,96},{17,1},{33... | collective-permute-start | bytes 368648 | tf_op jit(solution)/shard_map/ppermute | solution.py:16
  (13 other events, 22.8 us)
Sparse Core Ops, SparseCore 0:
  32.2 152.3 all-reduce.13
where the time goes:
time: 262 us; the launch traced here: 258 us
  waiting for transfers between devices  124 us (47%)
  local copies, waits for them, and re-layouts  36.6 us (14%)
  other arithmetic  36.5 us (14%)
  starting transfers between devices  28.3 us (11%)
  matrix products  16.9 us (6%)
  between operations  14.9 us (6%)
    psum x1, waiting for transfers between devices, shards(): whole_box = lax.psum(partial_box, ('gx', 'gy'))  112 us
    ppermute x8, starting transfers between devices, from_behind(): return lax.ppermute(value, axis, pairs)  28.2 us
    ppermute x8, waiting for transfers between devices, from_behind(): return lax.ppermute(value, axis, pairs)  12.8 us
    unnamed x7, other arithmetic  11.8 us
    slice x19, local copies, waits for them, and re-layouts, ahead_diff(): lax.slice_in_dim(values, 1, count, axis=dimension)  11.7 us
    add x2, other arithmetic, shards(): speed_x + time_step * buoyancy * (back_diff(stress_xx, 0, lower_x[0][None...  11.6 us
    unnamed x68, local copies, waits for them, and re-layouts  6.85 us
    slice x4, local copies, waits for them, and re-layouts, back_diff(): lax.slice_in_dim(values, 0, count - 1, axis=dimension)  6.17 us
  transfers between devices with their start and end apart: 9, of which 4 were waited for; matrix products, arithmetic and copies ran while one was open for 16% of the time, Pallas kernels for 0%

commit v1 on v0

v1 whole, which is shorter than its diff:
```python
import functools

import jax
import jax.numpy as jnp
from jax import lax
from jax.experimental import pallas as pl
from jax.experimental.pallas import tpu as pltpu
from jax.sharding import PartitionSpec as P

time_step = 0.2
precise = lax.Precision.HIGHEST
planes_per_block = 4


def neighbour(value, axis, by):
    size = lax.axis_size(axis)
    pairs = [(i, i + by) for i in range(size) if 0 <= i + by < size]
    return lax.ppermute(value, axis, pairs)


def shifted_up(values, dimension, first):
    where = lax.broadcasted_iota(jnp.int32, values.shape, dimension)
    return jnp.where(where == 0, first, pltpu.roll(values, 1, dimension))


def shifted_down(values, dimension, last):
    count = values.shape[dimension]
    where = lax.broadcasted_iota(jnp.int32, values.shape, dimension)
    return jnp.where(where == count - 1, last, pltpu.roll(values, count - 1, dimension))


def velocity_kernel(with_source, *refs):
    if with_source:
        (stress, velocity, buoyancy, plane, rows, source, source_plane, source_rows) = refs[:8]
        out, first_plane, first_rows, carry = refs[8:]
    else:
        (stress, velocity, buoyancy, plane, rows) = refs[:5]
        out, first_plane, first_rows, carry = refs[5:]
    block = pl.program_id(0)

    @pl.when(block == 0)
    def _():
        carry[...] = plane[0:3]
        if with_source:
            carry[0] = plane[0] + source_plane[...]

    count = out.shape[1]
    before = [carry[0], carry[1], carry[2]]
    for t in range(count):
        s_xx, s_yy, s_zz = stress[0, t], stress[1, t], stress[2, t]
        s_xy, s_xz, s_yz = stress[3, t], stress[4, t], stress[5, t]
        row_xy, row_yy, row_yz = rows[t, 0:1], rows[t, 1:2], rows[t, 2:3]
        if with_source:
            extra = source[t]
            s_xx, s_yy, s_zz = s_xx + extra, s_yy + extra, s_zz + extra
            row_yy = row_yy + source_rows[t]
        factor = time_step * buoyancy[t]
        v_x = velocity[0, t] + factor * (
            (s_xx - before[0])
            + (s_xy - shifted_up(s_xy, 0, row_xy))
            + (s_xz - shifted_up(s_xz, 1, 0.0))
        )
        v_y = velocity[1, t] + factor * (
            (s_xy - before[1])
            + (s_yy - shifted_up(s_yy, 0, row_yy))
            + (s_yz - shifted_up(s_yz, 1, 0.0))
        )
        v_z = velocity[2, t] + factor * (
            (s_xz - before[2])
            + (s_yz - shifted_up(s_yz, 0, row_yz))
            + (s_zz - shifted_up(s_zz, 1, 0.0))
        )
        for c, v in enumerate((v_x, v_y, v_z)):
            out[c, t] = v
            first_rows[t, c : c + 1] = v[0:1]
        if t == 0:

            @pl.when(block == 0)
            def _():
                for c, v in enumerate((v_x, v_y, v_z)):
                    first_plane[c] = v

        before = [s_xx, s_xy, s_xz]
    for c in range(3):
        carry[c] = before[c]


def stress_kernel(with_source, *refs):
    if with_source:
        (stress, velocity, lame_lambda, lame_mu, attenuation, plane, rows, source) = refs[:8]
        out, carry = refs[8:]
    else:
        (stress, velocity, lame_lambda, lame_mu, attenuation, plane, rows) = refs[:7]
        out, last_plane, last_rows, carry = refs[7:]
    block = pl.program_id(0)

    @pl.when(block == 0)
    def _():
        carry[...] = plane[...]

    count = out.shape[1]
    after = [carry[0], carry[1], carry[2]]
    for t in reversed(range(count)):
        v = [velocity[0, t], velocity[1, t], velocity[2, t]]
        in_x = [after[c] - v[c] for c in range(3)]
        in_y = [shifted_down(v[c], 0, rows[t, c : c + 1]) - v[c] for c in range(3)]
        in_z = [shifted_down(v[c], 1, 0.0) - v[c] for c in range(3)]
        decay = jnp.exp(-time_step * attenuation[t])
        shear = time_step * lame_mu[t]
        common = time_step * lame_lambda[t] * (in_x[0] + in_y[1] + in_z[2])
        normal = [in_x[0], in_y[1], in_z[2]]
        values = []
        for c in range(3):
            value = stress[c, t] + common + 2.0 * shear * normal[c]
            if with_source:
                value = decay * (value + source[t]) + source[t]
            else:
                value = decay * value
            values.append(value)
        values.append(decay * (stress[3, t] + shear * (in_y[0] + in_x[1])))
        values.append(decay * (stress[4, t] + shear * (in_z[0] + in_x[2])))
        values.append(decay * (stress[5, t] + shear * (in_z[1] + in_y[2])))
        for c in range(6):
            out[c, t] = values[c]
        if not with_source:
            for c, which in enumerate((3, 1, 5)):
                last_rows[t, c : c + 1] = values[which][values[which].shape[0] - 1 :]
            if t == count - 1:

                @pl.when(block == 0)
                def _():
                    for c, which in enumerate((0, 3, 4)):
                        last_plane[c] = values[which]

        after = v
    for c in range(3):
        carry[c] = after[c]


def update_velocity(stress, velocity, buoyancy, plane, rows, source=None):
    _, nx, ny, nz = velocity.shape
    per = planes_per_block
    along = lambda g: (0, g, 0, 0)
    in_specs = [
        pl.BlockSpec((6, per, ny, nz), along),
        pl.BlockSpec((3, per, ny, nz), along),
        pl.BlockSpec((per, ny, nz), lambda g: (g, 0, 0)),
        pl.BlockSpec(plane.shape, lambda g: (0, 0, 0)),
        pl.BlockSpec((per,) + rows.shape[1:], lambda g: (g, 0, 0)),
    ]
    args = [stress, velocity, buoyancy, plane, rows]
    if source is not None:
        in_specs += [
            pl.BlockSpec((per, ny, nz), lambda g: (g, 0, 0)),
            pl.BlockSpec((ny, nz), lambda g: (0, 0)),
            pl.BlockSpec((per, 1, nz), lambda g: (g, 0, 0)),
        ]
        args += list(source)
    cells = nx * ny * nz
    return pl.pallas_call(
        functools.partial(velocity_kernel, source is not None),
        grid=(nx // per,),
        in_specs=in_specs,
        out_specs=(
            pl.BlockSpec((3, per, ny, nz), along),
            pl.BlockSpec((3, ny, nz), lambda g: (0, 0, 0)),
            pl.BlockSpec((per, 3, nz), lambda g: (g, 0, 0)),
        ),
        out_shape=(
            jax.ShapeDtypeStruct(velocity.shape, jnp.float32),
            jax.ShapeDtypeStruct((3, ny, nz), jnp.float32),
            jax.ShapeDtypeStruct((nx, 3, nz), jnp.float32),
        ),
        scratch_shapes=[pltpu.VMEM((3, ny, nz), jnp.float32)],
        cost_estimate=pl.CostEstimate(
            flops=40 * cells, bytes_accessed=4 * 14 * cells, transcendentals=0
        ),
        name="velocity_second" if source is not None else "velocity_first",
    )(*args)


def update_stress(stress, velocity, coefficients, plane, rows, source=None):
    _, nx, ny, nz = velocity.shape
    per = planes_per_block
    blocks = nx // per
    along = lambda g: (0, blocks - 1 - g, 0, 0)
    cell = lambda g: (blocks - 1 - g, 0, 0)
    in_specs = [
        pl.BlockSpec((6, per, ny, nz), along),
        pl.BlockSpec((3, per, ny, nz), along),
        pl.BlockSpec((per, ny, nz), cell),
        pl.BlockSpec((per, ny, nz), cell),
        pl.BlockSpec((per, ny, nz), cell),
        pl.BlockSpec((3, ny, nz), lambda g: (0, 0, 0)),
        pl.BlockSpec((per, 3, nz), cell),
    ]
    args = [stress, velocity, *coefficients, plane, rows]
    out_specs = [pl.BlockSpec((6, per, ny, nz), along)]
    out_shape = [jax.ShapeDtypeStruct(stress.shape, jnp.float32)]
    if source is not None:
        in_specs.append(pl.BlockSpec((per, ny, nz), cell))
        args.append(source)
    else:
        out_specs += [
            pl.BlockSpec((3, ny, nz), lambda g: (0, 0, 0)),
            pl.BlockSpec((per, 3, nz), cell),
        ]
        out_shape += [
            jax.ShapeDtypeStruct((3, ny, nz), jnp.float32),
            jax.ShapeDtypeStruct((nx, 3, nz), jnp.float32),
        ]
    cells = nx * ny * nz
    return pl.pallas_call(
        functools.partial(stress_kernel, source is not None),
        grid=(blocks,),
        in_specs=in_specs,
        out_specs=tuple(out_specs),
        out_shape=tuple(out_shape),
        scratch_shapes=[pltpu.VMEM((3, ny, nz), jnp.float32)],
        cost_estimate=pl.CostEstimate(
            flops=60 * cells, bytes_accessed=4 * 18 * cells, transcendentals=cells
        ),
        name="stress_second" if source is not None else "stress_first",
    )(*args)


def shards(
    source_planes,
    weight_x,
    weight_y,
    weight_z,
    box_anchor,
    velocity,
    stress,
    lame_lambda,
    lame_mu,
    buoyancy,
    attenuation,
):
    nx, ny, nz = lame_mu.shape
    box_x, sources = weight_x.shape
    box_y, box_z = weight_y.shape[0], weight_z.shape[0]
    size_x, size_y = lax.axis_size("gx"), lax.axis_size("gy")
    columns = box_y // ny
    part = ny // size_x

    send_x = jnp.stack([stress[0, -1], stress[3, -1], stress[4, -1], attenuation[-1]])
    send_y = jnp.stack(
        [stress[3, :, -1], stress[1, :, -1], stress[5, :, -1], attenuation[:, -1]], axis=1
    )
    plane = neighbour(send_x, "gx", 1)
    rows = neighbour(send_y, "gy", 1)

    reduced = jnp.einsum("abc,zc->abz", source_planes, weight_z, precision=precise)
    reduced = jnp.einsum("abz,yb->ayz", reduced, weight_y, precision=precise)
    own = reduced.shape[0]
    padded = jnp.pad(reduced, ((0, 0), (1, 0), (0, 0)))
    pieces = []
    for i in range(size_x):
        for k in range(columns):
            start = k * ny + i * part
            pieces.append(padded[:, start : start + part + 1])
    pieces = jnp.stack(pieces).reshape(size_x, columns, own * (part + 1), box_z)
    pieces = jnp.pad(pieces, ((0, 0), (size_y - columns, 0), (0, 0), (0, 0)))
    pieces = pieces.reshape(size_x * size_y, own * (part + 1), box_z)

    speed, edge_x, edge_y = update_velocity(stress, velocity, buoyancy, plane, rows)
    upper_x = neighbour(edge_x, "gx", -1)
    upper_y = neighbour(edge_y, "gy", -1)

    gathered = lax.all_to_all(pieces, ("gx", "gy"), 0, 0, tiled=True)
    gathered = gathered.reshape(sources, part + 1, box_z)
    placed = jnp.zeros((size_x * nx + 1, sources), jnp.float32)
    placed = lax.dynamic_update_slice(placed, weight_x, (box_anchor[0] + 1, 0))
    windows = jnp.stack([placed[i * nx : i * nx + nx + 1] for i in range(size_x)])
    shares = jnp.einsum("ixa,arz->ixrz", windows, gathered, precision=precise)

    coefficients = (lame_lambda, lame_mu, attenuation)
    strained, edge_x, edge_y = update_stress(stress, speed, coefficients, upper_x, upper_y)
    lower_x = neighbour(edge_x, "gx", 1)
    lower_y = neighbour(edge_y, "gy", 1)

    box = lax.all_to_all(shares, "gx", 0, 0, tiled=True)

    def place(values):
        out = jnp.zeros(values.shape[:-1] + (nz,), jnp.float32)
        start = (0,) * (values.ndim - 1) + (box_anchor[2],)
        return lax.dynamic_update_slice(out, values, start)

    def lost(values, rate):
        return -time_step * jnp.exp(-time_step * rate) * values

    inner = box[:, 1:, 1:].transpose(1, 0, 2, 3).reshape(nx, ny, box_z)
    source = lost(place(inner), attenuation)
    source_plane = lost(place(box[:, 0, 1:].reshape(ny, box_z)), plane[3])
    source_rows = lost(place(box[0, 1:, 0]), rows[:, 3])[:, None]

    speed, edge_x, edge_y = update_velocity(
        strained, speed, buoyancy, lower_x, lower_y, (source, source_plane, source_rows)
    )
    upper_x = neighbour(edge_x, "gx", -1)
    upper_y = neighbour(edge_y, "gy", -1)
    (strained,) = update_stress(strained, speed, coefficients, upper_x, upper_y, source)
    return (speed, strained)


def solution(mesh):
    in_specs = (
        P(("gx", "gy"), None, None),
        P(),
        P(),
        P(),
        P(),
        P(None, "gx", "gy", None),
        P(None, "gx", "gy", None),
        P("gx", "gy", None),
        P("gx", "gy", None),
        P("gx", "gy", None),
        P("gx", "gy", None),
    )
    out_specs = (P(None, "gx", "gy", None), P(None, "gx", "gy", None))
    return jax.shard_map(shards, mesh=mesh, in_specs=in_specs, out_specs=out_specs, check_vma=False)
```

time: 262 us -> 150 us (0.57); the launches traced: 258 us -> 149 us
  waiting for transfers between devices: 124 us -> 24.1 us
  Pallas kernels: 0 us -> 39.4 us
  other arithmetic: 36.5 us -> 5.59 us
  starting transfers between devices: 28.3 us -> 43.8 us
  local copies, waits for them, and re-layouts: 36.6 us -> 24.7 us
  between operations: 14.9 us -> 4.17 us
  matrix products: 16.9 us -> 7.01 us
    psum x1 -> x0, waiting for transfers between devices: 112 us -> none  [shards(): whole_box = lax.psum(partial_box, ('gx', 'gy'))]
    pallas_call x0 -> x4, Pallas kernels: none -> 39.4 us  [the longest x2 20.7 us: update_stress(): pl.pallas_call(functools.partial(stress_kernel, source is not None), grid...]
    add x4 -> x0, other arithmetic: 15.1 us -> none  [the longest x2 11.6 us: shards(): speed_x + time_step * buoyancy * (back_diff(stress_xx, 0, lower_x[0][None...]
    slice x39 -> x5, local copies, waits for them, and re-layouts: 19.5 us -> 4.67 us  [the longest x1 1.24 us: shards(): stress[3, :, -1]]
    all_to_all x0 -> x2, starting transfers between devices: none -> 14.5 us  [the longest x1 10.2 us: shards(): gathered = lax.all_to_all(pieces, ('gx', 'gy'), 0, 0, tiled=True)]
    unnamed x7 -> x0, other arithmetic: 11.8 us -> none
    dot_general x4 -> x1, matrix products: 14.2 us -> 3.53 us  [shards(): shares = jnp.einsum('ixa,arz->ixrz', windows, gathered, precision=precise)]
    all_to_all x0 -> x2, waiting for transfers between devices: none -> 7.96 us  [the longest x1 7.96 us: shards(): gathered = lax.all_to_all(pieces, ('gx', 'gy'), 0, 0, tiled=True)]
  transfers between devices with their start and end apart: 9 -> 10, of which waited for: 4 -> 4; matrix products, arithmetic and copies ran while one was open for 16% -> 20% of each run, Pallas kernels for 0% -> 13%
where the time goes in v1:
time: 150 us; the launch traced here: 149 us
  starting transfers between devices  43.8 us (29%)
  Pallas kernels  39.4 us (26%)
  local copies, waits for them, and re-layouts  24.7 us (16%)
  waiting for transfers between devices  24.1 us (16%)
  matrix products  7.01 us (5%)
  other arithmetic  5.59 us (4%)
  between operations  4.17 us (3%)
    ppermute x8, starting transfers between devices, neighbour(): return lax.ppermute(value, axis, pairs)  29.2 us
    pallas_call x2, Pallas kernels, update_stress(): pl.pallas_call(functools.partial(stress_kernel, source is not None), grid...  20.7 us
    pallas_call x2, Pallas kernels, update_velocity(): pl.pallas_call(functools.partial(velocity_kernel, source is not None), gr...  18.7 us
    ppermute x8, waiting for transfers between devices, neighbour(): return lax.ppermute(value, axis, pairs)  16.1 us
    all_to_all x1, starting transfers between devices, shards(): gathered = lax.all_to_all(pieces, ('gx', 'gy'), 0, 0, tiled=True)  10.2 us
    all_to_all x1, waiting for transfers between devices, shards(): gathered = lax.all_to_all(pieces, ('gx', 'gy'), 0, 0, tiled=True)  7.96 us
    unnamed x68, local copies, waits for them, and re-layouts  5.83 us
    mul x3, other arithmetic, lost(): return -time_step * jnp.exp(-time_step * rate) * values  4.87 us
  transfers between devices with their start and end apart: 10, of which 4 were waited for; matrix products, arithmetic and copies ran while one was open for 20% of the time, Pallas kernels for 13%

profile of v1, /device:TPU:57, one launch (start us, length us, event | category | flops | bytes accessed | tf_op | source)
XLA Modules:
  0.0 148.7 jit_solution(18318492584563712193)
XLA Ops:
  0.6 0.9 slice.169
  3.1 4.8 %collective-permute-start = (f32[4,32,320]{2,1,0:T(8,128)}, f32[4,32,320]{2,1,0:T(8,128)S(1)}, u32[]{:S(2)}, u32[]{:S(2)}) collective-permute-start(f32[4,32,320]{2,1,0:T(8,128)} %pad_maximum_fusion), channel_id=1, source_target_pairs={{0,16},{16,32},{32,48},{48,64},{64,80},{80,96},{96,112},{1,17},{17... | collective-permute-start | bytes 491528 | tf_op jit(solution)/shard_map/ppermute | solution.py:18
  7.9 2.8 %fusion.4 = f32[3,384,96]{1,2,0:T(8,128)S(1)} fusion(f32[3,384,384]{2,1,0:T(8,128)S(1)} %copy-done, f32[96,384]{1,0:T(8,128)} %param.14), kind=kOutput, calls=%fused_computation.10 | convolution fusion | flops 509607936 | bytes 2359296 | tf_op jit(solution)/shard_map/abc,zc->abz/dot_general | solution.py:254
  12.0 1.5 %copy.25 = f32[128,15,96]{2,1,0:T(8,128)} copy(f32[128,15,96]{2,0,1:T(8,128)S(1)} %bitcast.177) | data formatting | bytes 1474560 | tf_op jit(solution)/shard_map/reshape | solution.py:265
  13.6 10.2 %all-to-all-start = ((f32[128,15,96]{2,1,0:T(8,128)}), f32[128,15,96]{2,1,0:T(8,128)}, u32[]{:S(2)}, u32[]{:S(2)}) async-start(f32[128,15,96]{2,1,0:T(8,128)} %copy.25), calls=%async_computation | async-start | bytes 2097152 | tf_op jit(solution)/shard_map/all_to_all | solution.py:271
  23.7 1.2 fusion.15
  27.8 1.0 slice.173
  31.4 8.0 %all-to-all-done = f32[128,15,96]{2,1,0:T(8,128)} async-done(((f32[128,15,96]{2,1,0:T(8,128)}), f32[128,15,96]{2,1,0:T(8,128)}, u32[]{:S(2)}, u32[]{:S(2)}) %all-to-all-start) | async-done | bytes 737312 | tf_op jit(solution)/shard_map/all_to_all | solution.py:271
  39.4 1.3 reshape.32
  40.7 1.3 copy.26
  42.0 3.5 %fusion = f32[8,25,5,96]{3,1,2,0:T(8,128)} fusion(f32[384,5,96]{0,2,1:T(8,128)} %copy.26, f32[8,25,384]{2,1,0:T(8,128)} %copy-done.3), kind=kOutput, calls=%fused_computation.2 | convolution fusion | flops 442368000 | bytes 1428480 | tf_op jit(solution)/shard_map/ixa,arz->ixrz/dot_general | solution.py:276
  45.5 4.4 %all-to-all-start.1 = ((f32[8,25,5,96]{3,1,2,0:T(8,128)}), f32[8,25,5,96]{3,1,2,0:T(8,128)S(1)}, u32[]{:S(2)}, u32[]{:S(2)}) async-start(f32[8,25,5,96]{3,1,2,0:T(8,128)} %fusion), calls=%async_computation.1 | async-start | bytes 1310720 | tf_op jit(solution)/shard_map/all_to_all | solution.py:283
  49.9 5.5 %collective-permute-start.1 = (f32[24,4,320]{2,0,1:T(8,128)S(1)}, f32[24,4,320]{2,0,1:T(8,128)S(1)}, u32[]{:S(2)}, u32[]{:S(2)}) collective-permute-start(f32[24,4,320]{2,0,1:T(8,128)S(1)} %pad_maximum_fusion.1), channel_id=1, source_target_pairs={{0,1},{1,2},{2,3},{3,4},{4,5},{5,6},{6,7},{7,8},{8,9},{9,10},{10,1... | collective-permute-start | bytes 368648 | tf_op jit(solution)/shard_map/ppermute | solution.py:18
  55.4 3.6 %collective-permute-done.1 = f32[24,4,320]{2,0,1:T(8,128)S(1)} collective-permute-done((f32[24,4,320]{2,0,1:T(8,128)S(1)}, f32[24,4,320]{2,0,1:T(8,128)S(1)}, u32[]{:S(2)}, u32[]{:S(2)}) %collective-permute-start.1) | collective-permute-done | bytes 122912 | tf_op jit(solution)/shard_map/ppermute | solution.py:18
  60.4 9.2 %velocity_first.1 = (f32[3,24,32,320]{3,2,1,0:T(8,128)}, f32[3,32,320]{2,1,0:T(8,128)}, f32[24,3,320]{2,1,0:T(4,128)}) custom-call(f32[6,24,32,320]{3,2,1,0:T(8,128)} %refs_0_.3, f32[3,24,32,320]{3,2,1,0:T(8,128)} %refs_1_.1, f32[24,32,320]{2,1,0:T(8,128)} %refs_2_.6, f32[4,32,320]{2,1,0:T(8,128)} %copy-done.4, f32[24,4,320]{2,1,0:T(4,128)} %copy.23.refs_4_), custom_call_target="tpu_custom_call" | custom-call | flops 9830400 | bytes 13762560 | tf_op jit(solution)/shard_map/velocity_first/pallas_call | solution.py:160
  69.7 4.7 %collective-permute-start.2 = (f32[3,32,320]{2,1,0:T(8,128)}, f32[3,32,320]{2,1,0:T(8,128)S(1)}, u32[]{:S(2)}, u32[]{:S(2)}) collective-permute-start(f32[3,32,320]{2,1,0:T(8,128)} %get-tuple-element.12), channel_id=1, source_target_pairs={{16,0},{32,16},{48,32},{64,48},{80,64},{96,80},{112,96},{17,1},{33... | collective-permute-start | bytes 368648 | tf_op jit(solution)/shard_map/ppermute | solution.py:18
  74.4 1.9 %collective-permute-start.3 = (f32[24,3,320]{2,1,0:T(4,128)}, f32[24,3,320]{2,1,0:T(4,128)S(1)}, u32[]{:S(2)}, u32[]{:S(2)}) collective-permute-start(f32[24,3,320]{2,1,0:T(4,128)} %get-tuple-element.13), channel_id=1, source_target_pairs={{1,0},{2,1},{3,2},{4,3},{5,4},{6,5},{7,6},{8,7},{9,8},{10,9},{11,1... | collective-permute-start | bytes 276488 | tf_op jit(solution)/shard_map/ppermute | solution.py:18
  78.0 5.6 %collective-permute-done.3.refs_6_ = f32[24,3,320]{2,1,0:T(4,128)S(1)} collective-permute-done((f32[24,3,320]{2,1,0:T(4,128)}, f32[24,3,320]{2,1,0:T(4,128)S(1)}, u32[]{:S(2)}, u32[]{:S(2)}) %collective-permute-start.3) | collective-permute-done | bytes 92192 | tf_op jit(solution)/shard_map/ppermute | solution.py:18
  84.3 10.2 %stress_first.1 = (f32[6,24,32,320]{3,2,1,0:T(8,128)}, f32[3,32,320]{2,1,0:T(8,128)}, f32[24,3,320]{2,1,0:T(4,128)}) custom-call(f32[6,24,32,320]{3,2,1,0:T(8,128)} %refs_0_.3, f32[3,24,32,320]{3,2,1,0:T(8,128)} %get-tuple-element.11.refs_1_, f32[24,32,320]{2,1,0:T(8,128)} %refs_2_.7, f32[24,32,320]{2,1,0:T(8,128)} %refs_3_.3, f32[24,32,320]{2,1,0:T(8,128)} %refs_4_.3, ...), custom_call_target="tpu_custom_call" | custom-call | flops 14745600 | bytes 17694720 | tf_op jit(solution)/shard_map/stress_first/pallas_call | solution.py:213
  94.5 3.3 %collective-permute-start.4 = (f32[3,32,320]{2,1,0:T(8,128)}, f32[3,32,320]{2,1,0:T(8,128)S(1)}, u32[]{:S(2)}, u32[]{:S(2)}) collective-permute-start(f32[3,32,320]{2,1,0:T(8,128)} %get-tuple-element.15), channel_id=1, source_target_pairs={{0,16},{16,32},{32,48},{48,64},{64,80},{80,96},{96,112},{1,17},{17... | collective-permute-start | bytes 368648 | tf_op jit(solution)/shard_map/ppermute | solution.py:18
  97.8 3.3 %collective-permute-start.5 = (f32[24,3,320]{2,1,0:T(4,128)}, f32[24,3,320]{2,1,0:T(4,128)}, u32[]{:S(2)}, u32[]{:S(2)}) collective-permute-start(f32[24,3,320]{2,1,0:T(4,128)} %get-tuple-element.16), channel_id=1, source_target_pairs={{0,1},{1,2},{2,3},{3,4},{4,5},{5,6},{6,7},{7,8},{8,9},{9,10},{10,1... | collective-permute-start | bytes 276488 | tf_op jit(solution)/shard_map/ppermute | solution.py:18
  101.2 0.9 copy-done.2
  102.1 1.2 broadcast_in_dim.15
  103.3 3.5 %dynamic_update_slice.13 = f32[24,32,320]{2,1,0:T(8,128)} dynamic-update-slice(f32[24,32,320]{2,1,0:T(8,128)} %broadcast_in_dim.15, f32[24,32,96]{2,1,0:T(8,128)S(1)} %bitcast.178, s32[]{:T(128)} %constant.9.clone.1, s32[]{:T(128)} %constant.9.clone.1, s32[]{:T(128)S(6)} %select_n.9) | dynamic-update-slice | bytes 589828 | tf_op jit(solution)/shard_map/dynamic_update_slice | solution.py:288
  106.8 2.7 %multiply_multiply_fusion.refs_5_.refs_7_ = f32[24,32,320]{2,1,0:T(8,128)} fusion(f32[24,32,320]{2,1,0:T(8,128)} %dynamic_update_slice.13, f32[24,32,320]{2,1,0:T(8,128)S(1)} %copy-done.1), kind=kLoop, calls=%fused_computation | loop fusion | flops 737280 | bytes 2949120 | tf_op jit(solution)/shard_map/mul | solution.py:291
  110.5 0.9 slice.246
  111.8 1.4 fusion.9.refs_6_
  115.3 9.4 %velocity_second.1 = (f32[3,24,32,320]{3,2,1,0:T(8,128)}, f32[3,32,320]{2,1,0:T(8,128)}, f32[24,3,320]{2,1,0:T(4,128)}) custom-call(f32[6,24,32,320]{3,2,1,0:T(8,128)} %get-tuple-element.14.refs_0_, f32[3,24,32,320]{3,2,1,0:T(8,128)} %get-tuple-element.11.refs_1_, f32[24,32,320]{2,1,0:T(8,128)} %refs_2_.6, f32[3,32,320]{2,1,0:T(8,128)} %copy-done.13, ...), custom_call_target="tpu_custom_call" | custom-call | flops 9830400 | bytes 13762560 | tf_op jit(solution)/shard_map/velocity_second/pallas_call | solution.py:160
  124.8 3.9 %collective-permute-start.6 = (f32[3,32,320]{2,1,0:T(8,128)}, f32[3,32,320]{2,1,0:T(8,128)S(1)}, u32[]{:S(2)}, u32[]{:S(2)}) collective-permute-start(f32[3,32,320]{2,1,0:T(8,128)} %get-tuple-element.18), channel_id=1, source_target_pairs={{16,0},{32,16},{48,32},{64,48},{80,64},{96,80},{112,96},{17,1},{33... | collective-permute-start | bytes 368648 | tf_op jit(solution)/shard_map/ppermute | solution.py:18
  128.6 1.9 %collective-permute-start.7 = (f32[24,3,320]{2,1,0:T(4,128)}, f32[24,3,320]{2,1,0:T(4,128)S(1)}, u32[]{:S(2)}, u32[]{:S(2)}) collective-permute-start(f32[24,3,320]{2,1,0:T(4,128)} %get-tuple-element.19), channel_id=1, source_target_pairs={{1,0},{2,1},{3,2},{4,3},{5,4},{6,5},{7,6},{8,7},{9,8},{10,9},{11,1... | collective-permute-start | bytes 276488 | tf_op jit(solution)/shard_map/ppermute | solution.py:18
  130.6 6.9 %collective-permute-done.7.refs_6_ = f32[24,3,320]{2,1,0:T(4,128)S(1)} collective-permute-done((f32[24,3,320]{2,1,0:T(4,128)}, f32[24,3,320]{2,1,0:T(4,128)S(1)}, u32[]{:S(2)}, u32[]{:S(2)}) %collective-permute-start.7) | collective-permute-done | bytes 92192 | tf_op jit(solution)/shard_map/ppermute | solution.py:18
  138.2 10.6 %stress_second.1 = f32[6,24,32,320]{3,2,1,0:T(8,128)} custom-call(f32[6,24,32,320]{3,2,1,0:T(8,128)} %get-tuple-element.14.refs_0_, f32[3,24,32,320]{3,2,1,0:T(8,128)} %get-tuple-element.9.refs_1_, f32[24,32,320]{2,1,0:T(8,128)} %refs_2_.7, f32[24,32,320]{2,1,0:T(8,128)} %refs_3_.3, f32[24,32,320]{2,1,0:T(8,128)} %refs_4_.3, f32[3,32,320]{2,1,0:T(8,128)} %copy-done.14, ...), custom_call_target="tpu_custom_call" | custom-call | flops 14745600 | bytes 17694720 | tf_op jit(solution)/shard_map/stress_second/pallas_call | solution.py:213
  (96 shorter events, 13.1 us)
Async XLA Ops:
  0.6 7.3 %copy-start = (f32[3,384,384]{2,1,0:T(8,128)S(1)}, f32[3,384,384]{2,1,0:T(8,128)}, u32[]{:S(2)}) copy-start(f32[3,384,384]{2,1,0:T(8,128)} %param.11) | copy-start | bytes 5308420
  3.1 7.6 %copy-start.12 = (f32[96,384]{1,0:T(8,128)S(1)}, f32[96,384]{1,0:T(8,128)}, u32[]{:S(2)}) copy-start(f32[96,384]{1,0:T(8,128)} %param.13) | copy-start | bytes 442372
  3.1 56.6 %collective-permute-start = (f32[4,32,320]{2,1,0:T(8,128)}, f32[4,32,320]{2,1,0:T(8,128)S(1)}, u32[]{:S(2)}, u32[]{:S(2)}) collective-permute-start(f32[4,32,320]{2,1,0:T(8,128)} %pad_maximum_fusion), channel_id=1, source_target_pairs={{0,16},{16,32},{32,48},{48,64},{64,80},{80,96},{96,112},{1,17},{17... | collective-permute-start | bytes 491528 | tf_op jit(solution)/shard_map/ppermute | solution.py:18
  13.6 11.4 %copy-start.17 = (s32[3]{0:T(128)S(1)}, s32[3]{0:T(128)}, u32[]{:S(2)}) copy-start(s32[3]{0:T(128)} %param.15) | copy-start | bytes 40
  13.6 13.3 %copy-start.16 = (f32[64,384]{1,0:T(8,128)S(1)}, f32[64,384]{1,0:T(8,128)}, u32[]{:S(2)}) copy-start(f32[64,384]{1,0:T(8,128)} %param.12) | copy-start | bytes 294916
  13.6 25.8 %all-to-all-start = ((f32[128,15,96]{2,1,0:T(8,128)}), f32[128,15,96]{2,1,0:T(8,128)}, u32[]{:S(2)}, u32[]{:S(2)}) async-start(f32[128,15,96]{2,1,0:T(8,128)} %copy.25), calls=%async_computation | async-start | bytes 2097152 | tf_op jit(solution)/shard_map/all_to_all | solution.py:271
  30.0 0.7 copy-start.3
  42.0 7.9 %copy-start.8 = (f32[24,1,320]{2,0,1:T(8,128)S(1)}, f32[24,1,320]{2,0,1:T(8,128)}, u32[]{:S(2)}) copy-start(f32[24,1,320]{2,0,1:T(8,128)} %copy.33) | copy-start | bytes 92164
  42.0 7.9 %copy-start.9 = (f32[1,24,1,320]{3,1,2,0:T(8,128)S(1)}, f32[1,24,1,320]{3,1,2,0:T(8,128)}, u32[]{:S(2)}) copy-start(f32[1,24,1,320]{3,1,2,0:T(8,128)} %copy.37) | copy-start | bytes 92164
  42.0 7.9 %copy-start.10 = (f32[24,1,320]{2,0,1:T(8,128)S(1)}, f32[24,1,320]{2,0,1:T(8,128)}, u32[]{:S(2)}) copy-start(f32[24,1,320]{2,0,1:T(8,128)} %get-tuple-element.28) | copy-start | bytes 92164
  42.0 7.9 %copy-start.11 = (f32[24,1,320]{2,0,1:T(8,128)S(1)}, f32[24,1,320]{2,0,1:T(8,128)}, u32[]{:S(2)}) copy-start(f32[24,1,320]{2,0,1:T(8,128)} %get-tuple-element.29) | copy-start | bytes 92164
  45.5 55.6 %all-to-all-start.1 = ((f32[8,25,5,96]{3,1,2,0:T(8,128)}), f32[8,25,5,96]{3,1,2,0:T(8,128)S(1)}, u32[]{:S(2)}, u32[]{:S(2)}) async-start(f32[8,25,5,96]{3,1,2,0:T(8,128)} %fusion), calls=%async_computation.1 | async-start | bytes 1310720 | tf_op jit(solution)/shard_map/all_to_all | solution.py:283
  49.9 9.1 %collective-permute-start.1 = (f32[24,4,320]{2,0,1:T(8,128)S(1)}, f32[24,4,320]{2,0,1:T(8,128)S(1)}, u32[]{:S(2)}, u32[]{:S(2)}) collective-permute-start(f32[24,4,320]{2,0,1:T(8,128)S(1)} %pad_maximum_fusion.1), channel_id=1, source_target_pairs={{0,1},{1,2},{2,3},{3,4},{4,5},{5,6},{6,7},{7,8},{8,9},{9,10},{10,1... | collective-permute-start | bytes 368648 | tf_op jit(solution)/shard_map/ppermute | solution.py:18
  59.1 10.6 %copy-start.5 = (f32[24,4,320]{2,0,1:T(8,128)}, f32[24,4,320]{2,0,1:T(8,128)S(1)}, u32[]{:S(2)}) copy-start(f32[24,4,320]{2,0,1:T(8,128)S(1)} %collective-permute-done.1) | copy-start | bytes 368644
  59.8 0.7 copy-start.4
  69.7 13.9 %collective-permute-start.2 = (f32[3,32,320]{2,1,0:T(8,128)}, f32[3,32,320]{2,1,0:T(8,128)S(1)}, u32[]{:S(2)}, u32[]{:S(2)}) collective-permute-start(f32[3,32,320]{2,1,0:T(8,128)} %get-tuple-element.12), channel_id=1, source_target_pairs={{16,0},{32,16},{48,32},{64,48},{80,64},{96,80},{112,96},{17,1},{33... | collective-permute-start | bytes 368648 | tf_op jit(solution)/shard_map/ppermute | solution.py:18
  74.4 9.2 %collective-permute-start.3 = (f32[24,3,320]{2,1,0:T(4,128)}, f32[24,3,320]{2,1,0:T(4,128)S(1)}, u32[]{:S(2)}, u32[]{:S(2)}) collective-permute-start(f32[24,3,320]{2,1,0:T(4,128)} %get-tuple-element.13), channel_id=1, source_target_pairs={{1,0},{2,1},{3,2},{4,3},{5,4},{6,5},{7,6},{8,7},{9,8},{10,9},{11,1... | collective-permute-start | bytes 276488 | tf_op jit(solution)/shard_map/ppermute | solution.py:18
  83.6 0.7 copy-start.7
  83.6 0.7 copy-start.6
  94.5 20.2 %collective-permute-start.4 = (f32[3,32,320]{2,1,0:T(8,128)}, f32[3,32,320]{2,1,0:T(8,128)S(1)}, u32[]{:S(2)}, u32[]{:S(2)}) collective-permute-start(f32[3,32,320]{2,1,0:T(8,128)} %get-tuple-element.15), channel_id=1, source_target_pairs={{0,16},{16,32},{32,48},{48,64},{64,80},{80,96},{96,112},{1,17},{17... | collective-permute-start | bytes 368648 | tf_op jit(solution)/shard_map/ppermute | solution.py:18
  97.8 16.9 %collective-permute-start.5 = (f32[24,3,320]{2,1,0:T(4,128)}, f32[24,3,320]{2,1,0:T(4,128)}, u32[]{:S(2)}, u32[]{:S(2)}) collective-permute-start(f32[24,3,320]{2,1,0:T(4,128)} %get-tuple-element.16), channel_id=1, source_target_pairs={{0,1},{1,2},{2,3},{3,4},{4,5},{5,6},{6,7},{7,8},{8,9},{9,10},{10,1... | collective-permute-start | bytes 276488 | tf_op jit(solution)/shard_map/ppermute | solution.py:18
  101.1 0.9 copy-start.2
  102.1 4.7 %copy-start.1 = (f32[24,32,320]{2,1,0:T(8,128)S(1)}, f32[24,32,320]{2,1,0:T(8,128)}, u32[]{:S(2)}) copy-start(f32[24,32,320]{2,1,0:T(8,128)} %refs_4_.3) | copy-start | bytes 2949124
  114.7 0.7 copy-start.13
  124.8 12.7 %collective-permute-start.6 = (f32[3,32,320]{2,1,0:T(8,128)}, f32[3,32,320]{2,1,0:T(8,128)S(1)}, u32[]{:S(2)}, u32[]{:S(2)}) collective-permute-start(f32[3,32,320]{2,1,0:T(8,128)} %get-tuple-element.18), channel_id=1, source_target_pairs={{16,0},{32,16},{48,32},{64,48},{80,64},{96,80},{112,96},{17,1},{33... | collective-permute-start | bytes 368648 | tf_op jit(solution)/shard_map/ppermute | solution.py:18
  128.6 8.8 %collective-permute-start.7 = (f32[24,3,320]{2,1,0:T(4,128)}, f32[24,3,320]{2,1,0:T(4,128)S(1)}, u32[]{:S(2)}, u32[]{:S(2)}) collective-permute-start(f32[24,3,320]{2,1,0:T(4,128)} %get-tuple-element.19), channel_id=1, source_target_pairs={{1,0},{2,1},{3,2},{4,3},{5,4},{6,5},{7,6},{8,7},{9,8},{10,9},{11,1... | collective-permute-start | bytes 276488 | tf_op jit(solution)/shard_map/ppermute | solution.py:18
  137.4 0.7 copy-start.15
  137.4 0.7 copy-start.14

commit v2 on v0

v2 whole, which is shorter than its diff:
```python
import functools

import jax
import jax.numpy as jnp
from jax import lax
from jax.experimental import pallas as pl
from jax.experimental.pallas import tpu as pltpu
from jax.sharding import PartitionSpec as P

time_step = 0.2
precise = lax.Precision.HIGHEST
strip = 8
lanes = 128
per = 6


def neighbour(value, axis, by):
    size = lax.axis_size(axis)
    pairs = [(i, i + by) for i in range(size) if 0 <= i + by < size]
    return lax.ppermute(value, axis, pairs)


def f32(*shape):
    return jax.ShapeDtypeStruct(shape, jnp.float32)


def dot(a, b, contract=((1,), (0,))):
    return lax.dot_general(
        a, b, (contract, ((), ())), precision=precise, preferred_element_type=jnp.float32
    )


def shifted_up(values):
    first = jnp.zeros((values.shape[0], 1), jnp.float32)
    return jnp.concatenate([first, values[:, :-1]], 1)


def shifted_down(values):
    last = jnp.zeros((values.shape[0], 1), jnp.float32)
    return jnp.concatenate([values[:, 1:], last], 1)


def after_row(values, row):
    where = lax.broadcasted_iota(jnp.int32, values.shape, 0)
    return jnp.where(where == 0, row, pltpu.roll(values, 1, 0))


def edges_kernel(plane, rate_plane, tile, rate_tile, out_plane, out_rows):
    for c, which in enumerate((0, 3, 4)):
        out_plane[c] = plane[which, 0]
    out_plane[3] = rate_plane[0]
    for c, which in enumerate((3, 1, 5)):
        out_rows[c] = tile[which, :, strip - 1]
    out_rows[3] = rate_tile[:, strip - 1]


def edges(stress, attenuation):
    _, nx, ny, nz = stress.shape
    last = ny // strip - 1
    return pl.pallas_call(
        edges_kernel,
        grid=(1,),
        in_specs=[
            pl.BlockSpec((6, 1, ny, nz), lambda g: (0, nx - 1, 0, 0)),
            pl.BlockSpec((1, ny, nz), lambda g: (nx - 1, 0, 0)),
            pl.BlockSpec((6, nx, strip, nz), lambda g: (0, 0, last, 0)),
            pl.BlockSpec((nx, strip, nz), lambda g: (0, last, 0)),
        ],
        out_specs=(
            pl.BlockSpec((4, ny, nz), lambda g: (0, 0, 0)),
            pl.BlockSpec((4, nx, nz), lambda g: (0, 0, 0)),
        ),
        out_shape=(f32(4, ny, nz), f32(4, nx, nz)),
        compiler_params=pltpu.CompilerParams(vmem_limit_bytes=12 << 20),
        name="edges",
    )(stress, attenuation, stress, attenuation)


def sections_kernel(size_x, size_y, columns, planes, weight_y, weight_z, out, held):
    own = planes.shape[0]
    box_y, box_z = weight_y.shape[0], weight_z.shape[0]
    part = box_y // (columns * size_x)
    out[...] = jnp.zeros_like(out)
    held[...] = jnp.zeros_like(held)
    for t in range(own):
        partly = dot(weight_y[...], planes[t])
        held[t, strip : strip + box_y, :box_z] = dot(partly, weight_z[...], ((1,), (1,)))
    for k in range(columns):
        for i in range(size_x):
            start = strip + (k * size_x + i) * part - 1
            for t in range(own):
                piece = held[t, start : start + part + 1]
                row = t * (part + 1)
                out[i * size_y + size_y - columns + k, row : row + part + 1] = piece


def sections(planes, weight_y, weight_z, size_x, size_y, columns, height):
    own = planes.shape[0]
    return pl.pallas_call(
        functools.partial(sections_kernel, size_x, size_y, columns),
        out_shape=f32(size_x * size_y, height, lanes),
        scratch_shapes=[pltpu.VMEM((own, strip + weight_y.shape[0], lanes), jnp.float32)],
        compiler_params=pltpu.CompilerParams(vmem_limit_bytes=16 << 20),
        name="sections",
    )(planes, weight_y, weight_z)


def contract_kernel(own, part, nx, anchor, weight_x, gathered, out, padded):
    box_x, count = weight_x.shape
    size_x, height, _ = out.shape
    rows = height // (part + 1)
    devices = count // own
    stride = gathered.shape[0] // devices
    section = lax.broadcasted_iota(jnp.int32, (count, count), 0)
    column = lax.broadcasted_iota(jnp.int32, (count, count), 1)
    pick = section == own * lax.rem(column, devices) + lax.div(column, devices)
    weights = dot(weight_x[...], pick.astype(jnp.float32))
    padded[...] = jnp.zeros_like(padded)
    for r in range(part + 1):
        terms = [
            gathered[pl.ds(t * (part + 1) + r, devices, stride=stride), :] for t in range(own)
        ]
        box = dot(weights, jnp.concatenate(terms, 0))
        padded[r, pl.ds(anchor[0] + strip, box_x), :] = box
    for i in range(size_x):
        start = strip + i * nx
        for r in range(part + 1):
            out[i, r * rows : r * rows + nx] = padded[r, start : start + nx]
            out[i, r * rows + nx : (r + 1) * rows] = padded[r, start - 1 : start - 1 + rows - nx]


def contract(anchor, weight_x, gathered, own, part, nx, size_x, rows):
    return pl.pallas_call(
        functools.partial(contract_kernel, own, part, nx),
        in_specs=[
            pl.BlockSpec(memory_space=pltpu.SMEM),
            pl.BlockSpec(memory_space=pltpu.VMEM),
            pl.BlockSpec(memory_space=pltpu.VMEM),
        ],
        out_shape=f32(size_x, (part + 1) * rows, lanes),
        scratch_shapes=[pltpu.VMEM((part + 1, 2 * strip + size_x * nx, lanes), jnp.float32)],
        compiler_params=pltpu.CompilerParams(vmem_limit_bytes=16 << 20),
        name="contract",
    )(anchor, weight_x, gathered)


def place_kernel(part, anchor, box, rate, rate_plane, rate_rows, out, out_plane, out_rows, held):
    size_x, height, _ = box.shape
    nx, ny, nz = out.shape
    rows = height // (part + 1)
    for i in range(size_x):
        for r in range(part):
            y = i * part + r
            first = (r + 1) * rows
            held[pl.ds(y, nx, stride=ny), :] = box[i, first : first + nx]
            held[nx * ny + y : nx * ny + y + 1] = box[i, first + nx : first + nx + 1]
    cell = lax.broadcasted_iota(jnp.int32, (lanes, nz), 1)
    which = lax.broadcasted_iota(jnp.int32, (lanes, nz), 0)
    pick = (cell - anchor[2] == which).astype(jnp.float32)

    def lost(values, rates):
        return (-time_step) * jnp.exp(-time_step * rates) * dot(values, pick)

    for t in range(0, nx, 4):
        values = (-time_step) * dot(held[t * ny : (t + 4) * ny], pick)
        for s in range(4):
            decay = jnp.exp(-time_step * rate[t + s])
            out[t + s] = decay * values[s * ny : (s + 1) * ny]
    out_plane[...] = lost(held[nx * ny :], rate_plane[3])
    out_rows[...] = lost(box[0, 0:nx], rate_rows[3])


def place(anchor, box, rate, rate_plane, rate_rows, part):
    nx, ny, nz = rate.shape
    return pl.pallas_call(
        functools.partial(place_kernel, part),
        in_specs=[pl.BlockSpec(memory_space=pltpu.SMEM)]
        + [pl.BlockSpec(memory_space=pltpu.VMEM)] * 4,
        out_shape=(f32(nx, ny, nz), f32(ny, nz), f32(nx, nz)),
        scratch_shapes=[pltpu.VMEM(((nx + 1) * ny, lanes), jnp.float32)],
        compiler_params=pltpu.CompilerParams(vmem_limit_bytes=16 << 20),
        name="place",
    )(anchor, box, rate, rate_plane, rate_rows)


def first_kernel(with_source, *refs):
    if with_source:
        (s_plane, v_plane, b_plane, s_tile, v_tile, b_tile, plane, rows) = refs[:8]
        q_plane, q_tile, source_plane, source_rows = refs[8:12]
    else:
        (s_plane, v_plane, b_plane, s_tile, v_tile, b_tile, plane, rows) = refs[:8]
    out_plane, out_rows = refs[-2:]
    low = [plane[c] for c in range(3)]
    edge = [rows[c] for c in range(3)]
    in_plane = [s_plane[c, 0] for c in range(6)]
    in_rows = [s_tile[c, :, 0] for c in range(6)]
    if with_source:
        low[0] = low[0] + source_plane[...]
        edge[1] = edge[1] + source_rows[...]
        for c in range(3):
            in_plane[c] = in_plane[c] + q_plane[0]
            in_rows[c] = in_rows[c] + q_tile[:, 0]

    xx, yy, zz, xy, xz, yz = in_plane
    factor = time_step * b_plane[0]
    head = [value[0:1] for value in edge]
    out_plane[0] = v_plane[0, 0] + factor * (
        (xx - low[0]) + (xy - after_row(xy, head[0])) + (xz - shifted_up(xz))
    )
    out_plane[1] = v_plane[1, 0] + factor * (
        (xy - low[1]) + (yy - after_row(yy, head[1])) + (yz - shifted_up(yz))
    )
    out_plane[2] = v_plane[2, 0] + factor * (
        (xz - low[2]) + (yz - after_row(yz, head[2])) + (zz - shifted_up(zz))
    )
    xx, yy, zz, xy, xz, yz = in_rows
    factor = time_step * b_tile[:, 0]
    head = [value[0:1] for value in low]
    out_rows[0] = v_tile[0, :, 0] + factor * (
        (xx - after_row(xx, head[0])) + (xy - edge[0]) + (xz - shifted_up(xz))
    )
    out_rows[1] = v_tile[1, :, 0] + factor * (
        (xy - after_row(xy, head[1])) + (yy - edge[1]) + (yz - shifted_up(yz))
    )
    out_rows[2] = v_tile[2, :, 0] + factor * (
        (xz - after_row(xz, head[2])) + (yz - edge[2]) + (zz - shifted_up(zz))
    )


def first_edges(stress, velocity, buoyancy, plane, rows, source=None):
    _, nx, ny, nz = velocity.shape
    fixed = lambda *shape: pl.BlockSpec(shape, lambda g: (0,) * len(shape))
    in_specs = [
        fixed(6, 1, ny, nz),
        fixed(3, 1, ny, nz),
        fixed(1, ny, nz),
        fixed(6, nx, strip, nz),
        fixed(3, nx, strip, nz),
        fixed(nx, strip, nz),
        fixed(*plane.shape),
        fixed(*rows.shape),
    ]
    args = [stress, velocity, buoyancy, stress, velocity, buoyancy, plane, rows]
    if source is not None:
        in_specs += [fixed(1, ny, nz), fixed(nx, strip, nz), fixed(ny, nz), fixed(nx, nz)]
        args += [source[0], *source]
    return pl.pallas_call(
        functools.partial(first_kernel, source is not None),
        grid=(1,),
        in_specs=in_specs,
        out_specs=(fixed(3, ny, nz), fixed(3, nx, nz)),
        out_shape=(f32(3, ny, nz), f32(3, nx, nz)),
        compiler_params=pltpu.CompilerParams(vmem_limit_bytes=16 << 20),
        cost_estimate=pl.CostEstimate(
            flops=80 * nz * (nx + ny), bytes_accessed=4 << 20, transcendentals=0
        ),
        name="first_edges",
    )(*args)


def step_kernel(with_source, *refs):
    (stress, velocity, buoyancy, lame_lambda, lame_mu, attenuation) = refs[:6]
    (below_xx, below_xy, below_xz, plane, rows, upper_plane, upper_rows) = refs[6:13]
    if with_source:
        source, below_source, source_plane, source_rows = refs[13:17]
        new_velocity, new_stress, carry = refs[17:]
    else:
        new_velocity, new_stress, last_plane, last_rows, carry = refs[13:]
    _, count, ny, nz = new_velocity.shape
    step = pl.program_id(0)
    block = pl.num_programs(0) - 1 - step
    carry_v, carry_s = carry.at[0:3], carry.at[3:6]

    @pl.when(step == 0)
    def _():
        for c in range(3):
            carry_v[c] = upper_plane[c]

    @pl.when(block == 0)
    def _():
        for c in range(3):
            carry_s[c] = plane[c]
        if with_source:
            carry_s[0] = plane[0] + source_plane[...]

    @pl.when(block != 0)
    def _():
        carry_s[0] = below_xx[0, 0]
        if with_source:
            carry_s[0] = below_xx[0, 0] + below_source[0]
        carry_s[1] = below_xy[0, 0]
        carry_s[2] = below_xz[0, 0]

    top = lax.broadcasted_iota(jnp.int32, (strip, nz), 0) == 0
    bottom = lax.broadcasted_iota(jnp.int32, (strip, nz), 0) == strip - 1

    def velocity_plane(t, _):
        x = block * count + t
        above = [rows[c, pl.ds(x, 1)] for c in range(3)]
        if with_source:
            above[1] = above[1] + source_rows[pl.ds(x, 1)]
        above = [jnp.broadcast_to(row, (strip, nz)) for row in above]
        for r in range(ny // strip):
            here = slice(strip * r, strip * (r + 1))
            s = [stress[c, t, here] for c in range(6)]
            if with_source:
                extra = source[t, here]
                s[:3] = [value + extra for value in s[:3]]
            s_xx, s_yy, s_zz, s_xy, s_xz, s_yz = s
            before = [carry_s[c, here] for c in range(3)]
            rolled = [pltpu.roll(value, 1, 0) for value in (s_xy, s_yy, s_yz)]
            up = [jnp.where(top, above[c], rolled[c]) for c in range(3)]
            factor = time_step * buoyancy[t, here]
            sums = (
                (s_xx - before[0]) + (s_xy - up[0]) + (s_xz - shifted_up(s_xz)),
                (s_xy - before[1]) + (s_yy - up[1]) + (s_yz - shifted_up(s_yz)),
                (s_xz - before[2]) + (s_yz - up[2]) + (s_zz - shifted_up(s_zz)),
            )
            for c in range(3):
                new_velocity[c, t, here] = velocity[c, t, here] + factor * sums[c]
            for c, value in enumerate((s_xx, s_xy, s_xz)):
                carry_s[c, here] = value
            above = rolled
        return 0

    def stress_plane(back, _):
        t = count - 1 - back
        x = block * count + t
        below = [jnp.broadcast_to(upper_rows[c, pl.ds(x, 1)], (strip, nz)) for c in range(3)]
        for r in reversed(range(ny // strip)):
            here = slice(strip * r, strip * (r + 1))
            v = [new_velocity[c, t, here] for c in range(3)]
            rolled = [pltpu.roll(value, strip - 1, 0) for value in v]
            in_x = [carry_v[c, here] - v[c] for c in range(3)]
            in_y = [jnp.where(bottom, below[c], rolled[c]) - v[c] for c in range(3)]
            in_z = [shifted_down(v[c]) - v[c] for c in range(3)]
            decay = jnp.exp(-time_step * attenuation[t, here])
            shear = time_step * lame_mu[t, here]
            normal = [in_x[0], in_y[1], in_z[2]]
            common = time_step * lame_lambda[t, here] * (normal[0] + normal[1] + normal[2])
            twice = 2.0 * shear
            if with_source:
                extra = source[t, here]
                common = common + extra
            values = []
            for c in range(3):
                value = decay * (stress[c, t, here] + (common + twice * normal[c]))
                values.append(value + extra if with_source else value)
            values.append(decay * (stress[3, t, here] + shear * (in_y[0] + in_x[1])))
            values.append(decay * (stress[4, t, here] + shear * (in_z[0] + in_x[2])))
            values.append(decay * (stress[5, t, here] + shear * (in_z[1] + in_y[2])))
            for c in range(6):
                new_stress[c, t, here] = values[c]
            if not with_source and r == ny // strip - 1:
                for c, which in enumerate((3, 1, 5)):
                    last_rows[c, pl.ds(x, 1)] = values[which][strip - 1 :]
            for c in range(3):
                carry_v[c, here] = v[c]
            below = rolled
        return 0

    lax.fori_loop(0, count, velocity_plane, 0)
    lax.fori_loop(0, count, stress_plane, 0)
    if not with_source:

        @pl.when(step == 0)
        def _():
            for c, which in enumerate((0, 3, 4)):
                last_plane[c] = new_stress[which, count - 1]


def full_step(stress, velocity, coefficients, plane, rows, upper_plane, upper_rows, source=None):
    _, nx, ny, nz = velocity.shape
    blocks = nx // per
    field = lambda g: (0, blocks - 1 - g, 0, 0)
    cell = lambda g: (blocks - 1 - g, 0, 0)
    under = lambda g: jnp.maximum((blocks - 1 - g) * per - 1, 0)
    fixed = lambda *shape: pl.BlockSpec(shape, lambda g: (0,) * len(shape))
    in_specs = [
        pl.BlockSpec((6, per, ny, nz), field),
        pl.BlockSpec((3, per, ny, nz), field),
        *[pl.BlockSpec((per, ny, nz), cell)] * 4,
        *[pl.BlockSpec((1, 1, ny, nz), lambda g, c=c: (c, under(g), 0, 0)) for c in (0, 3, 4)],
        fixed(*plane.shape),
        fixed(*rows.shape),
        fixed(*upper_plane.shape),
        fixed(*upper_rows.shape),
    ]
    args = [stress, velocity, *coefficients, stress, stress, stress]
    args += [plane, rows, upper_plane, upper_rows]
    out_specs = [pl.BlockSpec((3, per, ny, nz), field), pl.BlockSpec((6, per, ny, nz), field)]
    out_shape = [f32(*velocity.shape), f32(*stress.shape)]
    if source is not None:
        in_specs += [
            pl.BlockSpec((per, ny, nz), cell),
            pl.BlockSpec((1, ny, nz), lambda g: (under(g), 0, 0)),
            fixed(ny, nz),
            fixed(nx, nz),
        ]
        args += [source[0], *source]
    else:
        out_specs += [fixed(3, ny, nz), fixed(3, nx, nz)]
        out_shape += [f32(3, ny, nz), f32(3, nx, nz)]
    cells = nx * ny * nz
    return pl.pallas_call(
        functools.partial(step_kernel, source is not None),
        grid=(blocks,),
        in_specs=in_specs,
        out_specs=tuple(out_specs),
        out_shape=tuple(out_shape),
        scratch_shapes=[pltpu.VMEM((6, ny, nz), jnp.float32)],
        compiler_params=pltpu.CompilerParams(vmem_limit_bytes=32 << 20),
        cost_estimate=pl.CostEstimate(
            flops=100 * cells, bytes_accessed=4 * 23 * cells, transcendentals=cells
        ),
        name="second_step" if source is not None else "first_step",
    )(*args)


def shards(
    source_planes,
    weight_x,
    weight_y,
    weight_z,
    box_anchor,
    velocity,
    stress,
    lame_lambda,
    lame_mu,
    buoyancy,
    attenuation,
):
    nx, ny, nz = lame_mu.shape
    box_x, sources = weight_x.shape
    box_y = weight_y.shape[0]
    size_x, size_y = lax.axis_size("gx"), lax.axis_size("gy")
    own = source_planes.shape[0]
    columns = box_y // ny
    part = ny // size_x
    height = -(-own * (part + 1) // strip) * strip
    coefficients = (buoyancy, lame_lambda, lame_mu, attenuation)

    send_x, send_y = edges(stress, attenuation)
    plane = neighbour(send_x, "gx", 1)
    rows = neighbour(send_y, "gy", 1)

    pieces = sections(source_planes, weight_y, weight_z, size_x, size_y, columns, height)
    gathered = lax.all_to_all(pieces, ("gx", "gy"), 0, 0, tiled=True)

    first_x, first_y = first_edges(stress, velocity, buoyancy, plane, rows)
    upper_x = neighbour(first_x, "gx", -1)
    upper_y = neighbour(first_y, "gy", -1)

    gathered = gathered.reshape(size_x * size_y * height, lanes)
    shares = contract(box_anchor, weight_x, gathered, own, part, nx, size_x, nx + strip)
    box = lax.all_to_all(shares, "gx", 0, 0, tiled=True)

    speed, strained, last_x, last_y = full_step(
        stress, velocity, coefficients, plane, rows, upper_x, upper_y
    )
    lower_x = neighbour(last_x, "gx", 1)
    lower_y = neighbour(last_y, "gy", 1)

    source = place(box_anchor, box, attenuation, plane, rows, part)
    first_x, first_y = first_edges(strained, speed, buoyancy, lower_x, lower_y, source)
    upper_x = neighbour(first_x, "gx", -1)
    upper_y = neighbour(first_y, "gy", -1)
    return tuple(
        full_step(
            strained, speed, coefficients, lower_x, lower_y, upper_x, upper_y, source
        )
    )


def solution(mesh):
    in_specs = (
        P(("gx", "gy"), None, None),
        P(),
        P(),
        P(),
        P(),
        P(None, "gx", "gy", None),
        P(None, "gx", "gy", None),
        P("gx", "gy", None),
        P("gx", "gy", None),
        P("gx", "gy", None),
        P("gx", "gy", None),
    )
    out_specs = (P(None, "gx", "gy", None), P(None, "gx", "gy", None))
    return jax.shard_map(shards, mesh=mesh, in_specs=in_specs, out_specs=out_specs, check_vma=False)
```

time: 262 us -> 124 us (0.47); the launches traced: 258 us -> 123 us
  waiting for transfers between devices: 124 us -> 15 us
  other arithmetic: 36.5 us -> 0.01 us
  Pallas kernels: 0 us -> 26.5 us
  blocking collectives: 0 us -> 26.2 us
  matrix products: 16.9 us -> 0 us
  local copies, waits for them, and re-layouts: 36.6 us -> 20.1 us
  between operations: 14.9 us -> 0.94 us
  starting transfers between devices: 28.3 us -> 34.4 us
    psum x1 -> x0, waiting for transfers between devices: 112 us -> none  [shards(): whole_box = lax.psum(partial_box, ('gx', 'gy'))]
    pallas_call x0 -> x8, Pallas kernels: none -> 26.5 us  [the longest x2 18.4 us: full_step(): pl.pallas_call(functools.partial(step_kernel, source is not None), grid=(...]
    all_to_all x0 -> x1, blocking collectives: none -> 26.2 us  [shards(): gathered = lax.all_to_all(pieces, ('gx', 'gy'), 0, 0, tiled=True)]
    slice x39 -> x0, local copies, waits for them, and re-layouts: 19.5 us -> none  [the longest x19 11.7 us: ahead_diff(): lax.slice_in_dim(values, 1, count, axis=dimension)]
    dot_general x6 -> x0, matrix products: 16.9 us -> none  [the longest x1 5.15 us: shards(): pressure = jnp.einsum('xYz,Zz->xYZ', pressure, place_z, precision=precise)]
    add x4 -> x0, other arithmetic: 15.1 us -> none  [the longest x2 11.6 us: shards(): speed_x + time_step * buoyancy * (back_diff(stress_xx, 0, lower_x[0][None...]
    unnamed x68 -> x58, local copies, waits for them, and re-layouts: 6.85 us -> 20.1 us
    unnamed x7 -> x1, other arithmetic: 11.8 us -> 0.01 us
  transfers between devices with their start and end apart: 9 -> 9, of which waited for: 4 -> 3; matrix products, arithmetic and copies ran while one was open for 16% -> 0% of each run, Pallas kernels for 0% -> 9%
where the time goes in v2:
time: 124 us; the launch traced here: 123 us
  starting transfers between devices  34.4 us (28%)
  Pallas kernels  26.5 us (21%)
  blocking collectives  26.2 us (21%)
  local copies, waits for them, and re-layouts  20.1 us (16%)
  waiting for transfers between devices  15 us (12%)
    ppermute x8, starting transfers between devices, neighbour(): return lax.ppermute(value, axis, pairs)  30 us
    all_to_all x1, blocking collectives, shards(): gathered = lax.all_to_all(pieces, ('gx', 'gy'), 0, 0, tiled=True)  26.2 us
    unnamed x58, local copies, waits for them, and re-layouts  20.1 us
    pallas_call x2, Pallas kernels, full_step(): pl.pallas_call(functools.partial(step_kernel, source is not None), grid=(...  18.4 us
    ppermute x8, waiting for transfers between devices, neighbour(): return lax.ppermute(value, axis, pairs)  15 us
    all_to_all x1, starting transfers between devices, shards(): box = lax.all_to_all(shares, 'gx', 0, 0, tiled=True)  4.37 us
  transfers between devices with their start and end apart: 9, of which 3 were waited for; matrix products, arithmetic and copies ran while one was open for 0% of the time, Pallas kernels for 9%

profile of v2, /device:TPU:57, one launch (start us, length us, event | category | flops | bytes accessed | tf_op | source)
XLA Modules:
  0.0 123.0 jit_solution(8570326734825413750)
XLA Ops:
  0.6 1.5 %copy-done.20 = f32[3,384,384]{2,1,0:T(8,128)S(1)} copy-done((f32[3,384,384]{2,1,0:T(8,128)S(1)}, f32[3,384,384]{2,1,0:T(8,128)}, u32[]{:S(2)}) %copy-start.20) | copy-done | bytes 1769496
  2.1 0.9 copy-done.23
  3.0 0.9 copy-done.24
  3.9 2.1 %sections.1 = f32[128,16,128]{2,1,0:T(8,128)S(1)} custom-call(f32[3,384,384]{2,1,0:T(8,128)S(1)} %copy-done.20, f32[96,384]{1,0:T(8,128)S(1)} %copy-done.23, f32[96,384]{1,0:T(8,128)S(1)} %copy-done.24), custom_call_target="tpu_custom_call" | custom-call | tf_op jit(solution)/shard_map/sections/pallas_call | solution.py:99
  6.0 26.2 %all_to_all.10 = f32[128,16,128]{2,1,0:T(8,128)S(1)} all-to-all(f32[128,16,128]{2,1,0:T(8,128)S(1)} %sections.1), channel_id=1, replica_groups=mesh['gx'=8,'gy'=16] {'gx','gy'}, dimensions={0} | all-to-all | bytes 2097152 | tf_op jit(solution)/shard_map/all_to_all | solution.py:448
  32.2 2.0 %contract.1 = f32[8,160,128]{2,1,0:T(8,128)S(1)} custom-call(s32[3]{0:T(128)S(1)} %copy-done.26, f32[64,384]{1,0:T(8,128)S(1)} %copy-done.25, f32[2048,128]{1,0:T(8,128)S(1)} %bitcast.3), custom_call_target="tpu_custom_call" | custom-call | tf_op jit(solution)/shard_map/contract/pallas_call | solution.py:133
  34.2 0.8 copy-done.17
  35.0 4.4 %all-to-all-start.1 = ((f32[8,160,128]{2,1,0:T(8,128)}), f32[8,160,128]{2,1,0:T(8,128)S(1)}, u32[]{:S(2)}, u32[]{:S(2)}) async-start(f32[8,160,128]{2,1,0:T(8,128)} %copy-done.17), calls=%async_computation.1 | async-start | bytes 1310720 | tf_op jit(solution)/shard_map/all_to_all | solution.py:456
  39.4 3.0 %copy-done = f32[6,24,32,320]{3,2,1,0:T(8,128)S(1)} copy-done((f32[6,24,32,320]{3,2,1,0:T(8,128)S(1)}, f32[6,24,32,320]{3,2,1,0:T(8,128)}, u32[]{:S(2)}) %copy-start) | copy-done | bytes 5898264
  42.4 1.3 %copy-done.10 = f32[24,32,320]{2,1,0:T(8,128)S(1)} copy-done((f32[24,32,320]{2,1,0:T(8,128)S(1)}, f32[24,32,320]{2,1,0:T(8,128)}, u32[]{:S(2)}) %copy-start.10) | copy-done | bytes 983064
  43.8 4.9 %collective-permute-start = (f32[4,32,320]{2,1,0:T(8,128)S(1)}, f32[4,32,320]{2,1,0:T(8,128)S(1)}, u32[]{:S(2)}, u32[]{:S(2)}) collective-permute-start(f32[4,32,320]{2,1,0:T(8,128)S(1)} %get-tuple-element.15), channel_id=1, source_target_pairs={{0,16},{16,32},{32,48},{48,64},{64,80},{80,96},{96,112},{1,17},{17... | collective-permute-start | bytes 491528 | tf_op jit(solution)/shard_map/ppermute | solution.py:20
  48.7 6.0 %collective-permute-start.1 = (f32[4,24,320]{2,1,0:T(8,128)S(1)}, f32[4,24,320]{2,1,0:T(8,128)S(1)}, u32[]{:S(2)}, u32[]{:S(2)}) collective-permute-start(f32[4,24,320]{2,1,0:T(8,128)S(1)} %get-tuple-element.16), channel_id=1, source_target_pairs={{0,1},{1,2},{2,3},{3,4},{4,5},{5,6},{6,7},{7,8},{8,9},{9,10},{10,1... | collective-permute-start | bytes 368648 | tf_op jit(solution)/shard_map/ppermute | solution.py:20
  54.8 2.1 %collective-permute-done.1.refs_7_.refs_10_.rate_rows = f32[4,24,320]{2,1,0:T(8,128)S(1)} collective-permute-done((f32[4,24,320]{2,1,0:T(8,128)S(1)}, f32[4,24,320]{2,1,0:T(8,128)S(1)}, u32[]{:S(2)}, u32[]{:S(2)}) %collective-permute-start.1) | collective-permute-done | bytes 122912 | tf_op jit(solution)/shard_map/ppermute | solution.py:20
  56.9 0.4 first_edges.2
  57.3 3.7 %collective-permute-start.2 = (f32[3,32,320]{2,1,0:T(8,128)S(1)}, f32[3,32,320]{2,1,0:T(8,128)S(1)}, u32[]{:S(2)}, u32[]{:S(2)}) collective-permute-start(f32[3,32,320]{2,1,0:T(8,128)S(1)} %get-tuple-element.17), channel_id=1, source_target_pairs={{16,0},{32,16},{48,32},{64,48},{80,64},{96,80},{112,96},{17,1},{33... | collective-permute-start | bytes 368648 | tf_op jit(solution)/shard_map/ppermute | solution.py:20
  61.0 2.1 %collective-permute-start.3 = (f32[3,24,320]{2,1,0:T(8,128)S(1)}, f32[3,24,320]{2,1,0:T(8,128)S(1)}, u32[]{:S(2)}, u32[]{:S(2)}) collective-permute-start(f32[3,24,320]{2,1,0:T(8,128)S(1)} %get-tuple-element.18), channel_id=1, source_target_pairs={{1,0},{2,1},{3,2},{4,3},{5,4},{6,5},{7,6},{8,7},{9,8},{10,9},{11,1... | collective-permute-start | bytes 276488 | tf_op jit(solution)/shard_map/ppermute | solution.py:20
  63.1 6.6 %collective-permute-done.3.refs_12_ = f32[3,24,320]{2,1,0:T(8,128)S(1)} collective-permute-done((f32[3,24,320]{2,1,0:T(8,128)S(1)}, f32[3,24,320]{2,1,0:T(8,128)S(1)}, u32[]{:S(2)}, u32[]{:S(2)}) %collective-permute-start.3) | collective-permute-done | bytes 92192 | tf_op jit(solution)/shard_map/ppermute | solution.py:20
  69.8 9.1 %first_step.1 = (f32[3,24,32,320]{3,2,1,0:T(8,128)S(1)}, f32[6,24,32,320]{3,2,1,0:T(8,128)S(1)}, f32[3,32,320]{2,1,0:T(8,128)}, f32[3,24,320]{2,1,0:T(8,128)}) custom-call(f32[6,24,32,320]{3,2,1,0:T(8,128)} %refs_8_.1, f32[3,24,32,320]{3,2,1,0:T(8,128)S(1)} %copy-done.6, f32[24,32,320]{2,1,0:T(8,128)S(1)} %copy-done.4, f32[24,32,320]{2,1,0:T(8,128)S(1)} %copy-done.13, ...), custom_call_target="tpu_custom_call" | custom-call | flops 24576000 | bytes 22609920 | tf_op jit(solution)/shard_map/first_step/pallas_call | solution.py:405
  78.9 3.0 %copy-done.1 = f32[6,24,32,320]{3,2,1,0:T(8,128)} copy-done((f32[6,24,32,320]{3,2,1,0:T(8,128)}, f32[6,24,32,320]{3,2,1,0:T(8,128)S(1)}, u32[]{:S(2)}) %copy-start.1) | copy-done | bytes 5898264
  81.9 1.8 %copy-done.7 = f32[3,24,32,320]{3,2,1,0:T(8,128)} copy-done((f32[3,24,32,320]{3,2,1,0:T(8,128)}, f32[3,24,32,320]{3,2,1,0:T(8,128)S(1)}, u32[]{:S(2)}) %copy-start.7) | copy-done | bytes 2949144
  83.7 4.3 %collective-permute-start.4 = (f32[3,32,320]{2,1,0:T(8,128)}, f32[3,32,320]{2,1,0:T(8,128)S(1)}, u32[]{:S(2)}, u32[]{:S(2)}) collective-permute-start(f32[3,32,320]{2,1,0:T(8,128)} %get-tuple-element.21), channel_id=1, source_target_pairs={{0,16},{16,32},{32,48},{48,64},{64,80},{80,96},{96,112},{1,17},{17... | collective-permute-start | bytes 368648 | tf_op jit(solution)/shard_map/ppermute | solution.py:20
  88.0 2.5 %collective-permute-start.5 = (f32[3,24,320]{2,1,0:T(8,128)}, f32[3,24,320]{2,1,0:T(8,128)}, u32[]{:S(2)}, u32[]{:S(2)}) collective-permute-start(f32[3,24,320]{2,1,0:T(8,128)} %get-tuple-element.22), channel_id=1, source_target_pairs={{0,1},{1,2},{2,3},{3,4},{4,5},{5,6},{6,7},{7,8},{8,9},{9,10},{10,1... | collective-permute-start | bytes 276488 | tf_op jit(solution)/shard_map/ppermute | solution.py:20
  90.5 0.9 copy-done.19
  91.5 0.9 copy-done.22
  92.4 2.0 %place.1 = (f32[24,32,320]{2,1,0:T(8,128)S(1)}, f32[32,320]{1,0:T(8,128)S(1)}, f32[24,320]{1,0:T(8,128)S(1)}) custom-call(s32[3]{0:T(128)S(1)} %copy-done.26, f32[8,160,128]{2,1,0:T(8,128)S(1)} %all-to-all-done.1.box, f32[24,32,320]{2,1,0:T(8,128)S(1)} %copy-done.12, f32[4,32,320]{2,1,0:T(8,128)S(1)} %copy-done.19, f32[4,24,320]{2,1,0:T(8,128)S(1)} %copy-done.22), custom_call_target="tpu_custom_call" | custom-call | tf_op jit(solution)/shard_map/place/pallas_call | solution.py:175
  94.4 3.0 %copy-done.2 = f32[6,24,32,320]{3,2,1,0:T(8,128)S(1)} copy-done((f32[6,24,32,320]{3,2,1,0:T(8,128)S(1)}, f32[6,24,32,320]{3,2,1,0:T(8,128)}, u32[]{:S(2)}) %copy-start.2) | copy-done | bytes 5898264
  97.4 2.0 %copy-done.8 = f32[3,24,32,320]{3,2,1,0:T(8,128)S(1)} copy-done((f32[3,24,32,320]{3,2,1,0:T(8,128)S(1)}, f32[3,24,32,320]{3,2,1,0:T(8,128)}, u32[]{:S(2)}) %copy-start.8) | copy-done | bytes 2949144
  99.4 1.5 %first_edges.3 = (f32[3,32,320]{2,1,0:T(8,128)S(1)}, f32[3,24,320]{2,1,0:T(8,128)S(1)}) custom-call(f32[6,24,32,320]{3,2,1,0:T(8,128)S(1)} %copy-done.2, f32[3,24,32,320]{3,2,1,0:T(8,128)S(1)} %copy-done.8, f32[24,32,320]{2,1,0:T(8,128)S(1)} %copy-done.5, f32[6,24,32,320]{3,2,1,0:T(8,128)S(1)} %copy-done.2, f32[3,24,32,320]{3,2,1,0:T(8,128)S(1)} %copy-done.8, ...), custom_call_target="tpu_custom_call" | custom-call | flops 1433600 | bytes 4194304 | tf_op jit(solution)/shard_map/first_edges/pallas_call | solution.py:247
  101.0 4.6 %collective-permute-start.6 = (f32[3,32,320]{2,1,0:T(8,128)S(1)}, f32[3,32,320]{2,1,0:T(8,128)S(1)}, u32[]{:S(2)}, u32[]{:S(2)}) collective-permute-start(f32[3,32,320]{2,1,0:T(8,128)S(1)} %get-tuple-element.26), channel_id=1, source_target_pairs={{16,0},{32,16},{48,32},{64,48},{80,64},{96,80},{112,96},{17,1},{33... | collective-permute-start | bytes 368648 | tf_op jit(solution)/shard_map/ppermute | solution.py:20
  105.5 1.9 %collective-permute-start.7 = (f32[3,24,320]{2,1,0:T(8,128)S(1)}, f32[3,24,320]{2,1,0:T(8,128)S(1)}, u32[]{:S(2)}, u32[]{:S(2)}) collective-permute-start(f32[3,24,320]{2,1,0:T(8,128)S(1)} %get-tuple-element.27), channel_id=1, source_target_pairs={{1,0},{2,1},{3,2},{4,3},{5,4},{6,5},{7,6},{8,7},{9,8},{10,9},{11,1... | collective-permute-start | bytes 276488 | tf_op jit(solution)/shard_map/ppermute | solution.py:20
  107.5 6.2 %collective-permute-done.7.refs_12_ = f32[3,24,320]{2,1,0:T(8,128)S(1)} collective-permute-done((f32[3,24,320]{2,1,0:T(8,128)S(1)}, f32[3,24,320]{2,1,0:T(8,128)S(1)}, u32[]{:S(2)}, u32[]{:S(2)}) %collective-permute-start.7) | collective-permute-done | bytes 92192 | tf_op jit(solution)/shard_map/ppermute | solution.py:20
  113.7 9.2 %second_step.1 = (f32[3,24,32,320]{3,2,1,0:T(8,128)}, f32[6,24,32,320]{3,2,1,0:T(8,128)}) custom-call(f32[6,24,32,320]{3,2,1,0:T(8,128)S(1)} %copy-done.3, f32[3,24,32,320]{3,2,1,0:T(8,128)S(1)} %copy-done.9, f32[24,32,320]{2,1,0:T(8,128)S(1)} %copy-done.5, f32[24,32,320]{2,1,0:T(8,128)S(1)} %copy-done.14, f32[24,32,320]{2,1,0:T(8,128)S(1)} %copy-done.16, ...), custom_call_target="tpu_custom_call" | custom-call | flops 24576000 | bytes 22609920 | tf_op jit(solution)/shard_map/second_step/pallas_call | solution.py:405
  (54 shorter events, 0.3 us)
Async XLA Ops:
  0.6 1.5 %copy-start.20 = (f32[3,384,384]{2,1,0:T(8,128)S(1)}, f32[3,384,384]{2,1,0:T(8,128)}, u32[]{:S(2)}) copy-start(f32[3,384,384]{2,1,0:T(8,128)} %planes.1) | copy-start | bytes 5308420
  3.9 28.3 %copy-start.25 = (f32[64,384]{1,0:T(8,128)S(1)}, f32[64,384]{1,0:T(8,128)}, u32[]{:S(2)}) copy-start(f32[64,384]{1,0:T(8,128)} %weight_x.1) | copy-start | bytes 294916
  3.9 28.3 %copy-start.26 = (s32[3]{0:T(128)S(1)}, s32[3]{0:T(128)}, u32[]{:S(2)}) copy-start(s32[3]{0:T(128)} %anchor.3) | copy-start | bytes 40
  6.0 50.8 %slice-start = ((s8[7077888]{0:T(1024)(128)(4,1)}), s8[2883584]{0:T(1024)(128)(4,1)S(1)}, s32[]{:S(2)}) async-start(s8[7077888]{0:T(1024)(128)(4,1)} %bitcast.1), calls=%async_computation.2 | async-start | bytes 5767168
  35.0 55.5 %all-to-all-start.1 = ((f32[8,160,128]{2,1,0:T(8,128)}), f32[8,160,128]{2,1,0:T(8,128)S(1)}, u32[]{:S(2)}, u32[]{:S(2)}) async-start(f32[8,160,128]{2,1,0:T(8,128)} %copy-done.17), calls=%async_computation.1 | async-start | bytes 1310720 | tf_op jit(solution)/shard_map/all_to_all | solution.py:456
  39.4 3.0 %copy-start = (f32[6,24,32,320]{3,2,1,0:T(8,128)S(1)}, f32[6,24,32,320]{3,2,1,0:T(8,128)}, u32[]{:S(2)}) copy-start(f32[6,24,32,320]{3,2,1,0:T(8,128)} %refs_8_.1) | copy-start | bytes 17694724
  43.7 13.2 %slice-start.1 = ((s8[7077888]{0:T(1024)(128)(4,1)}), s8[4194304]{0:T(1024)(128)(4,1)S(1)}, s32[]{:S(2)}) async-start(s8[7077888]{0:T(1024)(128)(4,1)} %bitcast.1), calls=%async_computation.3 | async-start | bytes 8388608
  43.7 13.2 %copy-start.4 = (f32[24,32,320]{2,1,0:T(8,128)S(1)}, f32[24,32,320]{2,1,0:T(8,128)}, u32[]{:S(2)}) copy-start(f32[24,32,320]{2,1,0:T(8,128)} %refs_2_.7) | copy-start | bytes 2949124
  43.7 13.2 %copy-start.6 = (f32[3,24,32,320]{3,2,1,0:T(8,128)S(1)}, f32[3,24,32,320]{3,2,1,0:T(8,128)}, u32[]{:S(2)}) copy-start(f32[3,24,32,320]{3,2,1,0:T(8,128)} %refs_1_.3) | copy-start | bytes 8847364
  43.8 13.0 %collective-permute-start = (f32[4,32,320]{2,1,0:T(8,128)S(1)}, f32[4,32,320]{2,1,0:T(8,128)S(1)}, u32[]{:S(2)}, u32[]{:S(2)}) collective-permute-start(f32[4,32,320]{2,1,0:T(8,128)S(1)} %get-tuple-element.15), channel_id=1, source_target_pairs={{0,16},{16,32},{32,48},{48,64},{64,80},{80,96},{96,112},{1,17},{17... | collective-permute-start | bytes 491528 | tf_op jit(solution)/shard_map/ppermute | solution.py:20
  48.7 21.0 %copy-start.11 = (f32[24,32,320]{2,1,0:T(8,128)S(1)}, f32[24,32,320]{2,1,0:T(8,128)}, u32[]{:S(2)}) copy-start(f32[24,32,320]{2,1,0:T(8,128)} %refs_5_.7) | copy-start | bytes 2949124
  48.7 21.0 %copy-start.13 = (f32[24,32,320]{2,1,0:T(8,128)S(1)}, f32[24,32,320]{2,1,0:T(8,128)}, u32[]{:S(2)}) copy-start(f32[24,32,320]{2,1,0:T(8,128)} %refs_3_.5) | copy-start | bytes 2949124
  48.7 21.0 %copy-start.15 = (f32[24,32,320]{2,1,0:T(8,128)S(1)}, f32[24,32,320]{2,1,0:T(8,128)}, u32[]{:S(2)}) copy-start(f32[24,32,320]{2,1,0:T(8,128)} %refs_4_.5) | copy-start | bytes 2949124
  48.7 8.1 %collective-permute-start.1 = (f32[4,24,320]{2,1,0:T(8,128)S(1)}, f32[4,24,320]{2,1,0:T(8,128)S(1)}, u32[]{:S(2)}, u32[]{:S(2)}) collective-permute-start(f32[4,24,320]{2,1,0:T(8,128)S(1)} %get-tuple-element.16), channel_id=1, source_target_pairs={{0,1},{1,2},{2,3},{3,4},{4,5},{5,6},{6,7},{7,8},{8,9},{9,10},{10,1... | collective-permute-start | bytes 368648 | tf_op jit(solution)/shard_map/ppermute | solution.py:20
  56.8 12.9 %copy-start.21 = (f32[4,24,320]{2,1,0:T(8,128)}, f32[4,24,320]{2,1,0:T(8,128)S(1)}, u32[]{:S(2)}) copy-start(f32[4,24,320]{2,1,0:T(8,128)S(1)} %collective-permute-done.1.refs_7_.refs_10_.rate_rows) | copy-start | bytes 368644
  56.9 12.8 %copy-start.18 = (f32[4,32,320]{2,1,0:T(8,128)}, f32[4,32,320]{2,1,0:T(8,128)S(1)}, u32[]{:S(2)}) copy-start(f32[4,32,320]{2,1,0:T(8,128)S(1)} %collective-permute-done.refs_6_.refs_9_.rate_plane) | copy-start | bytes 491524
  57.3 12.4 %collective-permute-start.2 = (f32[3,32,320]{2,1,0:T(8,128)S(1)}, f32[3,32,320]{2,1,0:T(8,128)S(1)}, u32[]{:S(2)}, u32[]{:S(2)}) collective-permute-start(f32[3,32,320]{2,1,0:T(8,128)S(1)} %get-tuple-element.17), channel_id=1, source_target_pairs={{16,0},{32,16},{48,32},{64,48},{80,64},{96,80},{112,96},{17,1},{33... | collective-permute-start | bytes 368648 | tf_op jit(solution)/shard_map/ppermute | solution.py:20
  61.0 29.6 %copy-start.12 = (f32[24,32,320]{2,1,0:T(8,128)S(1)}, f32[24,32,320]{2,1,0:T(8,128)}, u32[]{:S(2)}) copy-start(f32[24,32,320]{2,1,0:T(8,128)} %refs_5_.7) | copy-start | bytes 2949124
  61.0 33.4 %copy-start.5 = (f32[24,32,320]{2,1,0:T(8,128)S(1)}, f32[24,32,320]{2,1,0:T(8,128)}, u32[]{:S(2)}) copy-start(f32[24,32,320]{2,1,0:T(8,128)} %refs_2_.7) | copy-start | bytes 2949124
  61.0 8.7 %collective-permute-start.3 = (f32[3,24,320]{2,1,0:T(8,128)S(1)}, f32[3,24,320]{2,1,0:T(8,128)S(1)}, u32[]{:S(2)}, u32[]{:S(2)}) collective-permute-start(f32[3,24,320]{2,1,0:T(8,128)S(1)} %get-tuple-element.18), channel_id=1, source_target_pairs={{1,0},{2,1},{3,2},{4,3},{5,4},{6,5},{7,6},{8,7},{9,8},{10,9},{11,1... | collective-permute-start | bytes 276488 | tf_op jit(solution)/shard_map/ppermute | solution.py:20
  78.9 3.0 %copy-start.1 = (f32[6,24,32,320]{3,2,1,0:T(8,128)}, f32[6,24,32,320]{3,2,1,0:T(8,128)S(1)}, u32[]{:S(2)}) copy-start(f32[6,24,32,320]{3,2,1,0:T(8,128)S(1)} %get-tuple-element.19.refs_0_.refs_3_.refs_6_.refs_7_.refs_8_) | copy-start | bytes 17694724
  81.9 1.8 %copy-start.7 = (f32[3,24,32,320]{3,2,1,0:T(8,128)}, f32[3,24,32,320]{3,2,1,0:T(8,128)S(1)}, u32[]{:S(2)}) copy-start(f32[3,24,32,320]{3,2,1,0:T(8,128)S(1)} %get-tuple-element.20.refs_1_.refs_4_) | copy-start | bytes 8847364
  83.7 10.7 %collective-permute-start.4 = (f32[3,32,320]{2,1,0:T(8,128)}, f32[3,32,320]{2,1,0:T(8,128)S(1)}, u32[]{:S(2)}, u32[]{:S(2)}) collective-permute-start(f32[3,32,320]{2,1,0:T(8,128)} %get-tuple-element.21), channel_id=1, source_target_pairs={{0,16},{16,32},{32,48},{48,64},{64,80},{80,96},{96,112},{1,17},{17... | collective-permute-start | bytes 368648 | tf_op jit(solution)/shard_map/ppermute | solution.py:20
  88.0 6.4 %collective-permute-start.5 = (f32[3,24,320]{2,1,0:T(8,128)}, f32[3,24,320]{2,1,0:T(8,128)}, u32[]{:S(2)}, u32[]{:S(2)}) collective-permute-start(f32[3,24,320]{2,1,0:T(8,128)} %get-tuple-element.22), channel_id=1, source_target_pairs={{0,1},{1,2},{2,3},{3,4},{4,5},{5,6},{6,7},{7,8},{8,9},{9,10},{10,1... | collective-permute-start | bytes 276488 | tf_op jit(solution)/shard_map/ppermute | solution.py:20
  94.4 3.0 %copy-start.2 = (f32[6,24,32,320]{3,2,1,0:T(8,128)S(1)}, f32[6,24,32,320]{3,2,1,0:T(8,128)}, u32[]{:S(2)}) copy-start(f32[6,24,32,320]{3,2,1,0:T(8,128)} %copy-done.1) | copy-start | bytes 17694724
  97.4 2.0 %copy-start.8 = (f32[3,24,32,320]{3,2,1,0:T(8,128)S(1)}, f32[3,24,32,320]{3,2,1,0:T(8,128)}, u32[]{:S(2)}) copy-start(f32[3,24,32,320]{3,2,1,0:T(8,128)} %copy-done.7) | copy-start | bytes 8847364
  99.4 14.3 %copy-start.3 = (f32[6,24,32,320]{3,2,1,0:T(8,128)S(1)}, f32[6,24,32,320]{3,2,1,0:T(8,128)}, u32[]{:S(2)}) copy-start(f32[6,24,32,320]{3,2,1,0:T(8,128)} %copy-done.1) | copy-start | bytes 17694724
  99.4 14.3 %copy-start.9 = (f32[3,24,32,320]{3,2,1,0:T(8,128)S(1)}, f32[3,24,32,320]{3,2,1,0:T(8,128)}, u32[]{:S(2)}) copy-start(f32[3,24,32,320]{3,2,1,0:T(8,128)} %copy-done.7) | copy-start | bytes 8847364
  99.4 14.3 %copy-start.14 = (f32[24,32,320]{2,1,0:T(8,128)S(1)}, f32[24,32,320]{2,1,0:T(8,128)}, u32[]{:S(2)}) copy-start(f32[24,32,320]{2,1,0:T(8,128)} %refs_3_.5) | copy-start | bytes 2949124
  99.4 14.3 %copy-start.16 = (f32[24,32,320]{2,1,0:T(8,128)S(1)}, f32[24,32,320]{2,1,0:T(8,128)}, u32[]{:S(2)}) copy-start(f32[24,32,320]{2,1,0:T(8,128)} %refs_4_.5) | copy-start | bytes 2949124
  101.0 12.7 %collective-permute-start.6 = (f32[3,32,320]{2,1,0:T(8,128)S(1)}, f32[3,32,320]{2,1,0:T(8,128)S(1)}, u32[]{:S(2)}, u32[]{:S(2)}) collective-permute-start(f32[3,32,320]{2,1,0:T(8,128)S(1)} %get-tuple-element.26), channel_id=1, source_target_pairs={{16,0},{32,16},{48,32},{64,48},{80,64},{96,80},{112,96},{17,1},{33... | collective-permute-start | bytes 368648 | tf_op jit(solution)/shard_map/ppermute | solution.py:20
  105.5 8.2 %collective-permute-start.7 = (f32[3,24,320]{2,1,0:T(8,128)S(1)}, f32[3,24,320]{2,1,0:T(8,128)S(1)}, u32[]{:S(2)}, u32[]{:S(2)}) collective-permute-start(f32[3,24,320]{2,1,0:T(8,128)S(1)} %get-tuple-element.27), channel_id=1, source_target_pairs={{1,0},{2,1},{3,2},{4,3},{5,4},{6,5},{7,6},{8,7},{9,8},{10,9},{11,1... | collective-permute-start | bytes 276488 | tf_op jit(solution)/shard_map/ppermute | solution.py:20
  (6 other events, 5.8 us)

commit v3 on v2

v3 whole, which is shorter than its diff:
```python
import functools

import jax
import jax.numpy as jnp
from jax import lax
from jax.experimental import pallas as pl
from jax.experimental.pallas import tpu as pltpu
from jax.sharding import PartitionSpec as P

time_step = 0.2
precise = lax.Precision.HIGHEST
strip = 8
lanes = 128
per = 3


def neighbour(value, axis, by):
    size = lax.axis_size(axis)
    pairs = [(i, i + by) for i in range(size) if 0 <= i + by < size]
    return lax.ppermute(value, axis, pairs)


def in_hbm(value):
    return pltpu.with_memory_space_constraint(value, pltpu.HBM)


def in_vmem(value):
    return pltpu.with_memory_space_constraint(value, pltpu.VMEM)


def f32(*shape):
    return jax.ShapeDtypeStruct(shape, jnp.float32)


def dot(a, b, contract=((1,), (0,))):
    return lax.dot_general(
        a, b, (contract, ((), ())), precision=precise, preferred_element_type=jnp.float32
    )


def shifted_up(values):
    first = jnp.zeros((values.shape[0], 1), jnp.float32)
    return jnp.concatenate([first, values[:, :-1]], 1)


def shifted_down(values):
    last = jnp.zeros((values.shape[0], 1), jnp.float32)
    return jnp.concatenate([values[:, 1:], last], 1)


def after_row(values, row):
    where = lax.broadcasted_iota(jnp.int32, values.shape, 0)
    return jnp.where(where == 0, row, pltpu.roll(values, 1, 0))


def partial_velocity(stress, velocity, factor, out, before):
    xx, yy, zz, xy, xz, yz = stress
    along_x, along_y = before
    out[0] = velocity[0] + factor * (
        (xx - along_x(xx)) + (xy - along_y(xy)) + (xz - shifted_up(xz))
    )
    out[1] = velocity[1] + factor * (
        (xy - along_x(xy)) + (yy - along_y(yy)) + (yz - shifted_up(yz))
    )
    out[2] = velocity[2] + factor * (
        (xz - along_x(xz)) + (yz - along_y(yz)) + (zz - shifted_up(zz))
    )


def nothing(values):
    return jnp.zeros_like(values)


def row_before(values):
    return after_row(values, 0.0)


def edges_kernel(stress, velocity, buoyancy, attenuation, *refs):
    out_plane, out_rows, part_plane, part_rows, b_plane, b_rows = refs[:6]
    s_plane, s_rows, v_plane, v_rows, sems = refs[6:]
    _, nx, ny, _ = stress.shape
    moves = [
        (stress.at[:, 0], s_plane),
        (stress.at[:, :, 0], s_rows),
        (velocity.at[:, 0], v_plane),
        (velocity.at[:, :, 0], v_rows),
        (buoyancy.at[0], b_plane),
        (buoyancy.at[:, 0], b_rows),
        (stress.at[0, nx - 1], out_plane.at[0]),
        (stress.at[3:5, nx - 1], out_plane.at[1:3]),
        (attenuation.at[nx - 1], out_plane.at[3]),
        (stress.at[3, :, ny - 1], out_rows.at[0]),
        (stress.at[1, :, ny - 1], out_rows.at[1]),
        (stress.at[5, :, ny - 1], out_rows.at[2]),
        (attenuation.at[:, ny - 1], out_rows.at[3]),
    ]
    copies = [pltpu.make_async_copy(*move, sems.at[k]) for k, move in enumerate(moves)]
    for copy in copies:
        copy.start()
    for copy in copies:
        copy.wait()
    partial_velocity(
        [s_plane[c] for c in range(6)],
        [v_plane[c] for c in range(3)],
        time_step * b_plane[...],
        part_plane,
        (nothing, row_before),
    )
    partial_velocity(
        [s_rows[c] for c in range(6)],
        [v_rows[c] for c in range(3)],
        time_step * b_rows[...],
        part_rows,
        (row_before, nothing),
    )


def edges(stress, velocity, buoyancy, attenuation):
    _, nx, ny, nz = stress.shape
    return pl.pallas_call(
        edges_kernel,
        in_specs=[pl.BlockSpec(memory_space=pltpu.HBM)] * 4,
        out_shape=(
            f32(4, ny, nz),
            f32(4, nx, nz),
            f32(3, ny, nz),
            f32(3, nx, nz),
            f32(ny, nz),
            f32(nx, nz),
        ),
        scratch_shapes=[
            pltpu.VMEM((6, ny, nz), jnp.float32),
            pltpu.VMEM((6, nx, nz), jnp.float32),
            pltpu.VMEM((3, ny, nz), jnp.float32),
            pltpu.VMEM((3, nx, nz), jnp.float32),
            pltpu.SemaphoreType.DMA((13,)),
        ],
        compiler_params=pltpu.CompilerParams(vmem_limit_bytes=8 << 20),
        name="edges",
    )(*map(in_hbm, (stress, velocity, buoyancy, attenuation)))


def take_halo(part_plane, part_rows, b_plane, b_rows, plane, rows, out_plane, out_rows):
    factor_plane, factor_rows = time_step * b_plane[...], time_step * b_rows[...]
    for c in range(3):
        first_row = lax.broadcasted_iota(jnp.int32, factor_plane.shape, 0) == 0
        corner = jnp.where(first_row, rows[c, 0:1], 0.0)
        out_plane[c] = part_plane[c] - factor_plane * (plane[c] + corner)
        first_row = lax.broadcasted_iota(jnp.int32, factor_rows.shape, 0) == 0
        corner = jnp.where(first_row, plane[c, 0:1], 0.0)
        out_rows[c] = part_rows[c] - factor_rows * (rows[c] + corner)


def first_edges(part_plane, part_rows, b_plane, b_rows, plane, rows):
    return pl.pallas_call(
        take_halo,
        out_shape=(f32(*part_plane.shape), f32(*part_rows.shape)),
        compiler_params=pltpu.CompilerParams(vmem_limit_bytes=8 << 20),
        name="first_edges",
    )(part_plane, part_rows, b_plane, b_rows, plane, rows)


def sections_kernel(size_x, size_y, columns, planes, weight_y, weight_z, out, held):
    own = planes.shape[0]
    box_y, box_z = weight_y.shape[0], weight_z.shape[0]
    part = box_y // (columns * size_x)
    out[...] = jnp.zeros_like(out)
    held[...] = jnp.zeros_like(held)
    for t in range(own):
        partly = dot(weight_y[...], planes[t])
        held[t, strip : strip + box_y, :box_z] = dot(partly, weight_z[...], ((1,), (1,)))
    for k in range(columns):
        for i in range(size_x):
            start = strip + (k * size_x + i) * part - 1
            for t in range(own):
                piece = held[t, start : start + part + 1]
                row = t * (part + 1)
                out[i * size_y + size_y - columns + k, row : row + part + 1] = piece


def sections(planes, weight_y, weight_z, size_x, size_y, columns, height):
    own = planes.shape[0]
    return pl.pallas_call(
        functools.partial(sections_kernel, size_x, size_y, columns),
        out_shape=f32(size_x * size_y, height, lanes),
        scratch_shapes=[pltpu.VMEM((own, strip + weight_y.shape[0], lanes), jnp.float32)],
        compiler_params=pltpu.CompilerParams(vmem_limit_bytes=16 << 20),
        name="sections",
    )(planes, weight_y, weight_z)


def contract_kernel(own, part, nx, anchor, weight_x, gathered, out, padded):
    box_x, count = weight_x.shape
    size_x, height, _ = out.shape
    rows = height // (part + 1)
    devices = count // own
    stride = gathered.shape[0] // devices
    section = lax.broadcasted_iota(jnp.int32, (count, count), 0)
    column = lax.broadcasted_iota(jnp.int32, (count, count), 1)
    pick = section == own * lax.rem(column, devices) + lax.div(column, devices)
    weights = dot(weight_x[...], pick.astype(jnp.float32))
    padded[...] = jnp.zeros_like(padded)
    for r in range(part + 1):
        terms = [
            gathered[pl.ds(t * (part + 1) + r, devices, stride=stride), :] for t in range(own)
        ]
        box = dot(weights, jnp.concatenate(terms, 0))
        padded[r, pl.ds(anchor[0] + strip, box_x), :] = box
    for i in range(size_x):
        start = strip + i * nx
        for r in range(part + 1):
            out[i, r * rows : r * rows + nx] = padded[r, start : start + nx]
            out[i, r * rows + nx : (r + 1) * rows] = padded[r, start - 1 : start - 1 + rows - nx]


def contract(anchor, weight_x, gathered, own, part, nx, size_x, rows):
    return pl.pallas_call(
        functools.partial(contract_kernel, own, part, nx),
        in_specs=[
            pl.BlockSpec(memory_space=pltpu.SMEM),
            pl.BlockSpec(memory_space=pltpu.VMEM),
            pl.BlockSpec(memory_space=pltpu.VMEM),
        ],
        out_shape=f32(size_x, (part + 1) * rows, lanes),
        scratch_shapes=[pltpu.VMEM((part + 1, 2 * strip + size_x * nx, lanes), jnp.float32)],
        compiler_params=pltpu.CompilerParams(vmem_limit_bytes=16 << 20),
        name="contract",
    )(anchor, weight_x, gathered)


def place_kernel(part, *refs):
    anchor, box, cells, rate_plane, rate_rows = refs[:5]
    part_plane, part_rows, b_plane, b_rows, plane, rows = refs[5:11]
    out, out_plane, out_rows, first_plane, first_rows, held = refs[11:]
    size_x, height, _ = box.shape
    _, ny, nz = out.shape
    nx = out.shape[0] - 1
    span = height // (part + 1)
    for i in range(size_x):
        for r in range(part):
            y = i * part + r
            first = (r + 1) * span
            held[pl.ds(y, nx, stride=ny), :] = box[i, first : first + nx]
            held[nx * ny + y : nx * ny + y + 1] = box[i, first + nx : first + nx + 1]
    cell = lax.broadcasted_iota(jnp.int32, (lanes, nz), 1)
    which = lax.broadcasted_iota(jnp.int32, (lanes, nz), 0)
    pick = (cell - anchor[2] == which).astype(jnp.float32)

    def lost(values, rates):
        return (-time_step) * jnp.exp(-time_step * rates) * dot(values, pick)

    for t in range(0, nx, 4):
        values = (-time_step) * dot(held[t * ny : (t + 4) * ny], pick)
        for u in range(4):
            decay = jnp.exp(-time_step * cells[3, t + u])
            out[t + u + 1] = decay * values[u * ny : (u + 1) * ny]
    out[0] = jnp.zeros((ny, nz), jnp.float32)
    q_plane = lost(held[nx * ny :], rate_plane[3])
    q_rows = lost(box[0, 0:nx], rate_rows[3])
    out_plane[...] = q_plane
    out_rows[...] = q_rows
    take_halo(part_plane, part_rows, b_plane, b_rows, plane, rows, first_plane, first_rows)
    factor = time_step * b_plane[...]
    own = out[1]
    first_plane[0] = first_plane[0] + factor * (own - q_plane)
    first_plane[1] = first_plane[1] + factor * (own - after_row(own, q_rows[0:1]))
    first_plane[2] = first_plane[2] + factor * (own - shifted_up(own))
    factor = time_step * b_rows[...]
    own = out[1:, 0]
    first_rows[0] = first_rows[0] + factor * (own - after_row(own, q_plane[0:1]))
    first_rows[1] = first_rows[1] + factor * (own - q_rows)
    first_rows[2] = first_rows[2] + factor * (own - shifted_up(own))


def place(anchor, box, cells, rate_plane, rate_rows, halo, part):
    nx, ny, nz = cells.shape[1] - 1, *cells.shape[2:]
    on_chip = pl.BlockSpec(memory_space=pltpu.VMEM)
    return pl.pallas_call(
        functools.partial(place_kernel, part),
        in_specs=[pl.BlockSpec(memory_space=pltpu.SMEM)] + [on_chip] * (4 + len(halo)),
        out_specs=(on_chip,) * 5,
        out_shape=(
            pltpu.VMEM((nx + 1, ny, nz), jnp.float32),
            f32(ny, nz),
            f32(nx, nz),
            f32(3, ny, nz),
            f32(3, nx, nz),
        ),
        scratch_shapes=[pltpu.VMEM(((nx + 1) * ny, lanes), jnp.float32)],
        compiler_params=pltpu.CompilerParams(vmem_limit_bytes=12 << 20),
        name="place",
    )(anchor, box, in_vmem(cells), rate_plane, rate_rows, *halo)


def step_kernel(with_source, *refs):
    if with_source:
        source, plane, rows, upper_plane, upper_rows, source_plane, source_rows = refs[3:10]
        out_velocity, out_stress, stress, velocity = refs[10:14]
        cells, out_sems = refs[2], refs[14]
    else:
        fields, (plane, rows, upper_plane, upper_rows) = refs[:6], refs[6:10]
        stress, velocity, cells, last_plane, last_rows, part_plane, part_rows = refs[10:17]
        in_sems = refs[17]
    nx, ny, nz = cells.shape[1] - 1, *cells.shape[2:]
    chunks = nx // per

    def arriving(k):
        here, above = pl.ds(k * per, per), pl.ds(k * per + 1, per)
        moves = [
            (fields[0].at[:, here], stress.at[:, above]),
            (fields[1].at[:, here], velocity.at[:, here]),
        ]
        for n, field in enumerate(fields[2:6]):
            moves.append((field.at[here], cells.at[n, here]))
        return [pltpu.make_async_copy(*m, in_sems.at[k, n]) for n, m in enumerate(moves)]

    def leaving(k):
        here, above = pl.ds(k * per, per), pl.ds(k * per + 1, per)
        moves = [
            (velocity.at[:, here], out_velocity.at[:, here]),
            (stress.at[:, above], out_stress.at[:, here]),
        ]
        return [pltpu.make_async_copy(*m, out_sems.at[k, n]) for n, m in enumerate(moves)]

    def every(make, act):
        def one(n, _):
            for copy in make(chunks - 1 - n):
                act(copy)
            return 0

        lax.fori_loop(0, chunks, one, 0)

    if not with_source:
        every(arriving, lambda copy: copy.start())
    for c, which in enumerate((0, 3, 4)):
        stress[which, 0] = plane[c]
        velocity[c, nx] = upper_plane[c]
    if with_source:
        stress[0, 0] = plane[0] + source_plane[...]

    top = lax.broadcasted_iota(jnp.int32, (strip, nz), 0) == 0
    bottom = lax.broadcasted_iota(jnp.int32, (strip, nz), 0) == strip - 1

    def velocity_plane(x):
        above = [rows[c, pl.ds(x, 1)] for c in range(3)]
        if with_source:
            above[1] = above[1] + source_rows[pl.ds(x, 1)]
        above = [jnp.broadcast_to(row, (strip, nz)) for row in above]
        for r in range(ny // strip):
            here = slice(strip * r, strip * (r + 1))
            s = [stress[c, x + 1, here] for c in range(6)]
            before = [stress[c, x, here] for c in (0, 3, 4)]
            if with_source:
                extra = source[x + 1, here]
                s[:3] = [value + extra for value in s[:3]]
                before[0] = before[0] + source[x, here]
            s_xx, s_yy, s_zz, s_xy, s_xz, s_yz = s
            rolled = [pltpu.roll(value, 1, 0) for value in (s_xy, s_yy, s_yz)]
            up = [jnp.where(top, above[c], rolled[c]) for c in range(3)]
            factor = time_step * cells[0, x, here]
            sums = (
                (s_xx - before[0]) + (s_xy - up[0]) + (s_xz - shifted_up(s_xz)),
                (s_xy - before[1]) + (s_yy - up[1]) + (s_yz - shifted_up(s_yz)),
                (s_xz - before[2]) + (s_yz - up[2]) + (s_zz - shifted_up(s_zz)),
            )
            for c in range(3):
                velocity[c, x, here] = velocity[c, x, here] + factor * sums[c]
            above = rolled

    def stress_plane(x):
        below = [jnp.broadcast_to(upper_rows[c, pl.ds(x, 1)], (strip, nz)) for c in range(3)]
        for r in reversed(range(ny // strip)):
            here = slice(strip * r, strip * (r + 1))
            v = [velocity[c, x, here] for c in range(3)]
            rolled = [pltpu.roll(value, strip - 1, 0) for value in v]
            in_x = [velocity[c, x + 1, here] - v[c] for c in range(3)]
            in_y = [jnp.where(bottom, below[c], rolled[c]) - v[c] for c in range(3)]
            in_z = [shifted_down(v[c]) - v[c] for c in range(3)]
            decay = jnp.exp(-time_step * cells[3, x, here])
            shear = time_step * cells[2, x, here]
            normal = [in_x[0], in_y[1], in_z[2]]
            common = time_step * cells[1, x, here] * (normal[0] + normal[1] + normal[2])
            twice = 2.0 * shear
            if with_source:
                extra = source[x + 1, here]
                common = common + extra
            values = []
            for c in range(3):
                value = decay * (stress[c, x + 1, here] + (common + twice * normal[c]))
                values.append(value + extra if with_source else value)
            for c, (a, b) in enumerate(
                ((in_y[0], in_x[1]), (in_z[0], in_x[2]), (in_z[1], in_y[2])), 3
            ):
                values.append(decay * (stress[c, x + 1, here] + shear * (a + b)))
            for c in range(6):
                stress[c, x + 1, here] = values[c]
            if not with_source and r == ny // strip - 1:
                for c, which in enumerate((3, 1, 5)):
                    last_rows[c, pl.ds(x, 1)] = values[which][strip - 1 :]
            below = rolled

    def one_chunk(n, _):
        k = chunks - 1 - n

        if not with_source:

            @pl.when(k > 0)
            def _():
                for copy in arriving(k - 1):
                    copy.wait()

        def one_plane(m, _):
            x = k * per + (per - 1 - m)
            velocity_plane(x)
            stress_plane(x)
            return 0

        lax.fori_loop(0, per, one_plane, 0)
        if with_source:
            for copy in leaving(k):
                copy.start()
        return 0

    if not with_source:
        for copy in arriving(chunks - 1):
            copy.wait()
    lax.fori_loop(0, chunks, one_chunk, 0)
    if with_source:
        every(leaving, lambda copy: copy.wait())
    else:
        for c, which in enumerate((0, 3, 4)):
            last_plane[c] = stress[which, nx]
        partial_velocity(
            [stress[c, 1] for c in range(6)],
            [velocity[c, 0] for c in range(3)],
            time_step * cells[0, 0],
            part_plane,
            (nothing, row_before),
        )
        partial_velocity(
            [stress[c, 1:, 0] for c in range(6)],
            [velocity[c, :nx, 0] for c in range(3)],
            time_step * cells[0, :nx, 0],
            part_rows,
            (row_before, nothing),
        )


def estimate(nx, ny, nz, words):
    count = nx * ny * nz
    return pl.CostEstimate(
        flops=100 * count, bytes_accessed=4 * words * count, transcendentals=count
    )


def first_step(stress, velocity, coefficients, plane, rows, upper_plane, upper_rows):
    _, nx, ny, nz = velocity.shape
    fields = [in_hbm(a) for a in (stress, velocity, *coefficients)]
    on_chip = pl.BlockSpec(memory_space=pltpu.VMEM)
    return pl.pallas_call(
        functools.partial(step_kernel, False),
        in_specs=[pl.BlockSpec(memory_space=pltpu.HBM)] * len(fields) + [on_chip] * 4,
        out_specs=(on_chip,) * 7,
        out_shape=(
            *[pltpu.VMEM((n, nx + 1, ny, nz), jnp.float32) for n in (6, 3, 4)],
            *[f32(3, ny, nz), f32(3, nx, nz)] * 2,
        ),
        scratch_shapes=[pltpu.SemaphoreType.DMA((nx // per, len(fields)))],
        compiler_params=pltpu.CompilerParams(vmem_limit_bytes=20 << 20),
        cost_estimate=estimate(nx, ny, nz, 13),
        name="first_step",
    )(*fields, plane, rows, upper_plane, upper_rows)


def second_step(stress, velocity, cells, source, edges):
    _, nx, ny, nz = cells.shape
    nx = nx - 1
    held = [in_vmem(a) for a in (stress, velocity, cells, source)]
    on_chip = pl.BlockSpec(memory_space=pltpu.VMEM)
    out = pl.pallas_call(
        functools.partial(step_kernel, True),
        in_specs=[on_chip] * (len(held) + len(edges)),
        out_specs=(pl.BlockSpec(memory_space=pltpu.HBM),) * 2 + (on_chip,) * 2,
        out_shape=(
            *[pltpu.HBM((n, nx, ny, nz), jnp.float32) for n in (3, 6)],
            *[pltpu.VMEM(a.shape, jnp.float32) for a in (stress, velocity)],
        ),
        input_output_aliases={0: 2, 1: 3},
        scratch_shapes=[pltpu.SemaphoreType.DMA((nx // per, 2))],
        compiler_params=pltpu.CompilerParams(vmem_limit_bytes=20 << 20),
        cost_estimate=estimate(nx, ny, nz, 9),
        name="second_step",
    )(*held, *edges)
    return out[0], out[1]


def shards(
    source_planes,
    weight_x,
    weight_y,
    weight_z,
    box_anchor,
    velocity,
    stress,
    lame_lambda,
    lame_mu,
    buoyancy,
    attenuation,
):
    nx, ny, nz = lame_mu.shape
    box_x, sources = weight_x.shape
    box_y = weight_y.shape[0]
    size_x, size_y = lax.axis_size("gx"), lax.axis_size("gy")
    own = source_planes.shape[0]
    columns = box_y // ny
    part = ny // size_x
    height = -(-own * (part + 1) // strip) * strip
    coefficients = (buoyancy, lame_lambda, lame_mu, attenuation)

    pieces = sections(source_planes, weight_y, weight_z, size_x, size_y, columns, height)
    gathered = lax.all_to_all(pieces, ("gx", "gy"), 0, 0, tiled=True)
    send_x, send_y, *parts = edges(stress, velocity, buoyancy, attenuation)
    plane = neighbour(send_x, "gx", 1)
    rows = neighbour(send_y, "gy", 1)
    first_x, first_y = first_edges(*parts, plane, rows)

    gathered, first_x, first_y = lax.optimization_barrier((gathered, first_x, first_y))
    gathered = gathered.reshape(size_x * size_y * height, lanes)
    shares = contract(box_anchor, weight_x, gathered, own, part, nx, size_x, nx + strip)
    shares, first_x, first_y = lax.optimization_barrier((shares, first_x, first_y))
    box = lax.all_to_all(shares, "gx", 0, 0, tiled=True)
    upper_x = neighbour(first_x, "gx", -1)
    upper_y = neighbour(first_y, "gy", -1)
    box, upper_x, upper_y = lax.optimization_barrier((box, upper_x, upper_y))

    strained, speed, cells, last_x, last_y, *parts[:2] = first_step(
        stress, velocity, coefficients, plane, rows, upper_x, upper_y
    )
    lower_x = neighbour(last_x, "gx", 1)
    lower_y = neighbour(last_y, "gy", 1)
    halo = (*parts, lower_x, lower_y)
    *source, first_x, first_y = place(box_anchor, box, cells, plane, rows, halo, part)
    upper_x = neighbour(first_x, "gx", -1)
    upper_y = neighbour(first_y, "gy", -1)
    moved = (lower_x, lower_y, upper_x, upper_y, *source[1:])
    return second_step(strained, speed, cells, source[0], moved)


def solution(mesh):
    in_specs = (
        P(("gx", "gy"), None, None),
        P(),
        P(),
        P(),
        P(),
        P(None, "gx", "gy", None),
        P(None, "gx", "gy", None),
        P("gx", "gy", None),
        P("gx", "gy", None),
        P("gx", "gy", None),
        P("gx", "gy", None),
    )
    out_specs = (P(None, "gx", "gy", None), P(None, "gx", "gy", None))
    return jax.shard_map(shards, mesh=mesh, in_specs=in_specs, out_specs=out_specs, check_vma=False)
```

time: 124 us -> 98.1 us (0.79)
  blocking collectives: 26.2 us -> 0 us
  local copies, waits for them, and re-layouts: 20.1 us -> 3.3 us
  starting transfers between devices: 34.4 us -> 46.2 us
  waiting for transfers between devices: 15 us -> 21.7 us
    all_to_all x1 -> x0, blocking collectives: 26.2 us -> none  [shards(): gathered = lax.all_to_all(pieces, ('gx', 'gy'), 0, 0, tiled=True)]
    unnamed x58 -> x10, local copies, waits for them, and re-layouts: 20.1 us -> 3.3 us
    all_to_all x0 -> x1, starting transfers between devices: none -> 10.4 us  [shards(): gathered = lax.all_to_all(pieces, ('gx', 'gy'), 0, 0, tiled=True)]
    ppermute x8, waiting for transfers between devices: 15 us -> 21.7 us  [neighbour(): return lax.ppermute(value, axis, pairs)]
    pallas_call x5 -> x4, Pallas kernels: 20.4 us -> 17.8 us  [the longest x1 8.38 us: first_step(): pl.pallas_call(functools.partial(step_kernel, False), in_specs=[pl.BlockS...]
    all_to_all x1, starting transfers between devices: 4.37 us -> 5.82 us  [shards(): box = lax.all_to_all(shares, 'gx', 0, 0, tiled=True)]
  transfers between devices with their start and end apart: 9 -> 10, of which waited for: 3 -> 5; matrix products, arithmetic and copies ran while one was open for 0% -> 0% of each run, Pallas kernels for 9% -> 2%
where the time goes in v3:
time: 98.1 us; the launch traced here: 97.5 us
  starting transfers between devices  46.2 us (47%)
  Pallas kernels  25.6 us (26%)
  waiting for transfers between devices  21.7 us (22%)
  local copies, waits for them, and re-layouts  3.3 us (3%)
    ppermute x8, starting transfers between devices, neighbour(): return lax.ppermute(value, axis, pairs)  29.9 us
    ppermute x8, waiting for transfers between devices, neighbour(): return lax.ppermute(value, axis, pairs)  21.7 us
    all_to_all x1, starting transfers between devices, shards(): gathered = lax.all_to_all(pieces, ('gx', 'gy'), 0, 0, tiled=True)  10.4 us
    pallas_call x1, Pallas kernels, first_step(): pl.pallas_call(functools.partial(step_kernel, False), in_specs=[pl.BlockS...  8.38 us
    pallas_call x1, Pallas kernels, second_step(): pl.pallas_call(functools.partial(step_kernel, True), in_specs=[on_chip] *...  7.76 us
    all_to_all x1, starting transfers between devices, shards(): box = lax.all_to_all(shares, 'gx', 0, 0, tiled=True)  5.82 us
    unnamed x10, local copies, waits for them, and re-layouts  3.3 us
    pallas_call x1, Pallas kernels, sections(): pl.pallas_call(functools.partial(sections_kernel, size_x, size_y, columns...  3.04 us
  transfers between devices with their start and end apart: 10, of which 5 were waited for; matrix products, arithmetic and copies ran while one was open for 0% of the time, Pallas kernels for 2%

profile of v3, /device:TPU:57, one launch (start us, length us, event | category | flops | bytes accessed | tf_op | source)
XLA Modules:
  0.0 97.5 jit_solution(14553990150577133123)
XLA Ops:
  0.6 0.0 copy-start
  0.6 1.5 %copy-done = f32[3,384,384]{2,1,0:T(8,128)S(1)} copy-done((f32[3,384,384]{2,1,0:T(8,128)S(1)}, f32[3,384,384]{2,1,0:T(8,128)}, u32[]{:S(2)}) %copy-start) | copy-done | bytes 1769496
  2.1 0.9 copy-done.1
  3.0 0.9 copy-done.2
  3.9 3.0 %sections.1 = f32[128,16,128]{2,1,0:T(8,128)} custom-call(f32[3,384,384]{2,1,0:T(8,128)S(1)} %copy-done, f32[96,384]{1,0:T(8,128)S(1)} %copy-done.1, f32[96,384]{1,0:T(8,128)S(1)} %copy-done.2), custom_call_target="tpu_custom_call" | custom-call | tf_op jit(solution)/shard_map/sections/pallas_call | solution.py:183
  7.0 10.4 %all-to-all-start = ((f32[128,16,128]{2,1,0:T(8,128)}), f32[128,16,128]{2,1,0:T(8,128)S(1)}, u32[]{:S(2)}, u32[]{:S(2)}) async-start(f32[128,16,128]{2,1,0:T(8,128)} %sections.1), calls=%async_computation | async-start | bytes 2097152 | tf_op jit(solution)/shard_map/all_to_all | solution.py:521
  17.4 0.0 copy-start.3
  17.4 0.0 copy-start.4
  17.4 1.6 %edges.1 = (f32[4,32,320]{2,1,0:T(8,128)S(1)}, f32[4,24,320]{2,1,0:T(8,128)S(1)}, f32[3,32,320]{2,1,0:T(8,128)S(1)}, f32[3,24,320]{2,1,0:T(8,128)S(1)}, f32[32,320]{1,0:T(8,128)S(1)}, /*index=5*/f32[24,320]{1,0:T(8,128)S(1)}) custom-call(f32[6,24,32,320]{3,2,1,0:T(8,128)} %refs_0_.2, f32[3,24,32,320]{3,2,1,0:T(8,128)} %refs_1_.1, f32[24,32,320]{2,1,0:T(8,128)} %refs_2_.1, ...), custom_call_target="tpu_custom_call" | custom-call | tf_op jit(solution)/shard_map/edges/pallas_call | solution.py:120
  19.0 4.6 %collective-permute-start = (f32[4,32,320]{2,1,0:T(8,128)S(1)}, f32[4,32,320]{2,1,0:T(8,128)S(1)}, u32[]{:S(2)}, u32[]{:S(2)}) collective-permute-start(f32[4,32,320]{2,1,0:T(8,128)S(1)} %get-tuple-element.33), channel_id=1, source_target_pairs={{0,16},{16,32},{32,48},{48,64},{64,80},{80,96},{96,112},{1,17},{17... | collective-permute-start | bytes 491528 | tf_op jit(solution)/shard_map/ppermute | solution.py:20
  23.6 2.5 %collective-permute-start.1 = (f32[4,24,320]{2,1,0:T(8,128)S(1)}, f32[4,24,320]{2,1,0:T(8,128)S(1)}, u32[]{:S(2)}, u32[]{:S(2)}) collective-permute-start(f32[4,24,320]{2,1,0:T(8,128)S(1)} %get-tuple-element.34), channel_id=1, source_target_pairs={{0,1},{1,2},{2,3},{3,4},{4,5},{5,6},{6,7},{7,8},{8,9},{9,10},{10,1... | collective-permute-start | bytes 368648 | tf_op jit(solution)/shard_map/ppermute | solution.py:20
  26.2 8.1 %collective-permute-done.1.rows.refs_7_.refs_4_ = f32[4,24,320]{2,1,0:T(8,128)S(1)} collective-permute-done((f32[4,24,320]{2,1,0:T(8,128)S(1)}, f32[4,24,320]{2,1,0:T(8,128)S(1)}, u32[]{:S(2)}, u32[]{:S(2)}) %collective-permute-start.1) | collective-permute-done | bytes 122912 | tf_op jit(solution)/shard_map/ppermute | solution.py:20
  34.3 1.1 %collective-permute-done.plane.refs_6_.refs_3_ = f32[4,32,320]{2,1,0:T(8,128)S(1)} collective-permute-done((f32[4,32,320]{2,1,0:T(8,128)S(1)}, f32[4,32,320]{2,1,0:T(8,128)S(1)}, u32[]{:S(2)}, u32[]{:S(2)}) %collective-permute-start) | collective-permute-done | bytes 163872 | tf_op jit(solution)/shard_map/ppermute | solution.py:20
  35.4 0.0 all-to-all-done
  35.5 2.7 %contract.1 = f32[8,160,128]{2,1,0:T(8,128)} custom-call(s32[3]{0:T(128)S(1)} %copy-done.4, f32[64,384]{1,0:T(8,128)S(1)} %copy-done.3, f32[2048,128]{1,0:T(8,128)S(1)} %bitcast.1), custom_call_target="tpu_custom_call" | custom-call | tf_op jit(solution)/shard_map/contract/pallas_call | solution.py:217
  38.1 5.8 %all-to-all-start.1 = ((f32[8,160,128]{2,1,0:T(8,128)}), f32[8,160,128]{2,1,0:T(8,128)S(1)}, u32[]{:S(2)}, u32[]{:S(2)}) async-start(f32[8,160,128]{2,1,0:T(8,128)} %contract.1), calls=%async_computation.1 | async-start | bytes 1310720 | tf_op jit(solution)/shard_map/all_to_all | solution.py:531
  44.0 4.6 %collective-permute-start.2 = (f32[3,32,320]{2,1,0:T(8,128)S(1)}, f32[3,32,320]{2,1,0:T(8,128)S(1)}, u32[]{:S(2)}, u32[]{:S(2)}) collective-permute-start(f32[3,32,320]{2,1,0:T(8,128)S(1)} %get-tuple-element.45), channel_id=1, source_target_pairs={{16,0},{32,16},{48,32},{64,48},{80,64},{96,80},{112,96},{17,1},{33... | collective-permute-start | bytes 368648 | tf_op jit(solution)/shard_map/ppermute | solution.py:20
  48.6 3.0 %collective-permute-start.3 = (f32[3,24,320]{2,1,0:T(8,128)S(1)}, f32[3,24,320]{2,1,0:T(8,128)S(1)}, u32[]{:S(2)}, u32[]{:S(2)}) collective-permute-start(f32[3,24,320]{2,1,0:T(8,128)S(1)} %get-tuple-element.46), channel_id=1, source_target_pairs={{1,0},{2,1},{3,2},{4,3},{5,4},{6,5},{7,6},{8,7},{9,8},{10,9},{11,1... | collective-permute-start | bytes 276488 | tf_op jit(solution)/shard_map/ppermute | solution.py:20
  51.6 6.4 %collective-permute-done.3.refs_9_ = f32[3,24,320]{2,1,0:T(8,128)S(1)} collective-permute-done((f32[3,24,320]{2,1,0:T(8,128)S(1)}, f32[3,24,320]{2,1,0:T(8,128)S(1)}, u32[]{:S(2)}, u32[]{:S(2)}) %collective-permute-start.3) | collective-permute-done | bytes 92192 | tf_op jit(solution)/shard_map/ppermute | solution.py:20
  58.0 0.0 collective-permute-done.2.refs_8_
  58.0 0.0 all-to-all-done.1.refs_1_
  58.0 8.4 %first_step.1 = (f32[6,25,32,320]{3,2,1,0:T(8,128)S(1)}, f32[3,25,32,320]{3,2,1,0:T(8,128)S(1)}, f32[4,25,32,320]{3,2,1,0:T(8,128)S(1)}, f32[3,32,320]{2,1,0:T(8...) custom-call(f32[6,24,32,320]{3,2,1,0:T(8,128)} %refs_0_.2, ...), custom_call_target="tpu_custom_call" | custom-call | flops 24576000 | bytes 12779520 | tf_op jit(solution)/shard_map/first_step/pallas_call | solution.py:460
  66.4 3.7 %collective-permute-start.4 = (f32[3,32,320]{2,1,0:T(8,128)S(1)}, f32[3,32,320]{2,1,0:T(8,128)S(1)}, u32[]{:S(2)}, u32[]{:S(2)}) collective-permute-start(f32[3,32,320]{2,1,0:T(8,128)S(1)} %get-tuple-element.55), channel_id=1, source_target_pairs={{0,16},{16,32},{32,48},{48,64},{64,80},{80,96},{96,112},{1,17},{17... | collective-permute-start | bytes 368648 | tf_op jit(solution)/shard_map/ppermute | solution.py:20
  70.1 3.8 %collective-permute-start.5 = (f32[3,24,320]{2,1,0:T(8,128)S(1)}, f32[3,24,320]{2,1,0:T(8,128)S(1)}, u32[]{:S(2)}, u32[]{:S(2)}) collective-permute-start(f32[3,24,320]{2,1,0:T(8,128)S(1)} %get-tuple-element.56), channel_id=1, source_target_pairs={{0,1},{1,2},{2,3},{3,4},{4,5},{5,6},{6,7},{7,8},{8,9},{9,10},{10,1... | collective-permute-start | bytes 276488 | tf_op jit(solution)/shard_map/ppermute | solution.py:20
  73.9 1.7 %collective-permute-done.5.refs_10_.refs_5_ = f32[3,24,320]{2,1,0:T(8,128)S(1)} collective-permute-done((f32[3,24,320]{2,1,0:T(8,128)S(1)}, f32[3,24,320]{2,1,0:T(8,128)S(1)}, u32[]{:S(2)}, u32[]{:S(2)}) %collective-permute-start.5) | collective-permute-done | bytes 92192 | tf_op jit(solution)/shard_map/ppermute | solution.py:20
  75.7 0.0 collective-permute-done.4.refs_9_.refs_4_
  75.7 2.1 %place.1 = (f32[25,32,320]{2,1,0:T(8,128)S(1)}, f32[32,320]{1,0:T(8,128)S(1)}, f32[24,320]{1,0:T(8,128)S(1)}, f32[3,32,320]{2,1,0:T(8,128)S(1)}, f32[3,24,320]{2,1,0:T(8,128)S(1)}) custom-call(s32[3]{0:T(128)S(1)} %copy-done.4, f32[8,160,128]{2,1,0:T(8,128)S(1)} %all-to-all-done.1.refs_1_, f32[4,25,32,320]{3,2,1,0:T(8,128)S(1)} %get-tuple-element.51.refs_2_, ...), custom_call_target="tpu_custom_call" | custom-call | tf_op jit(solution)/shard_map/place/pallas_call | solution.py:278
  77.7 3.5 %collective-permute-start.6 = (f32[3,32,320]{2,1,0:T(8,128)S(1)}, f32[3,32,320]{2,1,0:T(8,128)S(1)}, u32[]{:S(2)}, u32[]{:S(2)}) collective-permute-start(f32[3,32,320]{2,1,0:T(8,128)S(1)} %get-tuple-element.58), channel_id=1, source_target_pairs={{16,0},{32,16},{48,32},{64,48},{80,64},{96,80},{112,96},{17,1},{33... | collective-permute-start | bytes 368648 | tf_op jit(solution)/shard_map/ppermute | solution.py:20
  81.2 4.2 %collective-permute-start.7 = (f32[3,24,320]{2,1,0:T(8,128)S(1)}, f32[3,24,320]{2,1,0:T(8,128)S(1)}, u32[]{:S(2)}, u32[]{:S(2)}) collective-permute-start(f32[3,24,320]{2,1,0:T(8,128)S(1)} %get-tuple-element.59), channel_id=1, source_target_pairs={{1,0},{2,1},{3,2},{4,3},{5,4},{6,5},{7,6},{8,7},{9,8},{10,9},{11,1... | collective-permute-start | bytes 276488 | tf_op jit(solution)/shard_map/ppermute | solution.py:20
  85.4 4.3 %collective-permute-done.7.refs_7_ = f32[3,24,320]{2,1,0:T(8,128)S(1)} collective-permute-done((f32[3,24,320]{2,1,0:T(8,128)S(1)}, f32[3,24,320]{2,1,0:T(8,128)S(1)}, u32[]{:S(2)}, u32[]{:S(2)}) %collective-permute-start.7) | collective-permute-done | bytes 92192 | tf_op jit(solution)/shard_map/ppermute | solution.py:20
  89.7 0.0 collective-permute-done.6.refs_6_
  89.7 7.8 %second_step.1 = (f32[3,24,32,320]{3,2,1,0:T(8,128)}, f32[6,24,32,320]{3,2,1,0:T(8,128)}, f32[6,25,32,320]{3,2,1,0:T(8,128)S(1)}, f32[3,25,32,320]{3,2,1,0:T(8,128)S(1)}) custom-call(f32[6,25,32,320]{3,2,1,0:T(8,128)S(1)} %get-tuple-element.49.refs_0_, ...), custom_call_target="tpu_custom_call", output_to_operand_aliasing={{2}: (0, {}), {3}: (1, {})} | custom-call | flops 24576000 | bytes 8847360 | tf_op jit(solution)/shard_map/second_step/pallas_call | solution.py:480
  (5 shorter events, 0.0 us)
Async XLA Ops:
  0.6 1.5 %copy-start = (f32[3,384,384]{2,1,0:T(8,128)S(1)}, f32[3,384,384]{2,1,0:T(8,128)}, u32[]{:S(2)}) copy-start(f32[3,384,384]{2,1,0:T(8,128)} %planes.1) | copy-start | bytes 5308420
  2.1 0.9 copy-start.1
  3.0 0.9 copy-start.2
  7.0 28.5 %all-to-all-start = ((f32[128,16,128]{2,1,0:T(8,128)}), f32[128,16,128]{2,1,0:T(8,128)S(1)}, u32[]{:S(2)}, u32[]{:S(2)}) async-start(f32[128,16,128]{2,1,0:T(8,128)} %sections.1), calls=%async_computation | async-start | bytes 2097152 | tf_op jit(solution)/shard_map/all_to_all | solution.py:521
  17.4 18.1 %copy-start.3 = (f32[64,384]{1,0:T(8,128)S(1)}, f32[64,384]{1,0:T(8,128)}, u32[]{:S(2)}) copy-start(f32[64,384]{1,0:T(8,128)} %weight_x.1) | copy-start | bytes 294916
  17.4 18.1 %copy-start.4 = (s32[3]{0:T(128)S(1)}, s32[3]{0:T(128)}, u32[]{:S(2)}) copy-start(s32[3]{0:T(128)} %refs_0_.3) | copy-start | bytes 40
  19.0 16.4 %collective-permute-start = (f32[4,32,320]{2,1,0:T(8,128)S(1)}, f32[4,32,320]{2,1,0:T(8,128)S(1)}, u32[]{:S(2)}, u32[]{:S(2)}) collective-permute-start(f32[4,32,320]{2,1,0:T(8,128)S(1)} %get-tuple-element.33), channel_id=1, source_target_pairs={{0,16},{16,32},{32,48},{48,64},{64,80},{80,96},{96,112},{1,17},{17... | collective-permute-start | bytes 491528 | tf_op jit(solution)/shard_map/ppermute | solution.py:20
  23.6 10.6 %collective-permute-start.1 = (f32[4,24,320]{2,1,0:T(8,128)S(1)}, f32[4,24,320]{2,1,0:T(8,128)S(1)}, u32[]{:S(2)}, u32[]{:S(2)}) collective-permute-start(f32[4,24,320]{2,1,0:T(8,128)S(1)} %get-tuple-element.34), channel_id=1, source_target_pairs={{0,1},{1,2},{2,3},{3,4},{4,5},{5,6},{6,7},{7,8},{8,9},{9,10},{10,1... | collective-permute-start | bytes 368648 | tf_op jit(solution)/shard_map/ppermute | solution.py:20
  38.1 19.9 %all-to-all-start.1 = ((f32[8,160,128]{2,1,0:T(8,128)}), f32[8,160,128]{2,1,0:T(8,128)S(1)}, u32[]{:S(2)}, u32[]{:S(2)}) async-start(f32[8,160,128]{2,1,0:T(8,128)} %contract.1), calls=%async_computation.1 | async-start | bytes 1310720 | tf_op jit(solution)/shard_map/all_to_all | solution.py:531
  44.0 14.0 %collective-permute-start.2 = (f32[3,32,320]{2,1,0:T(8,128)S(1)}, f32[3,32,320]{2,1,0:T(8,128)S(1)}, u32[]{:S(2)}, u32[]{:S(2)}) collective-permute-start(f32[3,32,320]{2,1,0:T(8,128)S(1)} %get-tuple-element.45), channel_id=1, source_target_pairs={{16,0},{32,16},{48,32},{64,48},{80,64},{96,80},{112,96},{17,1},{33... | collective-permute-start | bytes 368648 | tf_op jit(solution)/shard_map/ppermute | solution.py:20
  48.6 9.5 %collective-permute-start.3 = (f32[3,24,320]{2,1,0:T(8,128)S(1)}, f32[3,24,320]{2,1,0:T(8,128)S(1)}, u32[]{:S(2)}, u32[]{:S(2)}) collective-permute-start(f32[3,24,320]{2,1,0:T(8,128)S(1)} %get-tuple-element.46), channel_id=1, source_target_pairs={{1,0},{2,1},{3,2},{4,3},{5,4},{6,5},{7,6},{8,7},{9,8},{10,9},{11,1... | collective-permute-start | bytes 276488 | tf_op jit(solution)/shard_map/ppermute | solution.py:20
  66.4 9.3 %collective-permute-start.4 = (f32[3,32,320]{2,1,0:T(8,128)S(1)}, f32[3,32,320]{2,1,0:T(8,128)S(1)}, u32[]{:S(2)}, u32[]{:S(2)}) collective-permute-start(f32[3,32,320]{2,1,0:T(8,128)S(1)} %get-tuple-element.55), channel_id=1, source_target_pairs={{0,16},{16,32},{32,48},{48,64},{64,80},{80,96},{96,112},{1,17},{17... | collective-permute-start | bytes 368648 | tf_op jit(solution)/shard_map/ppermute | solution.py:20
  70.1 5.6 %collective-permute-start.5 = (f32[3,24,320]{2,1,0:T(8,128)S(1)}, f32[3,24,320]{2,1,0:T(8,128)S(1)}, u32[]{:S(2)}, u32[]{:S(2)}) collective-permute-start(f32[3,24,320]{2,1,0:T(8,128)S(1)} %get-tuple-element.56), channel_id=1, source_target_pairs={{0,1},{1,2},{2,3},{3,4},{4,5},{5,6},{6,7},{7,8},{8,9},{9,10},{10,1... | collective-permute-start | bytes 276488 | tf_op jit(solution)/shard_map/ppermute | solution.py:20
  77.7 12.0 %collective-permute-start.6 = (f32[3,32,320]{2,1,0:T(8,128)S(1)}, f32[3,32,320]{2,1,0:T(8,128)S(1)}, u32[]{:S(2)}, u32[]{:S(2)}) collective-permute-start(f32[3,32,320]{2,1,0:T(8,128)S(1)} %get-tuple-element.58), channel_id=1, source_target_pairs={{16,0},{32,16},{48,32},{64,48},{80,64},{96,80},{112,96},{17,1},{33... | collective-permute-start | bytes 368648 | tf_op jit(solution)/shard_map/ppermute | solution.py:20
  81.2 8.5 %collective-permute-start.7 = (f32[3,24,320]{2,1,0:T(8,128)S(1)}, f32[3,24,320]{2,1,0:T(8,128)S(1)}, u32[]{:S(2)}, u32[]{:S(2)}) collective-permute-start(f32[3,24,320]{2,1,0:T(8,128)S(1)} %get-tuple-element.59), channel_id=1, source_target_pairs={{1,0},{2,1},{3,2},{4,3},{5,4},{6,5},{7,6},{8,7},{9,8},{10,9},{11,1... | collective-permute-start | bytes 276488 | tf_op jit(solution)/shard_map/ppermute | solution.py:20

commit v4 on v3

--- a/solution.py
+++ b/solution.py
@@ -160,15 +160,24 @@
     )(part_plane, part_rows, b_plane, b_rows, plane, rows)
 
 
-def sections_kernel(size_x, size_y, columns, planes, weight_y, weight_z, out, held):
+def sections_kernel(size_x, size_y, columns, planes, weight_y, weight_z, out, *refs):
+    held, planes_in, y_in, z_in, sems = refs
     own = planes.shape[0]
     box_y, box_z = weight_y.shape[0], weight_z.shape[0]
     part = box_y // (columns * size_x)
+    moves = [(weight_y, y_in), (weight_z, z_in)]
+    moves += [(planes.at[t], planes_in.at[t]) for t in range(own)]
+    copies = [pltpu.make_async_copy(*move, sems.at[k]) for k, move in enumerate(moves)]
+    for copy in copies:
+        copy.start()
     out[...] = jnp.zeros_like(out)
     held[...] = jnp.zeros_like(held)
+    copies[0].wait()
+    copies[1].wait()
     for t in range(own):
-        partly = dot(weight_y[...], planes[t])
-        held[t, strip : strip + box_y, :box_z] = dot(partly, weight_z[...], ((1,), (1,)))
+        copies[2 + t].wait()
+        partly = dot(y_in[...], planes_in[t])
+        held[t, strip : strip + box_y, :box_z] = dot(partly, z_in[...], ((1,), (1,)))
     for k in range(columns):
         for i in range(size_x):
             start = strip + (k * size_x + i) * part - 1
@@ -179,14 +188,19 @@
 
 
 def sections(planes, weight_y, weight_z, size_x, size_y, columns, height):
-    own = planes.shape[0]
+    own, box_y = planes.shape[0], weight_y.shape[0]
     return pl.pallas_call(
         functools.partial(sections_kernel, size_x, size_y, columns),
+        in_specs=[pl.BlockSpec(memory_space=pltpu.HBM)] * 3,
         out_shape=f32(size_x * size_y, height, lanes),
-        scratch_shapes=[pltpu.VMEM((own, strip + weight_y.shape[0], lanes), jnp.float32)],
+        scratch_shapes=[
+            pltpu.VMEM((own, strip + box_y, lanes), jnp.float32),
+            *[pltpu.VMEM(a.shape, jnp.float32) for a in (planes, weight_y, weight_z)],
+            pltpu.SemaphoreType.DMA((2 + own,)),
+        ],
         compiler_params=pltpu.CompilerParams(vmem_limit_bytes=16 << 20),
         name="sections",
-    )(planes, weight_y, weight_z)
+    )(*map(in_hbm, (planes, weight_y, weight_z)))
 
 
 def contract_kernel(own, part, nx, anchor, weight_x, gathered, out, padded):
@@ -228,10 +242,8 @@
     )(anchor, weight_x, gathered)
 
 
-def place_kernel(part, *refs):
-    anchor, box, cells, rate_plane, rate_rows = refs[:5]
-    part_plane, part_rows, b_plane, b_rows, plane, rows = refs[5:11]
-    out, out_plane, out_rows, first_plane, first_rows, held = refs[11:]
+def place_kernel(part, anchor, box, cells, rate_plane, rate_rows, *refs):
+    out, out_plane, out_rows, held = refs
     size_x, height, _ = box.shape
     _, ny, nz = out.shape
     nx = out.shape[0] - 1
@@ -255,48 +267,61 @@
             decay = jnp.exp(-time_step * cells[3, t + u])
             out[t + u + 1] = decay * values[u * ny : (u + 1) * ny]
     out[0] = jnp.zeros((ny, nz), jnp.float32)
-    q_plane = lost(held[nx * ny :], rate_plane[3])
-    q_rows = lost(box[0, 0:nx], rate_rows[3])
-    out_plane[...] = q_plane
-    out_rows[...] = q_rows
+    out_plane[...] = lost(held[nx * ny :], rate_plane[3])
+    out_rows[...] = lost(box[0, 0:nx], rate_rows[3])
+
+
+def place(anchor, box, cells, rate_plane, rate_rows, part):
+    nx, ny, nz = cells.shape[1] - 1, *cells.shape[2:]
+    on_chip = pl.BlockSpec(memory_space=pltpu.VMEM)
+    return pl.pallas_call(
+        functools.partial(place_kernel, part),
+        in_specs=[pl.BlockSpec(memory_space=pltpu.SMEM)] + [on_chip] * 4,
+        out_specs=(on_chip,) * 3,
+        out_shape=(pltpu.VMEM((nx + 1, ny, nz), jnp.float32), f32(ny, nz), f32(nx, nz)),
+        scratch_shapes=[pltpu.VMEM(((nx + 1) * ny, lanes), jnp.float32)],
+        compiler_params=pltpu.CompilerParams(vmem_limit_bytes=12 << 20),
+        name="place",
+    )(anchor, box, in_vmem(cells), rate_plane, rate_rows)
+
+
+def second_edges_kernel(*refs):
+    part_plane, part_rows, b_plane, b_rows, plane, rows = refs[:6]
+    source, source_plane, source_rows, first_plane, first_rows = refs[6:]
     take_halo(part_plane, part_rows, b_plane, b_rows, plane, rows, first_plane, first_rows)
+    q_plane, q_rows = source_plane[...], source_rows[...]
     factor = time_step * b_plane[...]
-    own = out[1]
+    own = source[1]
     first_plane[0] = first_plane[0] + factor * (own - q_plane)
     first_plane[1] = first_plane[1] + factor * (own - after_row(own, q_rows[0:1]))
     first_plane[2] = first_plane[2] + factor * (own - shifted_up(own))
     factor = time_step * b_rows[...]
-    own = out[1:, 0]
+    own = source[1:, 0]
     first_rows[0] = first_rows[0] + factor * (own - after_row(own, q_plane[0:1]))
     first_rows[1] = first_rows[1] + factor * (own - q_rows)
     first_rows[2] = first_rows[2] + factor * (own - shifted_up(own))
 
 
-def place(anchor, box, cells, rate_plane, rate_rows, halo, part):
-    nx, ny, nz = cells.shape[1] - 1, *cells.shape[2:]
+def second_edges(parts, plane, rows, source):
     on_chip = pl.BlockSpec(memory_space=pltpu.VMEM)
     return pl.pallas_call(
-        functools.partial(place_kernel, part),
-        in_specs=[pl.BlockSpec(memory_space=pltpu.SMEM)] + [on_chip] * (4 + len(halo)),
-        out_specs=(on_chip,) * 5,
-        out_shape=(
-            pltpu.VMEM((nx + 1, ny, nz), jnp.float32),
-            f32(ny, nz),
-            f32(nx, nz),
-            f32(3, ny, nz),
-            f32(3, nx, nz),
-        ),
-        scratch_shapes=[pltpu.VMEM(((nx + 1) * ny, lanes), jnp.float32)],
-        compiler_params=pltpu.CompilerParams(vmem_limit_bytes=12 << 20),
-        name="place",
-    )(anchor, box, in_vmem(cells), rate_plane, rate_rows, *halo)
-
-
-def step_kernel(with_source, *refs):
-    if with_source:
-        source, plane, rows, upper_plane, upper_rows, source_plane, source_rows = refs[3:10]
-        out_velocity, out_stress, stress, velocity = refs[10:14]
-        cells, out_sems = refs[2], refs[14]
+        second_edges_kernel,
+        in_specs=[on_chip] * 9,
+        out_specs=(on_chip,) * 2,
+        out_shape=(f32(*parts[0].shape), f32(*parts[1].shape)),
+        compiler_params=pltpu.CompilerParams(vmem_limit_bytes=8 << 20),
+        name="second_edges",
+    )(*parts, plane, rows, in_vmem(source[0]), *source[1:])
+
+
+def step_kernel(kind, *refs):
+    with_source = kind != "first"
+    if kind == "velocity":
+        cells, source, plane, rows, source_plane, source_rows = refs[2:8]
+        out_velocity, stress, velocity, out_sems = refs[8:]
+    elif kind == "stress":
+        cells, source, upper_plane, upper_rows = refs[2:6]
+        out_stress, stress, velocity, out_sems = refs[6:]
     else:
         fields, (plane, rows, upper_plane, upper_rows) = refs[:6], refs[6:10]
         stress, velocity, cells, last_plane, last_rows, part_plane, part_rows = refs[10:17]
@@ -316,11 +341,11 @@
 
     def leaving(k):
         here, above = pl.ds(k * per, per), pl.ds(k * per + 1, per)
-        moves = [
-            (velocity.at[:, here], out_velocity.at[:, here]),
-            (stress.at[:, above], out_stress.at[:, here]),
-        ]
-        return [pltpu.make_async_copy(*m, out_sems.at[k, n]) for n, m in enumerate(moves)]
+        if kind == "velocity":
+            move = (velocity.at[:, here], out_velocity.at[:, here])
+        else:
+            move = (stress.at[:, above], out_stress.at[:, here])
+        return [pltpu.make_async_copy(*move, out_sems.at[k])]
 
     def every(make, act):
         def one(n, _):
@@ -332,11 +357,14 @@
 
     if not with_source:
         every(arriving, lambda copy: copy.start())
-    for c, which in enumerate((0, 3, 4)):
-        stress[which, 0] = plane[c]
-        velocity[c, nx] = upper_plane[c]
-    if with_source:
-        stress[0, 0] = plane[0] + source_plane[...]
+    if kind != "stress":
+        for c, which in enumerate((0, 3, 4)):
+            stress[which, 0] = plane[c]
+        if with_source:
+            stress[0, 0] = plane[0] + source_plane[...]
+    if kind != "velocity":
+        for c in range(3):
+            velocity[c, nx] = upper_plane[c]
 
     top = lax.broadcasted_iota(jnp.int32, (strip, nz), 0) == 0
     bottom = lax.broadcasted_iota(jnp.int32, (strip, nz), 0) == strip - 1
@@ -411,8 +439,10 @@
 
         def one_plane(m, _):
             x = k * per + (per - 1 - m)
-            velocity_plane(x)
-            stress_plane(x)
+            if kind != "stress":
+                velocity_plane(x)
+            if kind != "velocity":
+                stress_plane(x)
             return 0
 
         lax.fori_loop(0, per, one_plane, 0)
@@ -458,7 +488,7 @@
     fields = [in_hbm(a) for a in (stress, velocity, *coefficients)]
     on_chip = pl.BlockSpec(memory_space=pltpu.VMEM)
     return pl.pallas_call(
-        functools.partial(step_kernel, False),
+        functools.partial(step_kernel, "first"),
         in_specs=[pl.BlockSpec(memory_space=pltpu.HBM)] * len(fields) + [on_chip] * 4,
         out_specs=(on_chip,) * 7,
         out_shape=(
@@ -472,26 +502,25 @@
     )(*fields, plane, rows, upper_plane, upper_rows)
 
 
-def second_step(stress, velocity, cells, source, edges):
-    _, nx, ny, nz = cells.shape
-    nx = nx - 1
+def second_step(kind, stress, velocity, cells, source, edges):
+    nx, ny, nz = cells.shape[1] - 1, *cells.shape[2:]
     held = [in_vmem(a) for a in (stress, velocity, cells, source)]
     on_chip = pl.BlockSpec(memory_space=pltpu.VMEM)
-    out = pl.pallas_call(
-        functools.partial(step_kernel, True),
+    parts = 3 if kind == "velocity" else 6
+    return pl.pallas_call(
+        functools.partial(step_kernel, kind),
         in_specs=[on_chip] * (len(held) + len(edges)),
-        out_specs=(pl.BlockSpec(memory_space=pltpu.HBM),) * 2 + (on_chip,) * 2,
+        out_specs=(pl.BlockSpec(memory_space=pltpu.HBM), on_chip, on_chip),
         out_shape=(
-            *[pltpu.HBM((n, nx, ny, nz), jnp.float32) for n in (3, 6)],
+            pltpu.HBM((parts, nx, ny, nz), jnp.float32),
             *[pltpu.VMEM(a.shape, jnp.float32) for a in (stress, velocity)],
         ),
-        input_output_aliases={0: 2, 1: 3},
-        scratch_shapes=[pltpu.SemaphoreType.DMA((nx // per, 2))],
+        input_output_aliases={0: 1, 1: 2},
+        scratch_shapes=[pltpu.SemaphoreType.DMA((nx // per,))],
         compiler_params=pltpu.CompilerParams(vmem_limit_bytes=20 << 20),
-        cost_estimate=estimate(nx, ny, nz, 9),
-        name="second_step",
+        cost_estimate=estimate(nx, ny, nz, parts),
+        name="second_" + kind,
     )(*held, *edges)
-    return out[0], out[1]
 
 
 def shards(
@@ -538,12 +567,17 @@
     )
     lower_x = neighbour(last_x, "gx", 1)
     lower_y = neighbour(last_y, "gy", 1)
-    halo = (*parts, lower_x, lower_y)
-    *source, first_x, first_y = place(box_anchor, box, cells, plane, rows, halo, part)
+    source = place(box_anchor, box, cells, plane, rows, part)
+    first_x, first_y = second_edges(parts, lower_x, lower_y, source)
     upper_x = neighbour(first_x, "gx", -1)
     upper_y = neighbour(first_y, "gy", -1)
-    moved = (lower_x, lower_y, upper_x, upper_y, *source[1:])
-    return second_step(strained, speed, cells, source[0], moved)
+    velocity_out, strained, speed = second_step(
+        "velocity", strained, speed, cells, source[0], (lower_x, lower_y, *source[1:])
+    )
+    stress_out, _, _ = second_step(
+        "stress", strained, speed, cells, source[0], (upper_x, upper_y)
+    )
+    return (velocity_out, stress_out)
 
 
 def solution(mesh):

time: 98.1 us -> 91.2 us (0.930)
  waiting for transfers between devices: 21.7 us -> 16.3 us
  local copies, waits for them, and re-layouts: 3.3 us -> 0.01 us
  Pallas kernels: 25.6 us -> 27 us
    ppermute x8, waiting for transfers between devices: 21.7 us -> 16.3 us  [neighbour(): return lax.ppermute(value, axis, pairs)]
    unnamed x10 -> x4, local copies, waits for them, and re-layouts: 3.3 us -> 0.01 us
    pallas_call x1, Pallas kernels: 3.04 us -> 4.71 us  [sections(): pl.pallas_call(functools.partial(sections_kernel, size_x, size_y, columns...]
    pallas_call x2 -> x4, Pallas kernels: 16.1 us -> 16 us  [the longest x1 8.09 us: first_step(): pl.pallas_call(functools.partial(step_kernel, 'first'), in_specs=[pl.Bloc...]
  transfers between devices with their start and end apart: 10 -> 10, of which waited for: 5 -> 4; matrix products, arithmetic and copies ran while one was open for 0% -> 0% of each run, Pallas kernels for 2% -> 8%
where the time goes in v4:
time: 91.2 us; the launch traced here: 90 us
  starting transfers between devices  45.8 us (50%)
  Pallas kernels  27 us (30%)
  waiting for transfers between devices  16.3 us (18%)
    ppermute x8, starting transfers between devices, neighbour(): return lax.ppermute(value, axis, pairs)  29.6 us
    ppermute x8, waiting for transfers between devices, neighbour(): return lax.ppermute(value, axis, pairs)  16.3 us
    all_to_all x1, starting transfers between devices, shards(): gathered = lax.all_to_all(pieces, ('gx', 'gy'), 0, 0, tiled=True)  10.4 us
    pallas_call x1, Pallas kernels, first_step(): pl.pallas_call(functools.partial(step_kernel, 'first'), in_specs=[pl.Bloc...  8.09 us
    pallas_call x2, Pallas kernels, second_step(): pl.pallas_call(functools.partial(step_kernel, kind), in_specs=[on_chip] *...  7.78 us
    all_to_all x1, starting transfers between devices, shards(): box = lax.all_to_all(shares, 'gx', 0, 0, tiled=True)  5.82 us
    pallas_call x1, Pallas kernels, sections(): pl.pallas_call(functools.partial(sections_kernel, size_x, size_y, columns...  4.71 us
    pallas_call x1, Pallas kernels, contract(): pl.pallas_call(functools.partial(contract_kernel, own, part, nx), in_spec...  2.69 us
  transfers between devices with their start and end apart: 10, of which 4 were waited for; matrix products, arithmetic and copies ran while one was open for 0% of the time, Pallas kernels for 8%

profile of v4, /device:TPU:57, one launch (start us, length us, event | category | flops | bytes accessed | tf_op | source)
XLA Modules:
  0.0 90.0 jit_solution(17205236908137894741)
XLA Ops:
  0.6 4.7 %sections.1 = f32[128,16,128]{2,1,0:T(8,128)} custom-call(f32[3,384,384]{2,1,0:T(8,128)} %planes.1, f32[96,384]{1,0:T(8,128)} %weight_y.1, f32[96,384]{1,0:T(8,128)} %weight_z.1), custom_call_target="tpu_custom_call" | custom-call | tf_op jit(solution)/shard_map/sections/pallas_call | solution.py:192
  5.3 10.4 %all-to-all-start = ((f32[128,16,128]{2,1,0:T(8,128)}), f32[128,16,128]{2,1,0:T(8,128)S(1)}, u32[]{:S(2)}, u32[]{:S(2)}) async-start(f32[128,16,128]{2,1,0:T(8,128)} %sections.1), calls=%async_computation | async-start | bytes 2097152 | tf_op jit(solution)/shard_map/all_to_all | solution.py:550
  15.8 0.0 copy-start
  15.8 0.0 copy-start.1
  15.8 1.6 %edges.1 = (f32[4,32,320]{2,1,0:T(8,128)S(1)}, f32[4,24,320]{2,1,0:T(8,128)S(1)}, f32[3,32,320]{2,1,0:T(8,128)S(1)}, f32[3,24,320]{2,1,0:T(8,128)S(1)}, f32[32,320]{1,0:T(8,128)S(1)}, /*index=5*/f32[24,320]{1,0:T(8,128)S(1)}) custom-call(f32[6,24,32,320]{3,2,1,0:T(8,128)} %refs_0_.1, f32[3,24,32,320]{3,2,1,0:T(8,128)} %refs_1_.1, f32[24,32,320]{2,1,0:T(8,128)} %refs_2_.1, ...), custom_call_target="tpu_custom_call" | custom-call | tf_op jit(solution)/shard_map/edges/pallas_call | solution.py:120
  17.4 4.6 %collective-permute-start = (f32[4,32,320]{2,1,0:T(8,128)S(1)}, f32[4,32,320]{2,1,0:T(8,128)S(1)}, u32[]{:S(2)}, u32[]{:S(2)}) collective-permute-start(f32[4,32,320]{2,1,0:T(8,128)S(1)} %get-tuple-element.35), channel_id=1, source_target_pairs={{0,16},{16,32},{32,48},{48,64},{64,80},{80,96},{96,112},{1,17},{17... | collective-permute-start | bytes 491528 | tf_op jit(solution)/shard_map/ppermute | solution.py:20
  22.0 2.5 %collective-permute-start.1 = (f32[4,24,320]{2,1,0:T(8,128)S(1)}, f32[4,24,320]{2,1,0:T(8,128)S(1)}, u32[]{:S(2)}, u32[]{:S(2)}) collective-permute-start(f32[4,24,320]{2,1,0:T(8,128)S(1)} %get-tuple-element.36), channel_id=1, source_target_pairs={{0,1},{1,2},{2,3},{3,4},{4,5},{5,6},{6,7},{7,8},{8,9},{9,10},{10,1... | collective-permute-start | bytes 368648 | tf_op jit(solution)/shard_map/ppermute | solution.py:20
  24.5 8.1 %collective-permute-done.1.rows.refs_7_.rate_rows = f32[4,24,320]{2,1,0:T(8,128)S(1)} collective-permute-done((f32[4,24,320]{2,1,0:T(8,128)S(1)}, f32[4,24,320]{2,1,0:T(8,128)S(1)}, u32[]{:S(2)}, u32[]{:S(2)}) %collective-permute-start.1) | collective-permute-done | bytes 122912 | tf_op jit(solution)/shard_map/ppermute | solution.py:20
  32.6 1.1 %collective-permute-done.plane.refs_6_.rate_plane = f32[4,32,320]{2,1,0:T(8,128)S(1)} collective-permute-done((f32[4,32,320]{2,1,0:T(8,128)S(1)}, f32[4,32,320]{2,1,0:T(8,128)S(1)}, u32[]{:S(2)}, u32[]{:S(2)}) %collective-permute-start) | collective-permute-done | bytes 163872 | tf_op jit(solution)/shard_map/ppermute | solution.py:20
  33.8 0.0 all-to-all-done
  33.8 0.0 copy-done
  33.8 0.0 copy-done.1
  33.8 2.7 %contract.1 = f32[8,160,128]{2,1,0:T(8,128)} custom-call(s32[3]{0:T(128)S(1)} %copy-done.1, f32[64,384]{1,0:T(8,128)S(1)} %copy-done, f32[2048,128]{1,0:T(8,128)S(1)} %bitcast.1), custom_call_target="tpu_custom_call" | custom-call | tf_op jit(solution)/shard_map/contract/pallas_call | solution.py:231
  36.5 5.8 %all-to-all-start.1 = ((f32[8,160,128]{2,1,0:T(8,128)}), f32[8,160,128]{2,1,0:T(8,128)S(1)}, u32[]{:S(2)}, u32[]{:S(2)}) async-start(f32[8,160,128]{2,1,0:T(8,128)} %contract.1), calls=%async_computation.1 | async-start | bytes 1310720 | tf_op jit(solution)/shard_map/all_to_all | solution.py:560
  42.3 4.6 %collective-permute-start.2 = (f32[3,32,320]{2,1,0:T(8,128)S(1)}, f32[3,32,320]{2,1,0:T(8,128)S(1)}, u32[]{:S(2)}, u32[]{:S(2)}) collective-permute-start(f32[3,32,320]{2,1,0:T(8,128)S(1)} %get-tuple-element.47), channel_id=1, source_target_pairs={{16,0},{32,16},{48,32},{64,48},{80,64},{96,80},{112,96},{17,1},{33... | collective-permute-start | bytes 368648 | tf_op jit(solution)/shard_map/ppermute | solution.py:20
  46.9 3.0 %collective-permute-start.3 = (f32[3,24,320]{2,1,0:T(8,128)S(1)}, f32[3,24,320]{2,1,0:T(8,128)S(1)}, u32[]{:S(2)}, u32[]{:S(2)}) collective-permute-start(f32[3,24,320]{2,1,0:T(8,128)S(1)} %get-tuple-element.48), channel_id=1, source_target_pairs={{1,0},{2,1},{3,2},{4,3},{5,4},{6,5},{7,6},{8,7},{9,8},{10,9},{11,1... | collective-permute-start | bytes 276488 | tf_op jit(solution)/shard_map/ppermute | solution.py:20
  50.0 6.4 %collective-permute-done.3.refs_9_ = f32[3,24,320]{2,1,0:T(8,128)S(1)} collective-permute-done((f32[3,24,320]{2,1,0:T(8,128)S(1)}, f32[3,24,320]{2,1,0:T(8,128)S(1)}, u32[]{:S(2)}, u32[]{:S(2)}) %collective-permute-start.3) | collective-permute-done | bytes 92192 | tf_op jit(solution)/shard_map/ppermute | solution.py:20
  56.4 0.0 collective-permute-done.2.refs_8_
  56.4 0.0 all-to-all-done.1.box
  56.4 8.1 %first_step.1 = (f32[6,25,32,320]{3,2,1,0:T(8,128)S(1)}, f32[3,25,32,320]{3,2,1,0:T(8,128)S(1)}, f32[4,25,32,320]{3,2,1,0:T(8,128)S(1)}, f32[3,32,320]{2,1,0:T(8...) custom-call(f32[6,24,32,320]{3,2,1,0:T(8,128)} %refs_0_.1, ...), custom_call_target="tpu_custom_call" | custom-call | flops 24576000 | bytes 12779520 | tf_op jit(solution)/shard_map/first_step/pallas_call | solution.py:490
  64.5 3.7 %collective-permute-start.4 = (f32[3,32,320]{2,1,0:T(8,128)S(1)}, f32[3,32,320]{2,1,0:T(8,128)S(1)}, u32[]{:S(2)}, u32[]{:S(2)}) collective-permute-start(f32[3,32,320]{2,1,0:T(8,128)S(1)} %get-tuple-element.56), channel_id=1, source_target_pairs={{0,16},{16,32},{32,48},{48,64},{64,80},{80,96},{96,112},{1,17},{17... | collective-permute-start | bytes 368648 | tf_op jit(solution)/shard_map/ppermute | solution.py:20
  68.2 3.8 %collective-permute-start.5 = (f32[3,24,320]{2,1,0:T(8,128)S(1)}, f32[3,24,320]{2,1,0:T(8,128)S(1)}, u32[]{:S(2)}, u32[]{:S(2)}) collective-permute-start(f32[3,24,320]{2,1,0:T(8,128)S(1)} %get-tuple-element.57), channel_id=1, source_target_pairs={{0,1},{1,2},{2,3},{3,4},{4,5},{5,6},{6,7},{7,8},{8,9},{9,10},{10,1... | collective-permute-start | bytes 276488 | tf_op jit(solution)/shard_map/ppermute | solution.py:20
  72.0 2.0 %place.1 = (f32[25,32,320]{2,1,0:T(8,128)S(1)}, f32[32,320]{1,0:T(8,128)S(1)}, f32[24,320]{1,0:T(8,128)S(1)}) custom-call(s32[3]{0:T(128)S(1)} %copy-done.1, f32[8,160,128]{2,1,0:T(8,128)S(1)} %all-to-all-done.1.box, f32[4,25,32,320]{3,2,1,0:T(8,128)S(1)} %get-tuple-element.53.cells.refs_2_, f32[4,32,320]{2,1,0:T(8,128)S(1)} %collective-permute-done.plane.refs_6_.rate_plane, ...), custom_call_target="tpu_custom_call" | custom-call | tf_op jit(solution)/shard_map/place/pallas_call | solution.py:277
  74.0 0.0 collective-permute-done.5.refs_5_
  74.1 0.0 collective-permute-done.4.refs_4_
  74.1 0.1 second_edges.1
  74.2 3.5 %collective-permute-start.6 = (f32[3,32,320]{2,1,0:T(8,128)S(1)}, f32[3,32,320]{2,1,0:T(8,128)S(1)}, u32[]{:S(2)}, u32[]{:S(2)}) collective-permute-start(f32[3,32,320]{2,1,0:T(8,128)S(1)} %get-tuple-element.65), channel_id=1, source_target_pairs={{16,0},{32,16},{48,32},{64,48},{80,64},{96,80},{112,96},{17,1},{33... | collective-permute-start | bytes 368648 | tf_op jit(solution)/shard_map/ppermute | solution.py:20
  77.6 3.9 %collective-permute-start.7 = (f32[3,24,320]{2,1,0:T(8,128)S(1)}, f32[3,24,320]{2,1,0:T(8,128)S(1)}, u32[]{:S(2)}, u32[]{:S(2)}) collective-permute-start(f32[3,24,320]{2,1,0:T(8,128)S(1)} %get-tuple-element.66), channel_id=1, source_target_pairs={{1,0},{2,1},{3,2},{4,3},{5,4},{6,5},{7,6},{8,7},{9,8},{10,9},{11,1... | collective-permute-start | bytes 276488 | tf_op jit(solution)/shard_map/ppermute | solution.py:20
  81.5 3.6 %second_velocity.1 = (f32[3,24,32,320]{3,2,1,0:T(8,128)}, f32[6,25,32,320]{3,2,1,0:T(8,128)S(1)}, f32[3,25,32,320]{3,2,1,0:T(8,128)S(1)}) custom-call(f32[6,25,32,320]{3,2,1,0:T(8,128)S(1)} %get-tuple-element.51.refs_0_, f32[3,25,32,320]{3,2,1,0:T(8,128)S(1)} %get-tuple-element.52.refs_1_, ...), custom_call_target="tpu_custom_call", output_to_operand_aliasing={{1}: (0, {}), {2}: (1, {})} | custom-call | flops 24576000 | bytes 2949120 | tf_op jit(solution)/shard_map/second_velocity/pallas_call | solution.py:510
  85.2 0.7 collective-permute-done.7.refs_5_
  85.9 0.0 collective-permute-done.6.refs_4_
  85.9 4.1 %second_stress.1 = (f32[6,24,32,320]{3,2,1,0:T(8,128)}, f32[6,25,32,320]{3,2,1,0:T(8,128)S(1)}, f32[3,25,32,320]{3,2,1,0:T(8,128)S(1)}) custom-call(f32[6,25,32,320]{3,2,1,0:T(8,128)S(1)} %get-tuple-element.61.refs_0_, f32[3,25,32,320]{3,2,1,0:T(8,128)S(1)} %get-tuple-element.62.refs_1_, ...), custom_call_target="tpu_custom_call", output_to_operand_aliasing={{1}: (0, {}), {2}: (1, {})} | custom-call | flops 24576000 | bytes 5898240 | tf_op jit(solution)/shard_map/second_stress/pallas_call | solution.py:510
  (1 shorter events, 0.0 us)
Async XLA Ops:
  5.3 28.5 %all-to-all-start = ((f32[128,16,128]{2,1,0:T(8,128)}), f32[128,16,128]{2,1,0:T(8,128)S(1)}, u32[]{:S(2)}, u32[]{:S(2)}) async-start(f32[128,16,128]{2,1,0:T(8,128)} %sections.1), calls=%async_computation | async-start | bytes 2097152 | tf_op jit(solution)/shard_map/all_to_all | solution.py:550
  15.8 18.1 %copy-start = (f32[64,384]{1,0:T(8,128)S(1)}, f32[64,384]{1,0:T(8,128)}, u32[]{:S(2)}) copy-start(f32[64,384]{1,0:T(8,128)} %weight_x.1) | copy-start | bytes 294916
  15.8 18.1 %copy-start.1 = (s32[3]{0:T(128)S(1)}, s32[3]{0:T(128)}, u32[]{:S(2)}) copy-start(s32[3]{0:T(128)} %anchor.3) | copy-start | bytes 40
  17.4 16.4 %collective-permute-start = (f32[4,32,320]{2,1,0:T(8,128)S(1)}, f32[4,32,320]{2,1,0:T(8,128)S(1)}, u32[]{:S(2)}, u32[]{:S(2)}) collective-permute-start(f32[4,32,320]{2,1,0:T(8,128)S(1)} %get-tuple-element.35), channel_id=1, source_target_pairs={{0,16},{16,32},{32,48},{48,64},{64,80},{80,96},{96,112},{1,17},{17... | collective-permute-start | bytes 491528 | tf_op jit(solution)/shard_map/ppermute | solution.py:20
  22.0 10.6 %collective-permute-start.1 = (f32[4,24,320]{2,1,0:T(8,128)S(1)}, f32[4,24,320]{2,1,0:T(8,128)S(1)}, u32[]{:S(2)}, u32[]{:S(2)}) collective-permute-start(f32[4,24,320]{2,1,0:T(8,128)S(1)} %get-tuple-element.36), channel_id=1, source_target_pairs={{0,1},{1,2},{2,3},{3,4},{4,5},{5,6},{6,7},{7,8},{8,9},{9,10},{10,1... | collective-permute-start | bytes 368648 | tf_op jit(solution)/shard_map/ppermute | solution.py:20
  36.5 19.9 %all-to-all-start.1 = ((f32[8,160,128]{2,1,0:T(8,128)}), f32[8,160,128]{2,1,0:T(8,128)S(1)}, u32[]{:S(2)}, u32[]{:S(2)}) async-start(f32[8,160,128]{2,1,0:T(8,128)} %contract.1), calls=%async_computation.1 | async-start | bytes 1310720 | tf_op jit(solution)/shard_map/all_to_all | solution.py:560
  42.3 14.0 %collective-permute-start.2 = (f32[3,32,320]{2,1,0:T(8,128)S(1)}, f32[3,32,320]{2,1,0:T(8,128)S(1)}, u32[]{:S(2)}, u32[]{:S(2)}) collective-permute-start(f32[3,32,320]{2,1,0:T(8,128)S(1)} %get-tuple-element.47), channel_id=1, source_target_pairs={{16,0},{32,16},{48,32},{64,48},{80,64},{96,80},{112,96},{17,1},{33... | collective-permute-start | bytes 368648 | tf_op jit(solution)/shard_map/ppermute | solution.py:20
  46.9 9.5 %collective-permute-start.3 = (f32[3,24,320]{2,1,0:T(8,128)S(1)}, f32[3,24,320]{2,1,0:T(8,128)S(1)}, u32[]{:S(2)}, u32[]{:S(2)}) collective-permute-start(f32[3,24,320]{2,1,0:T(8,128)S(1)} %get-tuple-element.48), channel_id=1, source_target_pairs={{1,0},{2,1},{3,2},{4,3},{5,4},{6,5},{7,6},{8,7},{9,8},{10,9},{11,1... | collective-permute-start | bytes 276488 | tf_op jit(solution)/shard_map/ppermute | solution.py:20
  64.5 9.6 %collective-permute-start.4 = (f32[3,32,320]{2,1,0:T(8,128)S(1)}, f32[3,32,320]{2,1,0:T(8,128)S(1)}, u32[]{:S(2)}, u32[]{:S(2)}) collective-permute-start(f32[3,32,320]{2,1,0:T(8,128)S(1)} %get-tuple-element.56), channel_id=1, source_target_pairs={{0,16},{16,32},{32,48},{48,64},{64,80},{80,96},{96,112},{1,17},{17... | collective-permute-start | bytes 368648 | tf_op jit(solution)/shard_map/ppermute | solution.py:20
  68.2 5.9 %collective-permute-start.5 = (f32[3,24,320]{2,1,0:T(8,128)S(1)}, f32[3,24,320]{2,1,0:T(8,128)S(1)}, u32[]{:S(2)}, u32[]{:S(2)}) collective-permute-start(f32[3,24,320]{2,1,0:T(8,128)S(1)} %get-tuple-element.57), channel_id=1, source_target_pairs={{0,1},{1,2},{2,3},{3,4},{4,5},{5,6},{6,7},{7,8},{8,9},{9,10},{10,1... | collective-permute-start | bytes 276488 | tf_op jit(solution)/shard_map/ppermute | solution.py:20
  74.2 11.7 %collective-permute-start.6 = (f32[3,32,320]{2,1,0:T(8,128)S(1)}, f32[3,32,320]{2,1,0:T(8,128)S(1)}, u32[]{:S(2)}, u32[]{:S(2)}) collective-permute-start(f32[3,32,320]{2,1,0:T(8,128)S(1)} %get-tuple-element.65), channel_id=1, source_target_pairs={{16,0},{32,16},{48,32},{64,48},{80,64},{96,80},{112,96},{17,1},{33... | collective-permute-start | bytes 368648 | tf_op jit(solution)/shard_map/ppermute | solution.py:20
  77.6 8.2 %collective-permute-start.7 = (f32[3,24,320]{2,1,0:T(8,128)S(1)}, f32[3,24,320]{2,1,0:T(8,128)S(1)}, u32[]{:S(2)}, u32[]{:S(2)}) collective-permute-start(f32[3,24,320]{2,1,0:T(8,128)S(1)} %get-tuple-element.66), channel_id=1, source_target_pairs={{1,0},{2,1},{3,2},{4,3},{5,4},{6,5},{7,6},{8,7},{9,8},{10,9},{11,1... | collective-permute-start | bytes 276488 | tf_op jit(solution)/shard_map/ppermute | solution.py:20

commit v5 on v4

--- a/solution.py
+++ b/solution.py
@@ -8,7 +8,6 @@
 from jax.sharding import PartitionSpec as P
 
 time_step = 0.2
-precise = lax.Precision.HIGHEST
 strip = 8
 lanes = 128
 per = 3
@@ -32,9 +31,23 @@
     return jax.ShapeDtypeStruct(shape, jnp.float32)
 
 
+def split(values, parts=2):
+    out = []
+    for _ in range(parts):
+        out.append(values.astype(jnp.bfloat16))
+        values = values - out[-1].astype(jnp.float32)
+    return out
+
+
 def dot(a, b, contract=((1,), (0,))):
-    return lax.dot_general(
-        a, b, (contract, ((), ())), precision=precise, preferred_element_type=jnp.float32
+    return sum(
+        lax.dot_general(
+            a[i], b[j], (contract, ((), ())), preferred_element_type=jnp.float32
+        )
+        for i, j in sorted(
+            ((i, j) for i in range(len(a)) for j in range(len(b))), key=lambda ij: -sum(ij)
+        )
+        if i + j < max(len(a), len(b))
     )
 
 
@@ -174,10 +187,11 @@
     held[...] = jnp.zeros_like(held)
     copies[0].wait()
     copies[1].wait()
+    in_y, in_z = split(y_in[...]), split(z_in[...])
     for t in range(own):
         copies[2 + t].wait()
-        partly = dot(y_in[...], planes_in[t])
-        held[t, strip : strip + box_y, :box_z] = dot(partly, z_in[...], ((1,), (1,)))
+        partly = split(dot(in_y, split(planes_in[t])))
+        held[t, strip : strip + box_y, :box_z] = dot(partly, in_z, ((1,), (1,)))
     for k in range(columns):
         for i in range(size_x):
             start = strip + (k * size_x + i) * part - 1
@@ -205,29 +219,33 @@
 
 def contract_kernel(own, part, nx, anchor, weight_x, gathered, out, padded):
     box_x, count = weight_x.shape
-    size_x, height, _ = out.shape
-    rows = height // (part + 1)
+    size_x = out.shape[0]
+    span = nx + 1
     devices = count // own
     stride = gathered.shape[0] // devices
     section = lax.broadcasted_iota(jnp.int32, (count, count), 0)
     column = lax.broadcasted_iota(jnp.int32, (count, count), 1)
     pick = section == own * lax.rem(column, devices) + lax.div(column, devices)
-    weights = dot(weight_x[...], pick.astype(jnp.float32))
+    pick = pick.astype(jnp.bfloat16)
+    weights = [dot([w], [pick]).astype(jnp.bfloat16) for w in split(weight_x[...])]
     padded[...] = jnp.zeros_like(padded)
     for r in range(part + 1):
         terms = [
             gathered[pl.ds(t * (part + 1) + r, devices, stride=stride), :] for t in range(own)
         ]
-        box = dot(weights, jnp.concatenate(terms, 0))
+        box = dot(weights, split(jnp.concatenate(terms, 0)))
         padded[r, pl.ds(anchor[0] + strip, box_x), :] = box
     for i in range(size_x):
         start = strip + i * nx
         for r in range(part + 1):
-            out[i, r * rows : r * rows + nx] = padded[r, start : start + nx]
-            out[i, r * rows + nx : (r + 1) * rows] = padded[r, start - 1 : start - 1 + rows - nx]
-
-
-def contract(anchor, weight_x, gathered, own, part, nx, size_x, rows):
+            out[i, r * span : r * span + nx] = padded[r, start : start + nx]
+            out[i, r * span + nx : (r + 1) * span] = padded[r, start - 1 : start]
+        left = out.shape[1] - (part + 1) * span
+        out[i, (part + 1) * span :] = jnp.zeros((left, lanes), jnp.float32)
+
+
+def contract(anchor, weight_x, gathered, own, part, nx, size_x):
+    height = -(-(part + 1) * (nx + 1) // strip) * strip
     return pl.pallas_call(
         functools.partial(contract_kernel, own, part, nx),
         in_specs=[
@@ -235,7 +253,7 @@
             pl.BlockSpec(memory_space=pltpu.VMEM),
             pl.BlockSpec(memory_space=pltpu.VMEM),
         ],
-        out_shape=f32(size_x, (part + 1) * rows, lanes),
+        out_shape=f32(size_x, height, lanes),
         scratch_shapes=[pltpu.VMEM((part + 1, 2 * strip + size_x * nx, lanes), jnp.float32)],
         compiler_params=pltpu.CompilerParams(vmem_limit_bytes=16 << 20),
         name="contract",
@@ -244,10 +262,10 @@
 
 def place_kernel(part, anchor, box, cells, rate_plane, rate_rows, *refs):
     out, out_plane, out_rows, held = refs
-    size_x, height, _ = box.shape
+    size_x = box.shape[0]
     _, ny, nz = out.shape
     nx = out.shape[0] - 1
-    span = height // (part + 1)
+    span = nx + 1
     for i in range(size_x):
         for r in range(part):
             y = i * part + r
@@ -256,13 +274,16 @@
             held[nx * ny + y : nx * ny + y + 1] = box[i, first + nx : first + nx + 1]
     cell = lax.broadcasted_iota(jnp.int32, (lanes, nz), 1)
     which = lax.broadcasted_iota(jnp.int32, (lanes, nz), 0)
-    pick = (cell - anchor[2] == which).astype(jnp.float32)
+    pick = (cell - anchor[2] == which).astype(jnp.bfloat16)
+
+    def placed(values):
+        return (-time_step) * dot(split(values, 3), [pick])
 
     def lost(values, rates):
-        return (-time_step) * jnp.exp(-time_step * rates) * dot(values, pick)
+        return jnp.exp(-time_step * rates) * placed(values)
 
     for t in range(0, nx, 4):
-        values = (-time_step) * dot(held[t * ny : (t + 4) * ny], pick)
+        values = placed(held[t * ny : (t + 4) * ny])
         for u in range(4):
             decay = jnp.exp(-time_step * cells[3, t + u])
             out[t + u + 1] = decay * values[u * ny : (u + 1) * ny]
@@ -445,7 +466,7 @@
                 stress_plane(x)
             return 0
 
-        lax.fori_loop(0, per, one_plane, 0)
+        lax.fori_loop(0, per, one_plane, 0, unroll=True)
         if with_source:
             for copy in leaving(k):
                 copy.start()
@@ -555,7 +576,7 @@
 
     gathered, first_x, first_y = lax.optimization_barrier((gathered, first_x, first_y))
     gathered = gathered.reshape(size_x * size_y * height, lanes)
-    shares = contract(box_anchor, weight_x, gathered, own, part, nx, size_x, nx + strip)
+    shares = contract(box_anchor, weight_x, gathered, own, part, nx, size_x)
     shares, first_x, first_y = lax.optimization_barrier((shares, first_x, first_y))
     box = lax.all_to_all(shares, "gx", 0, 0, tiled=True)
     upper_x = neighbour(first_x, "gx", -1)

time: 91.2 us -> 87.3 us (0.957)
  Pallas kernels: 27 us -> 22.7 us
  waiting for transfers between devices: 16.3 us -> 19.5 us
  starting transfers between devices: 45.8 us -> 43.8 us
    ppermute x8, waiting for transfers between devices: 16.3 us -> 19.5 us  [neighbour(): return lax.ppermute(value, axis, pairs)]
    ppermute x8, starting transfers between devices: 29.6 us -> 27.5 us  [neighbour(): return lax.ppermute(value, axis, pairs)]
    pallas_call x2, Pallas kernels: 7.78 us -> 6.18 us  [second_step(): pl.pallas_call(functools.partial(step_kernel, kind), in_specs=[on_chip] *...]
  transfers between devices with their start and end apart: 10 -> 10, of which waited for: 4 -> 6; matrix products, arithmetic and copies ran while one was open for 0% -> 0% of each run, Pallas kernels for 8% -> 7%
where the time goes in v5:
time: 87.3 us; the launch traced here: 86.7 us
  starting transfers between devices  43.8 us (50%)
  Pallas kernels  22.7 us (26%)
  waiting for transfers between devices  19.5 us (22%)
    ppermute x8, starting transfers between devices, neighbour(): return lax.ppermute(value, axis, pairs)  27.5 us
    ppermute x8, waiting for transfers between devices, neighbour(): return lax.ppermute(value, axis, pairs)  19.5 us
    all_to_all x1, starting transfers between devices, shards(): gathered = lax.all_to_all(pieces, ('gx', 'gy'), 0, 0, tiled=True)  10.4 us
    pallas_call x1, Pallas kernels, first_step(): pl.pallas_call(functools.partial(step_kernel, 'first'), in_specs=[pl.Bloc...  7.25 us
    pallas_call x2, Pallas kernels, second_step(): pl.pallas_call(functools.partial(step_kernel, kind), in_specs=[on_chip] *...  6.18 us
    all_to_all x1, starting transfers between devices, shards(): box = lax.all_to_all(shares, 'gx', 0, 0, tiled=True)  5.83 us
    pallas_call x1, Pallas kernels, sections(): pl.pallas_call(functools.partial(sections_kernel, size_x, size_y, columns...  3.93 us
    pallas_call x1, Pallas kernels, contract(): pl.pallas_call(functools.partial(contract_kernel, own, part, nx), in_spec...  2.12 us
  transfers between devices with their start and end apart: 10, of which 6 were waited for; matrix products, arithmetic and copies ran while one was open for 0% of the time, Pallas kernels for 7%

profile of v5, /device:TPU:57, one launch (start us, length us, event | category | flops | bytes accessed | tf_op | source)
XLA Modules:
  0.0 86.7 jit_solution(2473103548436023736)
XLA Ops:
  0.6 3.9 %sections.1 = f32[128,16,128]{2,1,0:T(8,128)} custom-call(f32[3,384,384]{2,1,0:T(8,128)} %planes.1, f32[96,384]{1,0:T(8,128)} %weight_y.1, f32[96,384]{1,0:T(8,128)} %weight_z.1), custom_call_target="tpu_custom_call" | custom-call | tf_op jit(solution)/shard_map/sections/pallas_call | solution.py:206
  4.6 10.4 %all-to-all-start = ((f32[128,16,128]{2,1,0:T(8,128)}), f32[128,16,128]{2,1,0:T(8,128)S(1)}, u32[]{:S(2)}, u32[]{:S(2)}) async-start(f32[128,16,128]{2,1,0:T(8,128)} %sections.1), calls=%async_computation | async-start | bytes 2097152 | tf_op jit(solution)/shard_map/all_to_all | solution.py:571
  15.0 0.0 copy-start
  15.0 0.0 copy-start.1
  15.0 1.6 %edges.1 = (f32[4,32,320]{2,1,0:T(8,128)S(1)}, f32[4,24,320]{2,1,0:T(8,128)S(1)}, f32[3,32,320]{2,1,0:T(8,128)S(1)}, f32[3,24,320]{2,1,0:T(8,128)S(1)}, f32[32,320]{1,0:T(8,128)S(1)}, /*index=5*/f32[24,320]{1,0:T(8,128)S(1)}) custom-call(f32[6,24,32,320]{3,2,1,0:T(8,128)} %refs_0_.1, f32[3,24,32,320]{3,2,1,0:T(8,128)} %refs_1_.1, f32[24,32,320]{2,1,0:T(8,128)} %refs_2_.1, ...), custom_call_target="tpu_custom_call" | custom-call | tf_op jit(solution)/shard_map/edges/pallas_call | solution.py:133
  16.6 4.6 %collective-permute-start = (f32[4,32,320]{2,1,0:T(8,128)S(1)}, f32[4,32,320]{2,1,0:T(8,128)S(1)}, u32[]{:S(2)}, u32[]{:S(2)}) collective-permute-start(f32[4,32,320]{2,1,0:T(8,128)S(1)} %get-tuple-element.35), channel_id=1, source_target_pairs={{0,16},{16,32},{32,48},{48,64},{64,80},{80,96},{96,112},{1,17},{17... | collective-permute-start | bytes 491528 | tf_op jit(solution)/shard_map/ppermute | solution.py:19
  21.2 2.5 %collective-permute-start.1 = (f32[4,24,320]{2,1,0:T(8,128)S(1)}, f32[4,24,320]{2,1,0:T(8,128)S(1)}, u32[]{:S(2)}, u32[]{:S(2)}) collective-permute-start(f32[4,24,320]{2,1,0:T(8,128)S(1)} %get-tuple-element.36), channel_id=1, source_target_pairs={{0,1},{1,2},{2,3},{3,4},{4,5},{5,6},{6,7},{7,8},{8,9},{9,10},{10,1... | collective-permute-start | bytes 368648 | tf_op jit(solution)/shard_map/ppermute | solution.py:19
  23.8 8.1 %collective-permute-done.1.rows.refs_7_.rate_rows = f32[4,24,320]{2,1,0:T(8,128)S(1)} collective-permute-done((f32[4,24,320]{2,1,0:T(8,128)S(1)}, f32[4,24,320]{2,1,0:T(8,128)S(1)}, u32[]{:S(2)}, u32[]{:S(2)}) %collective-permute-start.1) | collective-permute-done | bytes 122912 | tf_op jit(solution)/shard_map/ppermute | solution.py:19
  31.9 1.1 %collective-permute-done.plane.refs_6_.rate_plane = f32[4,32,320]{2,1,0:T(8,128)S(1)} collective-permute-done((f32[4,32,320]{2,1,0:T(8,128)S(1)}, f32[4,32,320]{2,1,0:T(8,128)S(1)}, u32[]{:S(2)}, u32[]{:S(2)}) %collective-permute-start) | collective-permute-done | bytes 163872 | tf_op jit(solution)/shard_map/ppermute | solution.py:19
  33.0 0.0 all-to-all-done
  33.0 0.0 copy-done
  33.0 0.0 copy-done.1
  33.1 2.1 %contract.1 = f32[8,128,128]{2,1,0:T(8,128)} custom-call(s32[3]{0:T(128)S(1)} %copy-done.1, f32[64,384]{1,0:T(8,128)S(1)} %copy-done, f32[2048,128]{1,0:T(8,128)S(1)} %bitcast.1), custom_call_target="tpu_custom_call" | custom-call | tf_op jit(solution)/shard_map/contract/pallas_call | solution.py:249
  35.2 5.8 %all-to-all-start.1 = ((f32[8,128,128]{2,1,0:T(8,128)}), f32[8,128,128]{2,1,0:T(8,128)S(1)}, u32[]{:S(2)}, u32[]{:S(2)}) async-start(f32[8,128,128]{2,1,0:T(8,128)} %contract.1), calls=%async_computation.1 | async-start | bytes 1048576 | tf_op jit(solution)/shard_map/all_to_all | solution.py:581
  41.0 4.6 %collective-permute-start.2 = (f32[3,32,320]{2,1,0:T(8,128)S(1)}, f32[3,32,320]{2,1,0:T(8,128)S(1)}, u32[]{:S(2)}, u32[]{:S(2)}) collective-permute-start(f32[3,32,320]{2,1,0:T(8,128)S(1)} %get-tuple-element.47), channel_id=1, source_target_pairs={{16,0},{32,16},{48,32},{64,48},{80,64},{96,80},{112,96},{17,1},{33... | collective-permute-start | bytes 368648 | tf_op jit(solution)/shard_map/ppermute | solution.py:19
  45.6 3.0 %collective-permute-start.3 = (f32[3,24,320]{2,1,0:T(8,128)S(1)}, f32[3,24,320]{2,1,0:T(8,128)S(1)}, u32[]{:S(2)}, u32[]{:S(2)}) collective-permute-start(f32[3,24,320]{2,1,0:T(8,128)S(1)} %get-tuple-element.48), channel_id=1, source_target_pairs={{1,0},{2,1},{3,2},{4,3},{5,4},{6,5},{7,6},{8,7},{9,8},{10,9},{11,1... | collective-permute-start | bytes 276488 | tf_op jit(solution)/shard_map/ppermute | solution.py:19
  48.7 6.1 %collective-permute-done.3.refs_9_ = f32[3,24,320]{2,1,0:T(8,128)S(1)} collective-permute-done((f32[3,24,320]{2,1,0:T(8,128)S(1)}, f32[3,24,320]{2,1,0:T(8,128)S(1)}, u32[]{:S(2)}, u32[]{:S(2)}) %collective-permute-start.3) | collective-permute-done | bytes 92192 | tf_op jit(solution)/shard_map/ppermute | solution.py:19
  54.8 0.0 collective-permute-done.2.refs_8_
  54.8 0.0 all-to-all-done.1.box
  54.8 7.3 %first_step.1 = (f32[6,25,32,320]{3,2,1,0:T(8,128)S(1)}, f32[3,25,32,320]{3,2,1,0:T(8,128)S(1)}, f32[4,25,32,320]{3,2,1,0:T(8,128)S(1)}, f32[3,32,320]{2,1,0:T(8...) custom-call(f32[6,24,32,320]{3,2,1,0:T(8,128)} %refs_0_.1, ...), custom_call_target="tpu_custom_call" | custom-call | flops 24576000 | bytes 12779520 | tf_op jit(solution)/shard_map/first_step/pallas_call | solution.py:511
  62.0 3.0 %collective-permute-start.4 = (f32[3,32,320]{2,1,0:T(8,128)S(1)}, f32[3,32,320]{2,1,0:T(8,128)S(1)}, u32[]{:S(2)}, u32[]{:S(2)}) collective-permute-start(f32[3,32,320]{2,1,0:T(8,128)S(1)} %get-tuple-element.56), channel_id=1, source_target_pairs={{0,16},{16,32},{32,48},{48,64},{64,80},{80,96},{96,112},{1,17},{17... | collective-permute-start | bytes 368648 | tf_op jit(solution)/shard_map/ppermute | solution.py:19
  65.1 4.1 %collective-permute-start.5 = (f32[3,24,320]{2,1,0:T(8,128)S(1)}, f32[3,24,320]{2,1,0:T(8,128)S(1)}, u32[]{:S(2)}, u32[]{:S(2)}) collective-permute-start(f32[3,24,320]{2,1,0:T(8,128)S(1)} %get-tuple-element.57), channel_id=1, source_target_pairs={{0,1},{1,2},{2,3},{3,4},{4,5},{5,6},{6,7},{7,8},{8,9},{9,10},{10,1... | collective-permute-start | bytes 276488 | tf_op jit(solution)/shard_map/ppermute | solution.py:19
  69.1 1.4 %place.1 = (f32[25,32,320]{2,1,0:T(8,128)S(1)}, f32[32,320]{1,0:T(8,128)S(1)}, f32[24,320]{1,0:T(8,128)S(1)}) custom-call(s32[3]{0:T(128)S(1)} %copy-done.1, f32[8,128,128]{2,1,0:T(8,128)S(1)} %all-to-all-done.1.box, f32[4,25,32,320]{3,2,1,0:T(8,128)S(1)} %get-tuple-element.53.cells.refs_2_, f32[4,32,320]{2,1,0:T(8,128)S(1)} %collective-permute-done.plane.refs_6_.rate_plane, ...), custom_call_target="tpu_custom_call" | custom-call | tf_op jit(solution)/shard_map/place/pallas_call | solution.py:298
  70.6 0.3 collective-permute-done.5.refs_5_
  70.9 1.3 %collective-permute-done.4.refs_4_ = f32[3,32,320]{2,1,0:T(8,128)S(1)} collective-permute-done((f32[3,32,320]{2,1,0:T(8,128)S(1)}, f32[3,32,320]{2,1,0:T(8,128)S(1)}, u32[]{:S(2)}, u32[]{:S(2)}) %collective-permute-start.4) | collective-permute-done | bytes 122912 | tf_op jit(solution)/shard_map/ppermute | solution.py:19
  72.2 0.1 second_edges.1
  72.3 2.4 %collective-permute-start.6 = (f32[3,32,320]{2,1,0:T(8,128)S(1)}, f32[3,32,320]{2,1,0:T(8,128)S(1)}, u32[]{:S(2)}, u32[]{:S(2)}) collective-permute-start(f32[3,32,320]{2,1,0:T(8,128)S(1)} %get-tuple-element.65), channel_id=1, source_target_pairs={{16,0},{32,16},{48,32},{64,48},{80,64},{96,80},{112,96},{17,1},{33... | collective-permute-start | bytes 368648 | tf_op jit(solution)/shard_map/ppermute | solution.py:19
  74.7 3.3 %collective-permute-start.7 = (f32[3,24,320]{2,1,0:T(8,128)S(1)}, f32[3,24,320]{2,1,0:T(8,128)S(1)}, u32[]{:S(2)}, u32[]{:S(2)}) collective-permute-start(f32[3,24,320]{2,1,0:T(8,128)S(1)} %get-tuple-element.66), channel_id=1, source_target_pairs={{1,0},{2,1},{3,2},{4,3},{5,4},{6,5},{7,6},{8,7},{9,8},{10,9},{11,1... | collective-permute-start | bytes 276488 | tf_op jit(solution)/shard_map/ppermute | solution.py:19
  77.9 2.8 %second_velocity.1 = (f32[3,24,32,320]{3,2,1,0:T(8,128)}, f32[6,25,32,320]{3,2,1,0:T(8,128)S(1)}, f32[3,25,32,320]{3,2,1,0:T(8,128)S(1)}) custom-call(f32[6,25,32,320]{3,2,1,0:T(8,128)S(1)} %get-tuple-element.51.refs_0_, f32[3,25,32,320]{3,2,1,0:T(8,128)S(1)} %get-tuple-element.52.refs_1_, ...), custom_call_target="tpu_custom_call", output_to_operand_aliasing={{1}: (0, {}), {2}: (1, {})} | custom-call | flops 24576000 | bytes 2949120 | tf_op jit(solution)/shard_map/second_velocity/pallas_call | solution.py:531
  80.7 2.6 %collective-permute-done.7.refs_5_ = f32[3,24,320]{2,1,0:T(8,128)S(1)} collective-permute-done((f32[3,24,320]{2,1,0:T(8,128)S(1)}, f32[3,24,320]{2,1,0:T(8,128)S(1)}, u32[]{:S(2)}, u32[]{:S(2)}) %collective-permute-start.7) | collective-permute-done | bytes 92192 | tf_op jit(solution)/shard_map/ppermute | solution.py:19
  83.3 0.0 collective-permute-done.6.refs_4_
  83.3 3.4 %second_stress.1 = (f32[6,24,32,320]{3,2,1,0:T(8,128)}, f32[6,25,32,320]{3,2,1,0:T(8,128)S(1)}, f32[3,25,32,320]{3,2,1,0:T(8,128)S(1)}) custom-call(f32[6,25,32,320]{3,2,1,0:T(8,128)S(1)} %get-tuple-element.61.refs_0_, f32[3,25,32,320]{3,2,1,0:T(8,128)S(1)} %get-tuple-element.62.refs_1_, ...), custom_call_target="tpu_custom_call", output_to_operand_aliasing={{1}: (0, {}), {2}: (1, {})} | custom-call | flops 24576000 | bytes 5898240 | tf_op jit(solution)/shard_map/second_stress/pallas_call | solution.py:531
  (1 shorter events, 0.0 us)
Async XLA Ops:
  4.6 28.5 %all-to-all-start = ((f32[128,16,128]{2,1,0:T(8,128)}), f32[128,16,128]{2,1,0:T(8,128)S(1)}, u32[]{:S(2)}, u32[]{:S(2)}) async-start(f32[128,16,128]{2,1,0:T(8,128)} %sections.1), calls=%async_computation | async-start | bytes 2097152 | tf_op jit(solution)/shard_map/all_to_all | solution.py:571
  15.0 18.1 %copy-start = (f32[64,384]{1,0:T(8,128)S(1)}, f32[64,384]{1,0:T(8,128)}, u32[]{:S(2)}) copy-start(f32[64,384]{1,0:T(8,128)} %weight_x.1) | copy-start | bytes 294916
  15.0 18.1 %copy-start.1 = (s32[3]{0:T(128)S(1)}, s32[3]{0:T(128)}, u32[]{:S(2)}) copy-start(s32[3]{0:T(128)} %anchor.3) | copy-start | bytes 40
  16.6 16.4 %collective-permute-start = (f32[4,32,320]{2,1,0:T(8,128)S(1)}, f32[4,32,320]{2,1,0:T(8,128)S(1)}, u32[]{:S(2)}, u32[]{:S(2)}) collective-permute-start(f32[4,32,320]{2,1,0:T(8,128)S(1)} %get-tuple-element.35), channel_id=1, source_target_pairs={{0,16},{16,32},{32,48},{48,64},{64,80},{80,96},{96,112},{1,17},{17... | collective-permute-start | bytes 491528 | tf_op jit(solution)/shard_map/ppermute | solution.py:19
  21.2 10.6 %collective-permute-start.1 = (f32[4,24,320]{2,1,0:T(8,128)S(1)}, f32[4,24,320]{2,1,0:T(8,128)S(1)}, u32[]{:S(2)}, u32[]{:S(2)}) collective-permute-start(f32[4,24,320]{2,1,0:T(8,128)S(1)} %get-tuple-element.36), channel_id=1, source_target_pairs={{0,1},{1,2},{2,3},{3,4},{4,5},{5,6},{6,7},{7,8},{8,9},{9,10},{10,1... | collective-permute-start | bytes 368648 | tf_op jit(solution)/shard_map/ppermute | solution.py:19
  35.2 19.6 %all-to-all-start.1 = ((f32[8,128,128]{2,1,0:T(8,128)}), f32[8,128,128]{2,1,0:T(8,128)S(1)}, u32[]{:S(2)}, u32[]{:S(2)}) async-start(f32[8,128,128]{2,1,0:T(8,128)} %contract.1), calls=%async_computation.1 | async-start | bytes 1048576 | tf_op jit(solution)/shard_map/all_to_all | solution.py:581
  41.0 13.8 %collective-permute-start.2 = (f32[3,32,320]{2,1,0:T(8,128)S(1)}, f32[3,32,320]{2,1,0:T(8,128)S(1)}, u32[]{:S(2)}, u32[]{:S(2)}) collective-permute-start(f32[3,32,320]{2,1,0:T(8,128)S(1)} %get-tuple-element.47), channel_id=1, source_target_pairs={{16,0},{32,16},{48,32},{64,48},{80,64},{96,80},{112,96},{17,1},{33... | collective-permute-start | bytes 368648 | tf_op jit(solution)/shard_map/ppermute | solution.py:19
  45.6 9.2 %collective-permute-start.3 = (f32[3,24,320]{2,1,0:T(8,128)S(1)}, f32[3,24,320]{2,1,0:T(8,128)S(1)}, u32[]{:S(2)}, u32[]{:S(2)}) collective-permute-start(f32[3,24,320]{2,1,0:T(8,128)S(1)} %get-tuple-element.48), channel_id=1, source_target_pairs={{1,0},{2,1},{3,2},{4,3},{5,4},{6,5},{7,6},{8,7},{9,8},{10,9},{11,1... | collective-permute-start | bytes 276488 | tf_op jit(solution)/shard_map/ppermute | solution.py:19
  62.0 10.1 %collective-permute-start.4 = (f32[3,32,320]{2,1,0:T(8,128)S(1)}, f32[3,32,320]{2,1,0:T(8,128)S(1)}, u32[]{:S(2)}, u32[]{:S(2)}) collective-permute-start(f32[3,32,320]{2,1,0:T(8,128)S(1)} %get-tuple-element.56), channel_id=1, source_target_pairs={{0,16},{16,32},{32,48},{48,64},{64,80},{80,96},{96,112},{1,17},{17... | collective-permute-start | bytes 368648 | tf_op jit(solution)/shard_map/ppermute | solution.py:19
  65.1 5.8 %collective-permute-start.5 = (f32[3,24,320]{2,1,0:T(8,128)S(1)}, f32[3,24,320]{2,1,0:T(8,128)S(1)}, u32[]{:S(2)}, u32[]{:S(2)}) collective-permute-start(f32[3,24,320]{2,1,0:T(8,128)S(1)} %get-tuple-element.57), channel_id=1, source_target_pairs={{0,1},{1,2},{2,3},{3,4},{4,5},{5,6},{6,7},{7,8},{8,9},{9,10},{10,1... | collective-permute-start | bytes 276488 | tf_op jit(solution)/shard_map/ppermute | solution.py:19
  72.3 11.0 %collective-permute-start.6 = (f32[3,32,320]{2,1,0:T(8,128)S(1)}, f32[3,32,320]{2,1,0:T(8,128)S(1)}, u32[]{:S(2)}, u32[]{:S(2)}) collective-permute-start(f32[3,32,320]{2,1,0:T(8,128)S(1)} %get-tuple-element.65), channel_id=1, source_target_pairs={{16,0},{32,16},{48,32},{64,48},{80,64},{96,80},{112,96},{17,1},{33... | collective-permute-start | bytes 368648 | tf_op jit(solution)/shard_map/ppermute | solution.py:19
  74.7 8.6 %collective-permute-start.7 = (f32[3,24,320]{2,1,0:T(8,128)S(1)}, f32[3,24,320]{2,1,0:T(8,128)S(1)}, u32[]{:S(2)}, u32[]{:S(2)}) collective-permute-start(f32[3,24,320]{2,1,0:T(8,128)S(1)} %get-tuple-element.66), channel_id=1, source_target_pairs={{1,0},{2,1},{3,2},{4,3},{5,4},{6,5},{7,6},{8,7},{9,8},{10,9},{11,1... | collective-permute-start | bytes 276488 | tf_op jit(solution)/shard_map/ppermute | solution.py:19

commit v6 on v5

--- a/solution.py
+++ b/solution.py
@@ -192,21 +192,28 @@
         copies[2 + t].wait()
         partly = split(dot(in_y, split(planes_in[t])))
         held[t, strip : strip + box_y, :box_z] = dot(partly, in_z, ((1,), (1,)))
+    free = lax.broadcasted_iota(jnp.int32, (1, lanes), 1) >= box_z
+    width = lanes - box_z
     for k in range(columns):
         for i in range(size_x):
-            start = strip + (k * size_x + i) * part - 1
+            start = strip + (k * size_x + i) * part
+            device = i * size_y + size_y - columns + k
             for t in range(own):
-                piece = held[t, start : start + part + 1]
-                row = t * (part + 1)
-                out[i * size_y + size_y - columns + k, row : row + part + 1] = piece
-
-
-def sections(planes, weight_y, weight_z, size_x, size_y, columns, height):
+                row = (device * own + t) * part
+                out[row : row + part] = held[t, start : start + part]
+                for p in range(box_z // width if i == 0 and k > 0 else 0):
+                    ahead = pltpu.roll(held[t, start - 1 : start], box_z - p * width, 1)
+                    here = held[t, start + p : start + p + 1]
+                    out[row + p : row + p + 1] = jnp.where(free, ahead, here)
+
+
+def sections(planes, weight_y, weight_z, size_x, size_y, columns):
     own, box_y = planes.shape[0], weight_y.shape[0]
+    height = own * (box_y // (columns * size_x))
     return pl.pallas_call(
         functools.partial(sections_kernel, size_x, size_y, columns),
         in_specs=[pl.BlockSpec(memory_space=pltpu.HBM)] * 3,
-        out_shape=f32(size_x * size_y, height, lanes),
+        out_shape=f32(size_x * size_y * height, lanes),
         scratch_shapes=[
             pltpu.VMEM((own, strip + box_y, lanes), jnp.float32),
             *[pltpu.VMEM(a.shape, jnp.float32) for a in (planes, weight_y, weight_z)],
@@ -222,30 +229,28 @@
     size_x = out.shape[0]
     span = nx + 1
     devices = count // own
-    stride = gathered.shape[0] // devices
+    stride = own * part
     section = lax.broadcasted_iota(jnp.int32, (count, count), 0)
     column = lax.broadcasted_iota(jnp.int32, (count, count), 1)
     pick = section == own * lax.rem(column, devices) + lax.div(column, devices)
     pick = pick.astype(jnp.bfloat16)
     weights = [dot([w], [pick]).astype(jnp.bfloat16) for w in split(weight_x[...])]
     padded[...] = jnp.zeros_like(padded)
-    for r in range(part + 1):
-        terms = [
-            gathered[pl.ds(t * (part + 1) + r, devices, stride=stride), :] for t in range(own)
-        ]
+    for r in range(part):
+        terms = [gathered[pl.ds(t * part + r, devices, stride=stride), :] for t in range(own)]
         box = dot(weights, split(jnp.concatenate(terms, 0)))
         padded[r, pl.ds(anchor[0] + strip, box_x), :] = box
     for i in range(size_x):
         start = strip + i * nx
-        for r in range(part + 1):
+        for r in range(part):
             out[i, r * span : r * span + nx] = padded[r, start : start + nx]
             out[i, r * span + nx : (r + 1) * span] = padded[r, start - 1 : start]
-        left = out.shape[1] - (part + 1) * span
-        out[i, (part + 1) * span :] = jnp.zeros((left, lanes), jnp.float32)
+        left = out.shape[1] - part * span
+        out[i, part * span :] = jnp.zeros((left, lanes), jnp.float32)
 
 
 def contract(anchor, weight_x, gathered, own, part, nx, size_x):
-    height = -(-(part + 1) * (nx + 1) // strip) * strip
+    height = -(-part * (nx + 1) // strip) * strip
     return pl.pallas_call(
         functools.partial(contract_kernel, own, part, nx),
         in_specs=[
@@ -254,13 +259,13 @@
             pl.BlockSpec(memory_space=pltpu.VMEM),
         ],
         out_shape=f32(size_x, height, lanes),
-        scratch_shapes=[pltpu.VMEM((part + 1, 2 * strip + size_x * nx, lanes), jnp.float32)],
+        scratch_shapes=[pltpu.VMEM((part, 2 * strip + size_x * nx, lanes), jnp.float32)],
         compiler_params=pltpu.CompilerParams(vmem_limit_bytes=16 << 20),
         name="contract",
     )(anchor, weight_x, gathered)
 
 
-def place_kernel(part, anchor, box, cells, rate_plane, rate_rows, *refs):
+def place_kernel(part, box_z, anchor, box, cells, rate_plane, rate_rows, *refs):
     out, out_plane, out_rows, held = refs
     size_x = box.shape[0]
     _, ny, nz = out.shape
@@ -269,12 +274,12 @@
     for i in range(size_x):
         for r in range(part):
             y = i * part + r
-            first = (r + 1) * span
+            first = r * span
             held[pl.ds(y, nx, stride=ny), :] = box[i, first : first + nx]
             held[nx * ny + y : nx * ny + y + 1] = box[i, first + nx : first + nx + 1]
     cell = lax.broadcasted_iota(jnp.int32, (lanes, nz), 1)
     which = lax.broadcasted_iota(jnp.int32, (lanes, nz), 0)
-    pick = (cell - anchor[2] == which).astype(jnp.bfloat16)
+    pick = ((cell - anchor[2] == which) & (which < box_z)).astype(jnp.bfloat16)
 
     def placed(values):
         return (-time_step) * dot(split(values, 3), [pick])
@@ -289,14 +294,20 @@
             out[t + u + 1] = decay * values[u * ny : (u + 1) * ny]
     out[0] = jnp.zeros((ny, nz), jnp.float32)
     out_plane[...] = lost(held[nx * ny :], rate_plane[3])
-    out_rows[...] = lost(box[0, 0:nx], rate_rows[3])
-
-
-def place(anchor, box, cells, rate_plane, rate_rows, part):
+    width = lanes - box_z
+    piece = lax.div(lax.broadcasted_iota(jnp.int32, (nx, lanes), 1), width)
+    ahead = jnp.zeros((nx, lanes), jnp.float32)
+    for p in range(box_z // width):
+        values = pltpu.roll(box[0, p * span : p * span + nx], lanes - box_z + p * width, 1)
+        ahead = jnp.where(piece == p, values, ahead)
+    out_rows[...] = lost(ahead, rate_rows[3])
+
+
+def place(anchor, box, cells, rate_plane, rate_rows, part, box_z):
     nx, ny, nz = cells.shape[1] - 1, *cells.shape[2:]
     on_chip = pl.BlockSpec(memory_space=pltpu.VMEM)
     return pl.pallas_call(
-        functools.partial(place_kernel, part),
+        functools.partial(place_kernel, part, box_z),
         in_specs=[pl.BlockSpec(memory_space=pltpu.SMEM)] + [on_chip] * 4,
         out_specs=(on_chip,) * 3,
         out_shape=(pltpu.VMEM((nx + 1, ny, nz), jnp.float32), f32(ny, nz), f32(nx, nz)),
@@ -564,10 +575,10 @@
     own = source_planes.shape[0]
     columns = box_y // ny
     part = ny // size_x
-    height = -(-own * (part + 1) // strip) * strip
     coefficients = (buoyancy, lame_lambda, lame_mu, attenuation)
 
-    pieces = sections(source_planes, weight_y, weight_z, size_x, size_y, columns, height)
+    pieces = sections(source_planes, weight_y, weight_z, size_x, size_y, columns)
+    pieces = pieces.reshape(sources, part, lanes)
     gathered = lax.all_to_all(pieces, ("gx", "gy"), 0, 0, tiled=True)
     send_x, send_y, *parts = edges(stress, velocity, buoyancy, attenuation)
     plane = neighbour(send_x, "gx", 1)
@@ -575,7 +586,7 @@
     first_x, first_y = first_edges(*parts, plane, rows)
 
     gathered, first_x, first_y = lax.optimization_barrier((gathered, first_x, first_y))
-    gathered = gathered.reshape(size_x * size_y * height, lanes)
+    gathered = gathered.reshape(sources * part, lanes)
     shares = contract(box_anchor, weight_x, gathered, own, part, nx, size_x)
     shares, first_x, first_y = lax.optimization_barrier((shares, first_x, first_y))
     box = lax.all_to_all(shares, "gx", 0, 0, tiled=True)
@@ -588,7 +599,7 @@
     )
     lower_x = neighbour(last_x, "gx", 1)
     lower_y = neighbour(last_y, "gy", 1)
-    source = place(box_anchor, box, cells, plane, rows, part)
+    source = place(box_anchor, box, cells, plane, rows, part, weight_z.shape[0])
     first_x, first_y = second_edges(parts, lower_x, lower_y, source)
     upper_x = neighbour(first_x, "gx", -1)
     upper_y = neighbour(first_y, "gy", -1)

time: 87.3 us -> 84.1 us (0.963)
  waiting for transfers between devices: 19.5 us -> 16 us
    ppermute x8, waiting for transfers between devices: 19.5 us -> 16 us  [neighbour(): return lax.ppermute(value, axis, pairs)]
where the time goes in v6:
time: 84.1 us; the launch traced here: 83.2 us
  starting transfers between devices  43.9 us (52%)
  Pallas kernels  22.5 us (27%)
  waiting for transfers between devices  16 us (19%)
    ppermute x8, starting transfers between devices, neighbour(): return lax.ppermute(value, axis, pairs)  27.7 us
    ppermute x8, waiting for transfers between devices, neighbour(): return lax.ppermute(value, axis, pairs)  16 us
    all_to_all x1, starting transfers between devices, shards(): gathered = lax.all_to_all(pieces, ('gx', 'gy'), 0, 0, tiled=True)  10.4 us
    pallas_call x1, Pallas kernels, first_step(): pl.pallas_call(functools.partial(step_kernel, 'first'), in_specs=[pl.Bloc...  7.25 us
    pallas_call x2, Pallas kernels, second_step(): pl.pallas_call(functools.partial(step_kernel, kind), in_specs=[on_chip] *...  6.18 us
    all_to_all x1, starting transfers between devices, shards(): box = lax.all_to_all(shares, 'gx', 0, 0, tiled=True)  5.82 us
    pallas_call x1, Pallas kernels, sections(): pl.pallas_call(functools.partial(sections_kernel, size_x, size_y, columns...  3.9 us
    pallas_call x1, Pallas kernels, contract(): pl.pallas_call(functools.partial(contract_kernel, own, part, nx), in_spec...  1.92 us
  transfers between devices with their start and end apart: 10, of which 6 were waited for; matrix products, arithmetic and copies ran while one was open for 0% of the time, Pallas kernels for 7%

profile of v6, /device:TPU:57, one launch (start us, length us, event | category | flops | bytes accessed | tf_op | source)
XLA Modules:
  0.0 83.2 jit_solution(2927837305781374915)
XLA Ops:
  0.6 3.9 %sections.1 = f32[1536,128]{1,0:T(8,128)} custom-call(f32[3,384,384]{2,1,0:T(8,128)} %planes.1, f32[96,384]{1,0:T(8,128)} %weight_y.1, f32[96,384]{1,0:T(8,128)} %weight_z.1), custom_call_target="tpu_custom_call" | custom-call | tf_op jit(solution)/shard_map/sections/pallas_call | solution.py:213
  4.5 10.4 %all-to-all-start = ((f32[384,4,128]{2,1,0:T(4,128)}), f32[384,4,128]{2,1,0:T(4,128)S(1)}, u32[]{:S(2)}, u32[]{:S(2)}) async-start(f32[384,4,128]{2,1,0:T(4,128)} %bitcast), calls=%async_computation | async-start | bytes 1572864 | tf_op jit(solution)/shard_map/all_to_all | solution.py:582
  15.0 0.0 copy-start
  15.0 0.0 copy-start.1
  15.0 1.6 %edges.1 = (f32[4,32,320]{2,1,0:T(8,128)S(1)}, f32[4,24,320]{2,1,0:T(8,128)S(1)}, f32[3,32,320]{2,1,0:T(8,128)S(1)}, f32[3,24,320]{2,1,0:T(8,128)S(1)}, f32[32,320]{1,0:T(8,128)S(1)}, /*index=5*/f32[24,320]{1,0:T(8,128)S(1)}) custom-call(f32[6,24,32,320]{3,2,1,0:T(8,128)} %refs_0_.1, f32[3,24,32,320]{3,2,1,0:T(8,128)} %refs_1_.1, f32[24,32,320]{2,1,0:T(8,128)} %refs_2_.1, ...), custom_call_target="tpu_custom_call" | custom-call | tf_op jit(solution)/shard_map/edges/pallas_call | solution.py:133
  16.6 4.6 %collective-permute-start = (f32[4,32,320]{2,1,0:T(8,128)S(1)}, f32[4,32,320]{2,1,0:T(8,128)S(1)}, u32[]{:S(2)}, u32[]{:S(2)}) collective-permute-start(f32[4,32,320]{2,1,0:T(8,128)S(1)} %get-tuple-element.35), channel_id=1, source_target_pairs={{0,16},{16,32},{32,48},{48,64},{64,80},{80,96},{96,112},{1,17},{17... | collective-permute-start | bytes 491528 | tf_op jit(solution)/shard_map/ppermute | solution.py:19
  21.2 2.5 %collective-permute-start.1 = (f32[4,24,320]{2,1,0:T(8,128)S(1)}, f32[4,24,320]{2,1,0:T(8,128)S(1)}, u32[]{:S(2)}, u32[]{:S(2)}) collective-permute-start(f32[4,24,320]{2,1,0:T(8,128)S(1)} %get-tuple-element.36), channel_id=1, source_target_pairs={{0,1},{1,2},{2,3},{3,4},{4,5},{5,6},{6,7},{7,8},{8,9},{9,10},{10,1... | collective-permute-start | bytes 368648 | tf_op jit(solution)/shard_map/ppermute | solution.py:19
  23.7 5.3 %collective-permute-done.1.rows.refs_7_.rate_rows = f32[4,24,320]{2,1,0:T(8,128)S(1)} collective-permute-done((f32[4,24,320]{2,1,0:T(8,128)S(1)}, f32[4,24,320]{2,1,0:T(8,128)S(1)}, u32[]{:S(2)}, u32[]{:S(2)}) %collective-permute-start.1) | collective-permute-done | bytes 122912 | tf_op jit(solution)/shard_map/ppermute | solution.py:19
  29.0 1.1 %collective-permute-done.plane.refs_6_.rate_plane = f32[4,32,320]{2,1,0:T(8,128)S(1)} collective-permute-done((f32[4,32,320]{2,1,0:T(8,128)S(1)}, f32[4,32,320]{2,1,0:T(8,128)S(1)}, u32[]{:S(2)}, u32[]{:S(2)}) %collective-permute-start) | collective-permute-done | bytes 163872 | tf_op jit(solution)/shard_map/ppermute | solution.py:19
  30.2 0.0 all-to-all-done
  30.2 0.0 copy-done
  30.2 0.0 copy-done.1
  30.2 1.9 %contract.1 = f32[8,104,128]{2,1,0:T(8,128)} custom-call(s32[3]{0:T(128)S(1)} %copy-done.1, f32[64,384]{1,0:T(8,128)S(1)} %copy-done, f32[1536,128]{1,0:T(8,128)S(1)} %bitcast.2), custom_call_target="tpu_custom_call" | custom-call | tf_op jit(solution)/shard_map/contract/pallas_call | solution.py:254
  32.1 5.8 %all-to-all-start.1 = ((f32[8,104,128]{2,1,0:T(8,128)}), f32[8,104,128]{2,1,0:T(8,128)S(1)}, u32[]{:S(2)}, u32[]{:S(2)}) async-start(f32[8,104,128]{2,1,0:T(8,128)} %contract.1), calls=%async_computation.1 | async-start | bytes 851968 | tf_op jit(solution)/shard_map/all_to_all | solution.py:592
  38.0 4.6 %collective-permute-start.2 = (f32[3,32,320]{2,1,0:T(8,128)S(1)}, f32[3,32,320]{2,1,0:T(8,128)S(1)}, u32[]{:S(2)}, u32[]{:S(2)}) collective-permute-start(f32[3,32,320]{2,1,0:T(8,128)S(1)} %get-tuple-element.47), channel_id=1, source_target_pairs={{16,0},{32,16},{48,32},{64,48},{80,64},{96,80},{112,96},{17,1},{33... | collective-permute-start | bytes 368648 | tf_op jit(solution)/shard_map/ppermute | solution.py:19
  42.6 3.0 %collective-permute-start.3 = (f32[3,24,320]{2,1,0:T(8,128)S(1)}, f32[3,24,320]{2,1,0:T(8,128)S(1)}, u32[]{:S(2)}, u32[]{:S(2)}) collective-permute-start(f32[3,24,320]{2,1,0:T(8,128)S(1)} %get-tuple-element.48), channel_id=1, source_target_pairs={{1,0},{2,1},{3,2},{4,3},{5,4},{6,5},{7,6},{8,7},{9,8},{10,9},{11,1... | collective-permute-start | bytes 276488 | tf_op jit(solution)/shard_map/ppermute | solution.py:19
  45.6 6.1 %collective-permute-done.3.refs_9_ = f32[3,24,320]{2,1,0:T(8,128)S(1)} collective-permute-done((f32[3,24,320]{2,1,0:T(8,128)S(1)}, f32[3,24,320]{2,1,0:T(8,128)S(1)}, u32[]{:S(2)}, u32[]{:S(2)}) %collective-permute-start.3) | collective-permute-done | bytes 92192 | tf_op jit(solution)/shard_map/ppermute | solution.py:19
  51.7 0.0 collective-permute-done.2.refs_8_
  51.7 0.0 all-to-all-done.1.box
  51.7 7.3 %first_step.1 = (f32[6,25,32,320]{3,2,1,0:T(8,128)S(1)}, f32[3,25,32,320]{3,2,1,0:T(8,128)S(1)}, f32[4,25,32,320]{3,2,1,0:T(8,128)S(1)}, f32[3,32,320]{2,1,0:T(8...) custom-call(f32[6,24,32,320]{3,2,1,0:T(8,128)} %refs_0_.1, ...), custom_call_target="tpu_custom_call" | custom-call | flops 24576000 | bytes 12779520 | tf_op jit(solution)/shard_map/first_step/pallas_call | solution.py:522
  59.0 2.8 %collective-permute-start.4 = (f32[3,32,320]{2,1,0:T(8,128)S(1)}, f32[3,32,320]{2,1,0:T(8,128)S(1)}, u32[]{:S(2)}, u32[]{:S(2)}) collective-permute-start(f32[3,32,320]{2,1,0:T(8,128)S(1)} %get-tuple-element.56), channel_id=1, source_target_pairs={{0,16},{16,32},{32,48},{48,64},{64,80},{80,96},{96,112},{1,17},{17... | collective-permute-start | bytes 368648 | tf_op jit(solution)/shard_map/ppermute | solution.py:19
  61.8 4.2 %collective-permute-start.5 = (f32[3,24,320]{2,1,0:T(8,128)S(1)}, f32[3,24,320]{2,1,0:T(8,128)S(1)}, u32[]{:S(2)}, u32[]{:S(2)}) collective-permute-start(f32[3,24,320]{2,1,0:T(8,128)S(1)} %get-tuple-element.57), channel_id=1, source_target_pairs={{0,1},{1,2},{2,3},{3,4},{4,5},{5,6},{6,7},{7,8},{8,9},{9,10},{10,1... | collective-permute-start | bytes 276488 | tf_op jit(solution)/shard_map/ppermute | solution.py:19
  66.0 1.5 %place.1 = (f32[25,32,320]{2,1,0:T(8,128)S(1)}, f32[32,320]{1,0:T(8,128)S(1)}, f32[24,320]{1,0:T(8,128)S(1)}) custom-call(s32[3]{0:T(128)S(1)} %copy-done.1, f32[8,104,128]{2,1,0:T(8,128)S(1)} %all-to-all-done.1.box, f32[4,25,32,320]{3,2,1,0:T(8,128)S(1)} %get-tuple-element.53.cells.refs_2_, f32[4,32,320]{2,1,0:T(8,128)S(1)} %collective-permute-done.plane.refs_6_.rate_plane, ...), custom_call_target="tpu_custom_call" | custom-call | tf_op jit(solution)/shard_map/place/pallas_call | solution.py:309
  67.5 0.2 collective-permute-done.5.refs_5_
  67.7 0.1 collective-permute-done.4.refs_4_
  67.8 0.1 second_edges.1
  67.9 3.3 %collective-permute-start.6 = (f32[3,32,320]{2,1,0:T(8,128)S(1)}, f32[3,32,320]{2,1,0:T(8,128)S(1)}, u32[]{:S(2)}, u32[]{:S(2)}) collective-permute-start(f32[3,32,320]{2,1,0:T(8,128)S(1)} %get-tuple-element.65), channel_id=1, source_target_pairs={{16,0},{32,16},{48,32},{64,48},{80,64},{96,80},{112,96},{17,1},{33... | collective-permute-start | bytes 368648 | tf_op jit(solution)/shard_map/ppermute | solution.py:19
  71.2 2.6 %collective-permute-start.7 = (f32[3,24,320]{2,1,0:T(8,128)S(1)}, f32[3,24,320]{2,1,0:T(8,128)S(1)}, u32[]{:S(2)}, u32[]{:S(2)}) collective-permute-start(f32[3,24,320]{2,1,0:T(8,128)S(1)} %get-tuple-element.66), channel_id=1, source_target_pairs={{1,0},{2,1},{3,2},{4,3},{5,4},{6,5},{7,6},{8,7},{9,8},{10,9},{11,1... | collective-permute-start | bytes 276488 | tf_op jit(solution)/shard_map/ppermute | solution.py:19
  73.8 2.8 %second_velocity.1 = (f32[3,24,32,320]{3,2,1,0:T(8,128)}, f32[6,25,32,320]{3,2,1,0:T(8,128)S(1)}, f32[3,25,32,320]{3,2,1,0:T(8,128)S(1)}) custom-call(f32[6,25,32,320]{3,2,1,0:T(8,128)S(1)} %get-tuple-element.51.refs_0_, f32[3,25,32,320]{3,2,1,0:T(8,128)S(1)} %get-tuple-element.52.refs_1_, ...), custom_call_target="tpu_custom_call", output_to_operand_aliasing={{1}: (0, {}), {2}: (1, {})} | custom-call | flops 24576000 | bytes 2949120 | tf_op jit(solution)/shard_map/second_velocity/pallas_call | solution.py:542
  76.6 3.2 %collective-permute-done.7.refs_5_ = f32[3,24,320]{2,1,0:T(8,128)S(1)} collective-permute-done((f32[3,24,320]{2,1,0:T(8,128)S(1)}, f32[3,24,320]{2,1,0:T(8,128)S(1)}, u32[]{:S(2)}, u32[]{:S(2)}) %collective-permute-start.7) | collective-permute-done | bytes 92192 | tf_op jit(solution)/shard_map/ppermute | solution.py:19
  79.8 0.0 collective-permute-done.6.refs_4_
  79.8 3.4 %second_stress.1 = (f32[6,24,32,320]{3,2,1,0:T(8,128)}, f32[6,25,32,320]{3,2,1,0:T(8,128)S(1)}, f32[3,25,32,320]{3,2,1,0:T(8,128)S(1)}) custom-call(f32[6,25,32,320]{3,2,1,0:T(8,128)S(1)} %get-tuple-element.61.refs_0_, f32[3,25,32,320]{3,2,1,0:T(8,128)S(1)} %get-tuple-element.62.refs_1_, ...), custom_call_target="tpu_custom_call", output_to_operand_aliasing={{1}: (0, {}), {2}: (1, {})} | custom-call | flops 24576000 | bytes 5898240 | tf_op jit(solution)/shard_map/second_stress/pallas_call | solution.py:542
  (1 shorter events, 0.0 us)
Async XLA Ops:
  4.5 25.7 %all-to-all-start = ((f32[384,4,128]{2,1,0:T(4,128)}), f32[384,4,128]{2,1,0:T(4,128)S(1)}, u32[]{:S(2)}, u32[]{:S(2)}) async-start(f32[384,4,128]{2,1,0:T(4,128)} %bitcast), calls=%async_computation | async-start | bytes 1572864 | tf_op jit(solution)/shard_map/all_to_all | solution.py:582
  15.0 15.2 %copy-start = (f32[64,384]{1,0:T(8,128)S(1)}, f32[64,384]{1,0:T(8,128)}, u32[]{:S(2)}) copy-start(f32[64,384]{1,0:T(8,128)} %weight_x.1) | copy-start | bytes 294916
  15.0 15.2 %copy-start.1 = (s32[3]{0:T(128)S(1)}, s32[3]{0:T(128)}, u32[]{:S(2)}) copy-start(s32[3]{0:T(128)} %anchor.3) | copy-start | bytes 40
  16.6 13.6 %collective-permute-start = (f32[4,32,320]{2,1,0:T(8,128)S(1)}, f32[4,32,320]{2,1,0:T(8,128)S(1)}, u32[]{:S(2)}, u32[]{:S(2)}) collective-permute-start(f32[4,32,320]{2,1,0:T(8,128)S(1)} %get-tuple-element.35), channel_id=1, source_target_pairs={{0,16},{16,32},{32,48},{48,64},{64,80},{80,96},{96,112},{1,17},{17... | collective-permute-start | bytes 491528 | tf_op jit(solution)/shard_map/ppermute | solution.py:19
  21.2 7.8 %collective-permute-start.1 = (f32[4,24,320]{2,1,0:T(8,128)S(1)}, f32[4,24,320]{2,1,0:T(8,128)S(1)}, u32[]{:S(2)}, u32[]{:S(2)}) collective-permute-start(f32[4,24,320]{2,1,0:T(8,128)S(1)} %get-tuple-element.36), channel_id=1, source_target_pairs={{0,1},{1,2},{2,3},{3,4},{4,5},{5,6},{6,7},{7,8},{8,9},{9,10},{10,1... | collective-permute-start | bytes 368648 | tf_op jit(solution)/shard_map/ppermute | solution.py:19
  32.1 19.6 %all-to-all-start.1 = ((f32[8,104,128]{2,1,0:T(8,128)}), f32[8,104,128]{2,1,0:T(8,128)S(1)}, u32[]{:S(2)}, u32[]{:S(2)}) async-start(f32[8,104,128]{2,1,0:T(8,128)} %contract.1), calls=%async_computation.1 | async-start | bytes 851968 | tf_op jit(solution)/shard_map/all_to_all | solution.py:592
  38.0 13.8 %collective-permute-start.2 = (f32[3,32,320]{2,1,0:T(8,128)S(1)}, f32[3,32,320]{2,1,0:T(8,128)S(1)}, u32[]{:S(2)}, u32[]{:S(2)}) collective-permute-start(f32[3,32,320]{2,1,0:T(8,128)S(1)} %get-tuple-element.47), channel_id=1, source_target_pairs={{16,0},{32,16},{48,32},{64,48},{80,64},{96,80},{112,96},{17,1},{33... | collective-permute-start | bytes 368648 | tf_op jit(solution)/shard_map/ppermute | solution.py:19
  42.6 9.2 %collective-permute-start.3 = (f32[3,24,320]{2,1,0:T(8,128)S(1)}, f32[3,24,320]{2,1,0:T(8,128)S(1)}, u32[]{:S(2)}, u32[]{:S(2)}) collective-permute-start(f32[3,24,320]{2,1,0:T(8,128)S(1)} %get-tuple-element.48), channel_id=1, source_target_pairs={{1,0},{2,1},{3,2},{4,3},{5,4},{6,5},{7,6},{8,7},{9,8},{10,9},{11,1... | collective-permute-start | bytes 276488 | tf_op jit(solution)/shard_map/ppermute | solution.py:19
  59.0 8.8 %collective-permute-start.4 = (f32[3,32,320]{2,1,0:T(8,128)S(1)}, f32[3,32,320]{2,1,0:T(8,128)S(1)}, u32[]{:S(2)}, u32[]{:S(2)}) collective-permute-start(f32[3,32,320]{2,1,0:T(8,128)S(1)} %get-tuple-element.56), channel_id=1, source_target_pairs={{0,16},{16,32},{32,48},{48,64},{64,80},{80,96},{96,112},{1,17},{17... | collective-permute-start | bytes 368648 | tf_op jit(solution)/shard_map/ppermute | solution.py:19
  61.8 5.9 %collective-permute-start.5 = (f32[3,24,320]{2,1,0:T(8,128)S(1)}, f32[3,24,320]{2,1,0:T(8,128)S(1)}, u32[]{:S(2)}, u32[]{:S(2)}) collective-permute-start(f32[3,24,320]{2,1,0:T(8,128)S(1)} %get-tuple-element.57), channel_id=1, source_target_pairs={{0,1},{1,2},{2,3},{3,4},{4,5},{5,6},{6,7},{7,8},{8,9},{9,10},{10,1... | collective-permute-start | bytes 276488 | tf_op jit(solution)/shard_map/ppermute | solution.py:19
  67.9 11.8 %collective-permute-start.6 = (f32[3,32,320]{2,1,0:T(8,128)S(1)}, f32[3,32,320]{2,1,0:T(8,128)S(1)}, u32[]{:S(2)}, u32[]{:S(2)}) collective-permute-start(f32[3,32,320]{2,1,0:T(8,128)S(1)} %get-tuple-element.65), channel_id=1, source_target_pairs={{16,0},{32,16},{48,32},{64,48},{80,64},{96,80},{112,96},{17,1},{33... | collective-permute-start | bytes 368648 | tf_op jit(solution)/shard_map/ppermute | solution.py:19
  71.2 8.5 %collective-permute-start.7 = (f32[3,24,320]{2,1,0:T(8,128)S(1)}, f32[3,24,320]{2,1,0:T(8,128)S(1)}, u32[]{:S(2)}, u32[]{:S(2)}) collective-permute-start(f32[3,24,320]{2,1,0:T(8,128)S(1)} %get-tuple-element.66), channel_id=1, source_target_pairs={{1,0},{2,1},{3,2},{4,3},{5,4},{6,5},{7,6},{8,7},{9,8},{10,9},{11,1... | collective-permute-start | bytes 276488 | tf_op jit(solution)/shard_map/ppermute | solution.py:19

commit v7 on v6

--- a/solution.py
+++ b/solution.py
@@ -10,7 +10,7 @@
 time_step = 0.2
 strip = 8
 lanes = 128
-per = 3
+per = 2
 
 
 def neighbour(value, axis, by):
@@ -88,7 +88,7 @@
     return after_row(values, 0.0)
 
 
-def edges_kernel(stress, velocity, buoyancy, attenuation, *refs):
+def edges_kernel(between, stress, velocity, buoyancy, *refs):
     out_plane, out_rows, part_plane, part_rows, b_plane, b_rows = refs[:6]
     s_plane, s_rows, v_plane, v_rows, sems = refs[6:]
     _, nx, ny, _ = stress.shape
@@ -101,15 +101,14 @@
         (buoyancy.at[:, 0], b_rows),
         (stress.at[0, nx - 1], out_plane.at[0]),
         (stress.at[3:5, nx - 1], out_plane.at[1:3]),
-        (attenuation.at[nx - 1], out_plane.at[3]),
         (stress.at[3, :, ny - 1], out_rows.at[0]),
         (stress.at[1, :, ny - 1], out_rows.at[1]),
         (stress.at[5, :, ny - 1], out_rows.at[2]),
-        (attenuation.at[:, ny - 1], out_rows.at[3]),
     ]
     copies = [pltpu.make_async_copy(*move, sems.at[k]) for k, move in enumerate(moves)]
     for copy in copies:
         copy.start()
+    between()
     for copy in copies:
         copy.wait()
     partial_velocity(
@@ -126,31 +125,6 @@
         part_rows,
         (row_before, nothing),
     )
-
-
-def edges(stress, velocity, buoyancy, attenuation):
-    _, nx, ny, nz = stress.shape
-    return pl.pallas_call(
-        edges_kernel,
-        in_specs=[pl.BlockSpec(memory_space=pltpu.HBM)] * 4,
-        out_shape=(
-            f32(4, ny, nz),
-            f32(4, nx, nz),
-            f32(3, ny, nz),
-            f32(3, nx, nz),
-            f32(ny, nz),
-            f32(nx, nz),
-        ),
-        scratch_shapes=[
-            pltpu.VMEM((6, ny, nz), jnp.float32),
-            pltpu.VMEM((6, nx, nz), jnp.float32),
-            pltpu.VMEM((3, ny, nz), jnp.float32),
-            pltpu.VMEM((3, nx, nz), jnp.float32),
-            pltpu.SemaphoreType.DMA((13,)),
-        ],
-        compiler_params=pltpu.CompilerParams(vmem_limit_bytes=8 << 20),
-        name="edges",
-    )(*map(in_hbm, (stress, velocity, buoyancy, attenuation)))
 
 
 def take_halo(part_plane, part_rows, b_plane, b_rows, plane, rows, out_plane, out_rows):
@@ -164,17 +138,9 @@
         out_rows[c] = part_rows[c] - factor_rows * (rows[c] + corner)
 
 
-def first_edges(part_plane, part_rows, b_plane, b_rows, plane, rows):
-    return pl.pallas_call(
-        take_halo,
-        out_shape=(f32(*part_plane.shape), f32(*part_rows.shape)),
-        compiler_params=pltpu.CompilerParams(vmem_limit_bytes=8 << 20),
-        name="first_edges",
-    )(part_plane, part_rows, b_plane, b_rows, plane, rows)
-
-
-def sections_kernel(size_x, size_y, columns, planes, weight_y, weight_z, out, *refs):
-    held, planes_in, y_in, z_in, sems = refs
+def sections_kernel(size_x, size_y, columns, *refs):
+    planes, weight_y, weight_z = refs[:3]
+    out, (held, planes_in, y_in, z_in, sems) = refs[6], refs[13:18]
     own = planes.shape[0]
     box_y, box_z = weight_y.shape[0], weight_z.shape[0]
     part = box_y // (columns * size_x)
@@ -183,48 +149,69 @@
     copies = [pltpu.make_async_copy(*move, sems.at[k]) for k, move in enumerate(moves)]
     for copy in copies:
         copy.start()
-    out[...] = jnp.zeros_like(out)
-    held[...] = jnp.zeros_like(held)
-    copies[0].wait()
-    copies[1].wait()
-    in_y, in_z = split(y_in[...]), split(z_in[...])
-    for t in range(own):
-        copies[2 + t].wait()
-        partly = split(dot(in_y, split(planes_in[t])))
-        held[t, strip : strip + box_y, :box_z] = dot(partly, in_z, ((1,), (1,)))
-    free = lax.broadcasted_iota(jnp.int32, (1, lanes), 1) >= box_z
-    width = lanes - box_z
-    for k in range(columns):
-        for i in range(size_x):
-            start = strip + (k * size_x + i) * part
-            device = i * size_y + size_y - columns + k
-            for t in range(own):
-                row = (device * own + t) * part
-                out[row : row + part] = held[t, start : start + part]
-                for p in range(box_z // width if i == 0 and k > 0 else 0):
-                    ahead = pltpu.roll(held[t, start - 1 : start], box_z - p * width, 1)
-                    here = held[t, start + p : start + p + 1]
-                    out[row + p : row + p + 1] = jnp.where(free, ahead, here)
-
-
-def sections(planes, weight_y, weight_z, size_x, size_y, columns):
+
+    def products():
+        out[...] = jnp.zeros_like(out)
+        held[...] = jnp.zeros_like(held)
+        copies[0].wait()
+        copies[1].wait()
+        in_y, in_z = split(y_in[...]), split(z_in[...])
+        for t in range(own):
+            copies[2 + t].wait()
+            partly = split(dot(in_y, split(planes_in[t])))
+            held[t, strip : strip + box_y, :box_z] = dot(partly, in_z, ((1,), (1,)))
+        free = lax.broadcasted_iota(jnp.int32, (1, lanes), 1) >= box_z
+        width = lanes - box_z
+        for k in range(columns):
+            for i in range(size_x):
+                start = strip + (k * size_x + i) * part
+                device = i * size_y + size_y - columns + k
+                for t in range(own):
+                    row = (device * own + t) * part
+                    out[row : row + part] = held[t, start : start + part]
+                    for p in range(box_z // width if i == 0 and k > 0 else 0):
+                        ahead = pltpu.roll(held[t, start - 1 : start], box_z - p * width, 1)
+                        here = held[t, start + p : start + p + 1]
+                        out[row + p : row + p + 1] = jnp.where(free, ahead, here)
+
+    edges_kernel(products, *refs[3:6], *refs[7:13], *refs[18:])
+
+
+def sections(planes, weight_y, weight_z, fields, size_x, size_y, columns):
     own, box_y = planes.shape[0], weight_y.shape[0]
     height = own * (box_y // (columns * size_x))
+    nx, ny, nz = fields[2].shape
+    on_chip = lambda *shape: pltpu.VMEM(shape, jnp.float32)
     return pl.pallas_call(
         functools.partial(sections_kernel, size_x, size_y, columns),
-        in_specs=[pl.BlockSpec(memory_space=pltpu.HBM)] * 3,
-        out_shape=f32(size_x * size_y * height, lanes),
+        in_specs=[pl.BlockSpec(memory_space=pltpu.HBM)] * 6,
+        out_shape=(
+            f32(size_x * size_y * height, lanes),
+            f32(3, ny, nz),
+            f32(3, nx, nz),
+            f32(3, ny, nz),
+            f32(3, nx, nz),
+            f32(ny, nz),
+            f32(nx, nz),
+        ),
         scratch_shapes=[
-            pltpu.VMEM((own, strip + box_y, lanes), jnp.float32),
-            *[pltpu.VMEM(a.shape, jnp.float32) for a in (planes, weight_y, weight_z)],
+            on_chip(own, strip + box_y, lanes),
+            *[on_chip(*a.shape) for a in (planes, weight_y, weight_z)],
             pltpu.SemaphoreType.DMA((2 + own,)),
+            on_chip(6, ny, nz),
+            on_chip(6, nx, nz),
+            on_chip(3, ny, nz),
+            on_chip(3, nx, nz),
+            pltpu.SemaphoreType.DMA((11,)),
         ],
         compiler_params=pltpu.CompilerParams(vmem_limit_bytes=16 << 20),
         name="sections",
-    )(*map(in_hbm, (planes, weight_y, weight_z)))
-
-
-def contract_kernel(own, part, nx, anchor, weight_x, gathered, out, padded):
+    )(*map(in_hbm, (planes, weight_y, weight_z, *fields)))
+
+
+def contract_kernel(own, part, nx, anchor, weight_x, gathered, *refs):
+    out, padded = refs[6], refs[9]
+    take_halo(*refs[:6], *refs[7:9])
     box_x, count = weight_x.shape
     size_x = out.shape[0]
     span = nx + 1
@@ -249,23 +236,24 @@
         out[i, part * span :] = jnp.zeros((left, lanes), jnp.float32)
 
 
-def contract(anchor, weight_x, gathered, own, part, nx, size_x):
+def contract(anchor, weight_x, gathered, edges, own, part, nx, size_x):
     height = -(-part * (nx + 1) // strip) * strip
     return pl.pallas_call(
         functools.partial(contract_kernel, own, part, nx),
-        in_specs=[
-            pl.BlockSpec(memory_space=pltpu.SMEM),
-            pl.BlockSpec(memory_space=pltpu.VMEM),
-            pl.BlockSpec(memory_space=pltpu.VMEM),
-        ],
-        out_shape=f32(size_x, height, lanes),
+        in_specs=[pl.BlockSpec(memory_space=pltpu.SMEM)]
+        + [pl.BlockSpec(memory_space=pltpu.VMEM)] * (2 + len(edges)),
+        out_shape=(
+            f32(size_x, height, lanes),
+            f32(*edges[0].shape),
+            f32(*edges[1].shape),
+        ),
         scratch_shapes=[pltpu.VMEM((part, 2 * strip + size_x * nx, lanes), jnp.float32)],
         compiler_params=pltpu.CompilerParams(vmem_limit_bytes=16 << 20),
         name="contract",
-    )(anchor, weight_x, gathered)
-
-
-def place_kernel(part, box_z, anchor, box, cells, rate_plane, rate_rows, *refs):
+    )(anchor, weight_x, gathered, *edges)
+
+
+def place_kernel(part, box_z, anchor, box, cells, *refs):
     out, out_plane, out_rows, held = refs
     size_x = box.shape[0]
     _, ny, nz = out.shape
@@ -284,44 +272,42 @@
     def placed(values):
         return (-time_step) * dot(split(values, 3), [pick])
 
-    def lost(values, rates):
-        return jnp.exp(-time_step * rates) * placed(values)
-
     for t in range(0, nx, 4):
         values = placed(held[t * ny : (t + 4) * ny])
         for u in range(4):
             decay = jnp.exp(-time_step * cells[3, t + u])
             out[t + u + 1] = decay * values[u * ny : (u + 1) * ny]
     out[0] = jnp.zeros((ny, nz), jnp.float32)
-    out_plane[...] = lost(held[nx * ny :], rate_plane[3])
+    out_plane[...] = placed(held[nx * ny :])
     width = lanes - box_z
     piece = lax.div(lax.broadcasted_iota(jnp.int32, (nx, lanes), 1), width)
     ahead = jnp.zeros((nx, lanes), jnp.float32)
     for p in range(box_z // width):
         values = pltpu.roll(box[0, p * span : p * span + nx], lanes - box_z + p * width, 1)
         ahead = jnp.where(piece == p, values, ahead)
-    out_rows[...] = lost(ahead, rate_rows[3])
-
-
-def place(anchor, box, cells, rate_plane, rate_rows, part, box_z):
+    out_rows[...] = placed(ahead)
+
+
+def place(anchor, box, cells, part, box_z):
     nx, ny, nz = cells.shape[1] - 1, *cells.shape[2:]
     on_chip = pl.BlockSpec(memory_space=pltpu.VMEM)
     return pl.pallas_call(
         functools.partial(place_kernel, part, box_z),
-        in_specs=[pl.BlockSpec(memory_space=pltpu.SMEM)] + [on_chip] * 4,
+        in_specs=[pl.BlockSpec(memory_space=pltpu.SMEM)] + [on_chip] * 2,
         out_specs=(on_chip,) * 3,
         out_shape=(pltpu.VMEM((nx + 1, ny, nz), jnp.float32), f32(ny, nz), f32(nx, nz)),
         scratch_shapes=[pltpu.VMEM(((nx + 1) * ny, lanes), jnp.float32)],
         compiler_params=pltpu.CompilerParams(vmem_limit_bytes=12 << 20),
         name="place",
-    )(anchor, box, in_vmem(cells), rate_plane, rate_rows)
+    )(anchor, box, in_vmem(cells))
 
 
 def second_edges_kernel(*refs):
     part_plane, part_rows, b_plane, b_rows, plane, rows = refs[:6]
-    source, source_plane, source_rows, first_plane, first_rows = refs[6:]
+    source, box_plane, box_rows, first_plane, first_rows = refs[6:]
     take_halo(part_plane, part_rows, b_plane, b_rows, plane, rows, first_plane, first_rows)
-    q_plane, q_rows = source_plane[...], source_rows[...]
+    q_plane = jnp.exp(-time_step * plane[3]) * box_plane[...]
+    q_rows = jnp.exp(-time_step * rows[3]) * box_rows[...]
     factor = time_step * b_plane[...]
     own = source[1]
     first_plane[0] = first_plane[0] + factor * (own - q_plane)
@@ -340,7 +326,7 @@
         second_edges_kernel,
         in_specs=[on_chip] * 9,
         out_specs=(on_chip,) * 2,
-        out_shape=(f32(*parts[0].shape), f32(*parts[1].shape)),
+        out_shape=tuple(f32(*a.shape) for a in parts[:2]),
         compiler_params=pltpu.CompilerParams(vmem_limit_bytes=8 << 20),
         name="second_edges",
     )(*parts, plane, rows, in_vmem(source[0]), *source[1:])
@@ -349,11 +335,13 @@
 def step_kernel(kind, *refs):
     with_source = kind != "first"
     if kind == "velocity":
-        cells, source, plane, rows, source_plane, source_rows = refs[2:8]
-        out_velocity, stress, velocity, out_sems = refs[8:]
-    elif kind == "stress":
+        stress, cells, source, velocity = refs[0], refs[2], refs[3], refs[4]
+    elif kind == "inner":
+        cells, source, first_plane, first_rows = refs[2:6]
+        out_stress, stress, velocity, out_velocity, out_sems = refs[6:]
+    elif kind == "outer":
         cells, source, upper_plane, upper_rows = refs[2:6]
-        out_stress, stress, velocity, out_sems = refs[6:]
+        out_stress, stress, velocity, out_sems = refs[7:]
     else:
         fields, (plane, rows, upper_plane, upper_rows) = refs[:6], refs[6:10]
         stress, velocity, cells, last_plane, last_rows, part_plane, part_rows = refs[10:17]
@@ -371,12 +359,13 @@
             moves.append((field.at[here], cells.at[n, here]))
         return [pltpu.make_async_copy(*m, in_sems.at[k, n]) for n, m in enumerate(moves)]
 
-    def leaving(k):
-        here, above = pl.ds(k * per, per), pl.ds(k * per + 1, per)
-        if kind == "velocity":
-            move = (velocity.at[:, here], out_velocity.at[:, here])
-        else:
-            move = (stress.at[:, above], out_stress.at[:, here])
+    inner = ny - strip
+
+    def leaving(k, first=0, count=per):
+        across = slice(0, inner) if kind == "inner" else slice(inner, ny)
+        here = pl.ds(k * per + first, count)
+        above = pl.ds(k * per + first + 1, count)
+        move = (stress.at[:, above, across], out_stress.at[:, here, across])
         return [pltpu.make_async_copy(*move, out_sems.at[k])]
 
     def every(make, act):
@@ -389,23 +378,24 @@
 
     if not with_source:
         every(arriving, lambda copy: copy.start())
-    if kind != "stress":
+    if kind == "first":
         for c, which in enumerate((0, 3, 4)):
             stress[which, 0] = plane[c]
-        if with_source:
-            stress[0, 0] = plane[0] + source_plane[...]
-    if kind != "velocity":
+    if kind in ("first", "outer"):
         for c in range(3):
             velocity[c, nx] = upper_plane[c]
+    if kind == "inner":
+        for c in range(3):
+            velocity[c, 0] = first_plane[c]
+            velocity[c, :nx, 0] = first_rows[c]
 
     top = lax.broadcasted_iota(jnp.int32, (strip, nz), 0) == 0
     bottom = lax.broadcasted_iota(jnp.int32, (strip, nz), 0) == strip - 1
 
     def velocity_plane(x):
-        above = [rows[c, pl.ds(x, 1)] for c in range(3)]
-        if with_source:
-            above[1] = above[1] + source_rows[pl.ds(x, 1)]
-        above = [jnp.broadcast_to(row, (strip, nz)) for row in above]
+        above = [jnp.zeros((strip, nz), jnp.float32)] * 3
+        if not with_source:
+            above = [jnp.broadcast_to(rows[c, pl.ds(x, 1)], (strip, nz)) for c in range(3)]
         for r in range(ny // strip):
             here = slice(strip * r, strip * (r + 1))
             s = [stress[c, x + 1, here] for c in range(6)]
@@ -427,9 +417,14 @@
                 velocity[c, x, here] = velocity[c, x, here] + factor * sums[c]
             above = rolled
 
-    def stress_plane(x):
-        below = [jnp.broadcast_to(upper_rows[c, pl.ds(x, 1)], (strip, nz)) for c in range(3)]
-        for r in reversed(range(ny // strip)):
+    def stress_plane(x, strips=range(ny // strip)):
+        if strips[-1] == ny // strip - 1:
+            below = [upper_rows[c, pl.ds(x, 1)] for c in range(3)]
+        else:
+            following = strip * (strips[-1] + 1)
+            below = [velocity[c, x, following : following + 1] for c in range(3)]
+        below = [jnp.broadcast_to(row, (strip, nz)) for row in below]
+        for r in reversed(strips):
             here = slice(strip * r, strip * (r + 1))
             v = [velocity[c, x, here] for c in range(3)]
             rolled = [pltpu.roll(value, strip - 1, 0) for value in v]
@@ -471,27 +466,59 @@
 
         def one_plane(m, _):
             x = k * per + (per - 1 - m)
-            if kind != "stress":
+            if kind in ("first", "velocity"):
                 velocity_plane(x)
-            if kind != "velocity":
+            if kind == "first":
                 stress_plane(x)
+            elif kind == "inner":
+                stress_plane(x, range(ny // strip - 1))
+            elif kind == "outer":
+                stress_plane(x, range(ny // strip - 1, ny // strip))
             return 0
 
         lax.fori_loop(0, per, one_plane, 0, unroll=True)
-        if with_source:
+        if kind in ("inner", "outer"):
             for copy in leaving(k):
                 copy.start()
         return 0
 
-    if not with_source:
+    if kind == "first":
         for copy in arriving(chunks - 1):
             copy.wait()
-    lax.fori_loop(0, chunks, one_chunk, 0)
-    if with_source:
-        every(leaving, lambda copy: copy.wait())
+    more = []
+    if kind == "inner":
+        more.append(
+            pltpu.make_async_copy(velocity.at[:, 0:nx], out_velocity, out_sems.at[chunks])
+        )
+        more[0].start()
+        for m in range(per - 1):
+            stress_plane(nx - 2 - m, range(ny // strip - 1))
+        more += leaving(chunks - 1, 0, per - 1)
+        more[1].start()
+        lax.fori_loop(1, chunks, one_chunk, 0)
+    elif kind == "outer":
+        stress_plane(nx - 1, range(ny // strip - 1))
+        move = (stress.at[:, nx, 0:inner], out_stress.at[:, nx - 1, 0:inner])
+        more.append(pltpu.make_async_copy(*move, out_sems.at[chunks]))
+        more[0].start()
+        lax.fori_loop(0, chunks, one_chunk, 0)
     else:
+        lax.fori_loop(0, chunks, one_chunk, 0)
+    if kind in ("inner", "outer"):
+
+        def done(n, _):
+            for copy in leaving(n):
+                copy.wait()
+            return 0
+
+        lax.fori_loop(0, chunks - (kind == "inner"), done, 0)
+        for copy in more:
+            copy.wait()
+    if kind == "first":
         for c, which in enumerate((0, 3, 4)):
             last_plane[c] = stress[which, nx]
+        last_plane[3] = cells[3, nx - 1]
+        last_rows[3] = cells[3, :nx, ny - 1]
         partial_velocity(
             [stress[c, 1] for c in range(6)],
             [velocity[c, 0] for c in range(3)],
@@ -525,7 +552,7 @@
         out_specs=(on_chip,) * 7,
         out_shape=(
             *[pltpu.VMEM((n, nx + 1, ny, nz), jnp.float32) for n in (6, 3, 4)],
-            *[f32(3, ny, nz), f32(3, nx, nz)] * 2,
+            *[f32(n, m, nz) for n in (4, 3) for m in (ny, nx)],
         ),
         scratch_shapes=[pltpu.SemaphoreType.DMA((nx // per, len(fields)))],
         compiler_params=pltpu.CompilerParams(vmem_limit_bytes=20 << 20),
@@ -534,25 +561,34 @@
     )(*fields, plane, rows, upper_plane, upper_rows)
 
 
-def second_step(kind, stress, velocity, cells, source, edges):
+def second_step(kind, stress, velocity, cells, source, edges=(), outside=None):
     nx, ny, nz = cells.shape[1] - 1, *cells.shape[2:]
     held = [in_vmem(a) for a in (stress, velocity, cells, source)]
-    on_chip = pl.BlockSpec(memory_space=pltpu.VMEM)
-    parts = 3 if kind == "velocity" else 6
+    on_chip, off_chip = [pl.BlockSpec(memory_space=m) for m in (pltpu.VMEM, pltpu.HBM)]
+    in_specs = [on_chip] * (len(held) + len(edges))
+    state = [pltpu.VMEM(a.shape, jnp.float32) for a in (stress, velocity)]
+    out = [pltpu.HBM((n, nx, ny, nz), jnp.float32) for n in (6, 3)]
+    args, sems = (*held, *edges), [pltpu.SemaphoreType.DMA((nx // per + 1,))]
+    if kind == "velocity":
+        out_shape, out_specs, aliases, sems = (state[1],), (on_chip,), {1: 0}, []
+    elif kind == "inner":
+        out_shape = (out[0], *state, out[1])
+        out_specs, aliases = (off_chip, on_chip, on_chip, off_chip), {0: 1, 1: 2}
+    else:
+        out_shape, out_specs = (out[0], *state), (off_chip, on_chip, on_chip)
+        aliases = {0: 1, 1: 2, len(args): 0}
+        in_specs, args = in_specs + [off_chip], (*args, in_hbm(outside))
     return pl.pallas_call(
         functools.partial(step_kernel, kind),
-        in_specs=[on_chip] * (len(held) + len(edges)),
-        out_specs=(pl.BlockSpec(memory_space=pltpu.HBM), on_chip, on_chip),
-        out_shape=(
-            pltpu.HBM((parts, nx, ny, nz), jnp.float32),
-            *[pltpu.VMEM(a.shape, jnp.float32) for a in (stress, velocity)],
-        ),
-        input_output_aliases={0: 1, 1: 2},
-        scratch_shapes=[pltpu.SemaphoreType.DMA((nx // per,))],
+        in_specs=in_specs,
+        out_specs=out_specs,
+        out_shape=out_shape,
+        input_output_aliases=aliases,
+        scratch_shapes=sems,
         compiler_params=pltpu.CompilerParams(vmem_limit_bytes=20 << 20),
-        cost_estimate=estimate(nx, ny, nz, parts),
+        cost_estimate=estimate(nx, ny, nz, 3),
         name="second_" + kind,
-    )(*held, *edges)
+    )(*args)
 
 
 def shards(
@@ -577,18 +613,19 @@
     part = ny // size_x
     coefficients = (buoyancy, lame_lambda, lame_mu, attenuation)
 
-    pieces = sections(source_planes, weight_y, weight_z, size_x, size_y, columns)
+    fields = (stress, velocity, buoyancy)
+    pieces, send_x, send_y, *parts = sections(
+        source_planes, weight_y, weight_z, fields, size_x, size_y, columns
+    )
     pieces = pieces.reshape(sources, part, lanes)
     gathered = lax.all_to_all(pieces, ("gx", "gy"), 0, 0, tiled=True)
-    send_x, send_y, *parts = edges(stress, velocity, buoyancy, attenuation)
     plane = neighbour(send_x, "gx", 1)
     rows = neighbour(send_y, "gy", 1)
-    first_x, first_y = first_edges(*parts, plane, rows)
-
-    gathered, first_x, first_y = lax.optimization_barrier((gathered, first_x, first_y))
+
     gathered = gathered.reshape(sources * part, lanes)
-    shares = contract(box_anchor, weight_x, gathered, own, part, nx, size_x)
-    shares, first_x, first_y = lax.optimization_barrier((shares, first_x, first_y))
+    shares, first_x, first_y = contract(
+        box_anchor, weight_x, gathered, (*parts, plane, rows), own, part, nx, size_x
+    )
     box = lax.all_to_all(shares, "gx", 0, 0, tiled=True)
     upper_x = neighbour(first_x, "gx", -1)
     upper_y = neighbour(first_y, "gy", -1)
@@ -599,15 +636,17 @@
     )
     lower_x = neighbour(last_x, "gx", 1)
     lower_y = neighbour(last_y, "gy", 1)
-    source = place(box_anchor, box, cells, plane, rows, part, weight_z.shape[0])
+    source = place(box_anchor, box, cells, part, weight_z.shape[0])
+    (speed,) = second_step("velocity", strained, speed, cells, source[0])
+    speed, lower_x, lower_y = lax.optimization_barrier((speed, lower_x, lower_y))
     first_x, first_y = second_edges(parts, lower_x, lower_y, source)
     upper_x = neighbour(first_x, "gx", -1)
     upper_y = neighbour(first_y, "gy", -1)
-    velocity_out, strained, speed = second_step(
-        "velocity", strained, speed, cells, source[0], (lower_x, lower_y, *source[1:])
+    partly, strained, speed, velocity_out = second_step(
+        "inner", strained, speed, cells, source[0], (first_x, first_y)
     )
     stress_out, _, _ = second_step(
-        "stress", strained, speed, cells, source[0], (upper_x, upper_y)
+        "outer", strained, speed, cells, source[0], (upper_x, upper_y), partly
     )
     return (velocity_out, stress_out)
 

time: 84.1 us -> 83 us (0.987)
    pallas_call x4 -> x3, Pallas kernels: 7.8 us -> 7.81 us  [second_step(): pl.pallas_call(functools.partial(step_kernel, kind), in_specs=in_specs, o...]
  transfers between devices with their start and end apart: 10 -> 10, of which waited for: 6 -> 4; matrix products, arithmetic and copies ran while one was open for 0% -> 0% of each run, Pallas kernels for 7% -> 9%
where the time goes in v7:
time: 83 us; the launch traced here: 82.5 us
  starting transfers between devices  43.3 us (52%)
  Pallas kernels  23 us (28%)
  waiting for transfers between devices  15.4 us (19%)
    ppermute x8, starting transfers between devices, neighbour(): return lax.ppermute(value, axis, pairs)  27.5 us
    ppermute x8, waiting for transfers between devices, neighbour(): return lax.ppermute(value, axis, pairs)  15.4 us
    all_to_all x1, starting transfers between devices, shards(): gathered = lax.all_to_all(pieces, ('gx', 'gy'), 0, 0, tiled=True)  10.4 us
    pallas_call x3, Pallas kernels, second_step(): pl.pallas_call(functools.partial(step_kernel, kind), in_specs=in_specs, o...  7.81 us
    pallas_call x1, Pallas kernels, first_step(): pl.pallas_call(functools.partial(step_kernel, 'first'), in_specs=[pl.Bloc...  7.55 us
    all_to_all x1, starting transfers between devices, shards(): box = lax.all_to_all(shares, 'gx', 0, 0, tiled=True)  5.43 us
    pallas_call x1, Pallas kernels, sections(): pl.pallas_call(functools.partial(sections_kernel, size_x, size_y, columns...  4.11 us
    pallas_call x1, Pallas kernels, contract(): pl.pallas_call(functools.partial(contract_kernel, own, part, nx), in_spec...  1.97 us
  transfers between devices with their start and end apart: 10, of which 4 were waited for; matrix products, arithmetic and copies ran while one was open for 0% of the time, Pallas kernels for 9%

profile of v7, /device:TPU:57, one launch (start us, length us, event | category | flops | bytes accessed | tf_op | source)
XLA Modules:
  0.0 82.5 jit_solution(5196334172975232028)
XLA Ops:
  0.6 0.0 copy-start.1
  0.6 0.0 copy-start
  0.7 4.1 %sections.1 = (f32[1536,128]{1,0:T(8,128)}, f32[3,32,320]{2,1,0:T(8,128)S(1)}, f32[3,24,320]{2,1,0:T(8,128)S(1)}, f32[3,32,320]{2,1,0:T(8,128)S(1)}, f32[3,24,32...) custom-call(f32[3,384,384]{2,1,0:T(8,128)} %refs_0_.2, f32[96,384]{1,0:T(8,128)} %refs_1_.2, ...), custom_call_target="tpu_custom_call" | custom-call | tf_op jit(solution)/shard_map/sections/pallas_call | solution.py:185
  4.8 10.4 %all-to-all-start = ((f32[384,4,128]{2,1,0:T(4,128)}), f32[384,4,128]{2,1,0:T(4,128)S(1)}, u32[]{:S(2)}, u32[]{:S(2)}) async-start(f32[384,4,128]{2,1,0:T(4,128)} %bitcast), calls=%async_computation | async-start | bytes 1572864 | tf_op jit(solution)/shard_map/all_to_all | solution.py:621
  15.2 4.6 %collective-permute-start = (f32[3,32,320]{2,1,0:T(8,128)S(1)}, f32[3,32,320]{2,1,0:T(8,128)S(1)}, u32[]{:S(2)}, u32[]{:S(2)}) collective-permute-start(f32[3,32,320]{2,1,0:T(8,128)S(1)} %get-tuple-element.35), channel_id=1, source_target_pairs={{0,16},{16,32},{32,48},{48,64},{64,80},{80,96},{96,112},{1,17},{17... | collective-permute-start | bytes 368648 | tf_op jit(solution)/shard_map/ppermute | solution.py:19
  19.8 2.5 %collective-permute-start.1 = (f32[3,24,320]{2,1,0:T(8,128)S(1)}, f32[3,24,320]{2,1,0:T(8,128)S(1)}, u32[]{:S(2)}, u32[]{:S(2)}) collective-permute-start(f32[3,24,320]{2,1,0:T(8,128)S(1)} %get-tuple-element.36), channel_id=1, source_target_pairs={{0,1},{1,2},{2,3},{3,4},{4,5},{5,6},{6,7},{7,8},{8,9},{9,10},{10,1... | collective-permute-start | bytes 276488 | tf_op jit(solution)/shard_map/ppermute | solution.py:19
  22.3 5.4 %collective-permute-done.1.refs_5_.refs_7_ = f32[3,24,320]{2,1,0:T(8,128)S(1)} collective-permute-done((f32[3,24,320]{2,1,0:T(8,128)S(1)}, f32[3,24,320]{2,1,0:T(8,128)S(1)}, u32[]{:S(2)}, u32[]{:S(2)}) %collective-permute-start.1) | collective-permute-done | bytes 92192 | tf_op jit(solution)/shard_map/ppermute | solution.py:19
  27.8 1.5 %collective-permute-done.refs_4_.refs_6_ = f32[3,32,320]{2,1,0:T(8,128)S(1)} collective-permute-done((f32[3,32,320]{2,1,0:T(8,128)S(1)}, f32[3,32,320]{2,1,0:T(8,128)S(1)}, u32[]{:S(2)}, u32[]{:S(2)}) %collective-permute-start) | collective-permute-done | bytes 122912 | tf_op jit(solution)/shard_map/ppermute | solution.py:19
  29.3 0.0 all-to-all-done
  29.3 0.0 copy-done.1
  29.3 0.0 copy-done
  29.3 2.0 %contract.1 = (f32[8,104,128]{2,1,0:T(8,128)}, f32[3,32,320]{2,1,0:T(8,128)S(1)}, f32[3,24,320]{2,1,0:T(8,128)S(1)}) custom-call(s32[3]{0:T(128)S(1)} %copy-done.1, f32[64,384]{1,0:T(8,128)S(1)} %copy-done, f32[1536,128]{1,0:T(8,128)S(1)} %bitcast.2, f32[3,32,320]{2,1,0:T(8,128)S(1)} %get-tuple-element.38.refs_0_, ...), custom_call_target="tpu_custom_call" | custom-call | tf_op jit(solution)/shard_map/contract/pallas_call | solution.py:241
  31.3 5.4 %all-to-all-start.1 = ((f32[8,104,128]{2,1,0:T(8,128)}), f32[8,104,128]{2,1,0:T(8,128)S(1)}, u32[]{:S(2)}, u32[]{:S(2)}) async-start(f32[8,104,128]{2,1,0:T(8,128)} %get-tuple-element.42), calls=%async_computation.1 | async-start | bytes 851968 | tf_op jit(solution)/shard_map/all_to_all | solution.py:629
  36.7 4.6 %collective-permute-start.2 = (f32[3,32,320]{2,1,0:T(8,128)S(1)}, f32[3,32,320]{2,1,0:T(8,128)S(1)}, u32[]{:S(2)}, u32[]{:S(2)}) collective-permute-start(f32[3,32,320]{2,1,0:T(8,128)S(1)} %get-tuple-element.43), channel_id=1, source_target_pairs={{16,0},{32,16},{48,32},{64,48},{80,64},{96,80},{112,96},{17,1},{33... | collective-permute-start | bytes 368648 | tf_op jit(solution)/shard_map/ppermute | solution.py:19
  41.3 3.4 %collective-permute-start.3 = (f32[3,24,320]{2,1,0:T(8,128)S(1)}, f32[3,24,320]{2,1,0:T(8,128)S(1)}, u32[]{:S(2)}, u32[]{:S(2)}) collective-permute-start(f32[3,24,320]{2,1,0:T(8,128)S(1)} %get-tuple-element.44), channel_id=1, source_target_pairs={{1,0},{2,1},{3,2},{4,3},{5,4},{6,5},{7,6},{8,7},{9,8},{10,9},{11,1... | collective-permute-start | bytes 276488 | tf_op jit(solution)/shard_map/ppermute | solution.py:19
  44.8 5.7 %collective-permute-done.3.refs_9_ = f32[3,24,320]{2,1,0:T(8,128)S(1)} collective-permute-done((f32[3,24,320]{2,1,0:T(8,128)S(1)}, f32[3,24,320]{2,1,0:T(8,128)S(1)}, u32[]{:S(2)}, u32[]{:S(2)}) %collective-permute-start.3) | collective-permute-done | bytes 92192 | tf_op jit(solution)/shard_map/ppermute | solution.py:19
  50.5 0.0 collective-permute-done.2.refs_8_
  50.5 0.0 all-to-all-done.1.box
  50.5 7.6 %first_step.1 = (f32[6,25,32,320]{3,2,1,0:T(8,128)S(1)}, f32[3,25,32,320]{3,2,1,0:T(8,128)S(1)}, f32[4,25,32,320]{3,2,1,0:T(8,128)S(1)}, f32[4,32,320]{2,1,0:T(8...) custom-call(f32[6,24,32,320]{3,2,1,0:T(8,128)} %refs_0_.3, ...), custom_call_target="tpu_custom_call" | custom-call | flops 24576000 | bytes 12779520 | tf_op jit(solution)/shard_map/first_step/pallas_call | solution.py:549
  58.0 2.8 %collective-permute-start.4 = (f32[4,32,320]{2,1,0:T(8,128)S(1)}, f32[4,32,320]{2,1,0:T(8,128)S(1)}, u32[]{:S(2)}, u32[]{:S(2)}) collective-permute-start(f32[4,32,320]{2,1,0:T(8,128)S(1)} %get-tuple-element.52), channel_id=1, source_target_pairs={{0,16},{16,32},{32,48},{48,64},{64,80},{80,96},{96,112},{1,17},{17... | collective-permute-start | bytes 491528 | tf_op jit(solution)/shard_map/ppermute | solution.py:19
  60.9 4.2 %collective-permute-start.5 = (f32[4,24,320]{2,1,0:T(8,128)S(1)}, f32[4,24,320]{2,1,0:T(8,128)S(1)}, u32[]{:S(2)}, u32[]{:S(2)}) collective-permute-start(f32[4,24,320]{2,1,0:T(8,128)S(1)} %get-tuple-element.53), channel_id=1, source_target_pairs={{0,1},{1,2},{2,3},{3,4},{4,5},{5,6},{6,7},{7,8},{8,9},{9,10},{10,1... | collective-permute-start | bytes 368648 | tf_op jit(solution)/shard_map/ppermute | solution.py:19
  65.1 1.5 %place.1 = (f32[25,32,320]{2,1,0:T(8,128)S(1)}, f32[32,320]{1,0:T(8,128)S(1)}, f32[24,320]{1,0:T(8,128)S(1)}) custom-call(s32[3]{0:T(128)S(1)} %copy-done.1, f32[8,104,128]{2,1,0:T(8,128)S(1)} %all-to-all-done.1.box, f32[4,25,32,320]{3,2,1,0:T(8,128)S(1)} %get-tuple-element.49.cells.refs_2_), custom_call_target="tpu_custom_call" | custom-call | tf_op jit(solution)/shard_map/place/pallas_call | solution.py:294
  66.5 2.1 %second_velocity.1.refs_1_ = f32[3,25,32,320]{3,2,1,0:T(8,128)S(1)} custom-call(f32[6,25,32,320]{3,2,1,0:T(8,128)S(1)} %get-tuple-element.47.refs_0_, f32[3,25,32,320]{3,2,1,0:T(8,128)S(1)} %get-tuple-element.48.refs_1_, f32[4,25,32,320]{3,2,1,0:T(8,128)S(1)} %get-tuple-element.49.cells.refs_2_, ...), custom_call_target="tpu_custom_call", output_to_operand_aliasing={{}: (1, {})} | custom-call | flops 24576000 | bytes 2949120 | tf_op jit(solution)/shard_map/second_velocity/pallas_call | solution.py:581
  68.6 0.0 collective-permute-done.5.refs_5_
  68.6 0.0 collective-permute-done.4.refs_4_
  68.6 0.1 second_edges.1
  68.8 3.4 %collective-permute-start.6 = (f32[3,32,320]{2,1,0:T(8,128)S(1)}, f32[3,32,320]{2,1,0:T(8,128)S(1)}, u32[]{:S(2)}, u32[]{:S(2)}) collective-permute-start(f32[3,32,320]{2,1,0:T(8,128)S(1)} %get-tuple-element.61.refs_4_), channel_id=1, source_target_pairs={{16,0},{32,16},{48,32},{64,48},{80,64},{96,80},{112,96},{17,1},{33... | collective-permute-start | bytes 368648 | tf_op jit(solution)/shard_map/ppermute | solution.py:19
  72.1 1.9 %collective-permute-start.7 = (f32[3,24,320]{2,1,0:T(8,128)S(1)}, f32[3,24,320]{2,1,0:T(8,128)S(1)}, u32[]{:S(2)}, u32[]{:S(2)}) collective-permute-start(f32[3,24,320]{2,1,0:T(8,128)S(1)} %get-tuple-element.62.refs_5_), channel_id=1, source_target_pairs={{1,0},{2,1},{3,2},{4,3},{5,4},{6,5},{7,6},{8,7},{9,8},{10,9},{11,1... | collective-permute-start | bytes 276488 | tf_op jit(solution)/shard_map/ppermute | solution.py:19
  74.1 3.6 %second_inner.1 = (f32[6,24,32,320]{3,2,1,0:T(8,128)}, f32[6,25,32,320]{3,2,1,0:T(8,128)S(1)}, f32[3,25,32,320]{3,2,1,0:T(8,128)S(1)}, f32[3,24,32,320]{3,2,1,0:T(8,128)}) custom-call(f32[6,25,32,320]{3,2,1,0:T(8,128)S(1)} %get-tuple-element.47.refs_0_, f32[3,25,32,320]{3,2,1,0:T(8,128)S(1)} %second_velocity.1.refs_1_, ...), custom_call_target="tpu_custom_call", output_to_operand_aliasing={{1}: (0, {}), {2}: (1, {})} | custom-call | flops 24576000 | bytes 2949120 | tf_op jit(solution)/shard_map/second_inner/pallas_call | solution.py:581
  77.6 2.7 %collective-permute-done.7.refs_5_ = f32[3,24,320]{2,1,0:T(8,128)S(1)} collective-permute-done((f32[3,24,320]{2,1,0:T(8,128)S(1)}, f32[3,24,320]{2,1,0:T(8,128)S(1)}, u32[]{:S(2)}, u32[]{:S(2)}) %collective-permute-start.7) | collective-permute-done | bytes 92192 | tf_op jit(solution)/shard_map/ppermute | solution.py:19
  80.3 0.0 collective-permute-done.6.refs_4_
  80.3 2.2 %second_outer.1 = (f32[6,24,32,320]{3,2,1,0:T(8,128)}, f32[6,25,32,320]{3,2,1,0:T(8,128)S(1)}, f32[3,25,32,320]{3,2,1,0:T(8,128)S(1)}) custom-call(f32[6,25,32,320]{3,2,1,0:T(8,128)S(1)} %get-tuple-element.64.refs_0_, f32[3,25,32,320]{3,2,1,0:T(8,128)S(1)} %get-tuple-element.65.refs_1_, ...), custom_call_target="tpu_custom_call", output_to_operand_aliasing={{1}: (0, {}), {2}: (1, {}), {0}: (6, {})} | custom-call | flops 24576000 | bytes 2949120 | tf_op jit(solution)/shard_map/second_outer/pallas_call | solution.py:581
Async XLA Ops:
  0.6 28.7 %copy-start.1 = (s32[3]{0:T(128)S(1)}, s32[3]{0:T(128)}, u32[]{:S(2)}) copy-start(s32[3]{0:T(128)} %anchor.3) | copy-start | bytes 40
  0.6 28.7 %copy-start = (f32[64,384]{1,0:T(8,128)S(1)}, f32[64,384]{1,0:T(8,128)}, u32[]{:S(2)}) copy-start(f32[64,384]{1,0:T(8,128)} %weight_x.1) | copy-start | bytes 294916
  4.8 24.5 %all-to-all-start = ((f32[384,4,128]{2,1,0:T(4,128)}), f32[384,4,128]{2,1,0:T(4,128)S(1)}, u32[]{:S(2)}, u32[]{:S(2)}) async-start(f32[384,4,128]{2,1,0:T(4,128)} %bitcast), calls=%async_computation | async-start | bytes 1572864 | tf_op jit(solution)/shard_map/all_to_all | solution.py:621
  15.2 14.1 %collective-permute-start = (f32[3,32,320]{2,1,0:T(8,128)S(1)}, f32[3,32,320]{2,1,0:T(8,128)S(1)}, u32[]{:S(2)}, u32[]{:S(2)}) collective-permute-start(f32[3,32,320]{2,1,0:T(8,128)S(1)} %get-tuple-element.35), channel_id=1, source_target_pairs={{0,16},{16,32},{32,48},{48,64},{64,80},{80,96},{96,112},{1,17},{17... | collective-permute-start | bytes 368648 | tf_op jit(solution)/shard_map/ppermute | solution.py:19
  19.8 8.0 %collective-permute-start.1 = (f32[3,24,320]{2,1,0:T(8,128)S(1)}, f32[3,24,320]{2,1,0:T(8,128)S(1)}, u32[]{:S(2)}, u32[]{:S(2)}) collective-permute-start(f32[3,24,320]{2,1,0:T(8,128)S(1)} %get-tuple-element.36), channel_id=1, source_target_pairs={{0,1},{1,2},{2,3},{3,4},{4,5},{5,6},{6,7},{7,8},{8,9},{9,10},{10,1... | collective-permute-start | bytes 276488 | tf_op jit(solution)/shard_map/ppermute | solution.py:19
  31.3 19.2 %all-to-all-start.1 = ((f32[8,104,128]{2,1,0:T(8,128)}), f32[8,104,128]{2,1,0:T(8,128)S(1)}, u32[]{:S(2)}, u32[]{:S(2)}) async-start(f32[8,104,128]{2,1,0:T(8,128)} %get-tuple-element.42), calls=%async_computation.1 | async-start | bytes 851968 | tf_op jit(solution)/shard_map/all_to_all | solution.py:629
  36.7 13.8 %collective-permute-start.2 = (f32[3,32,320]{2,1,0:T(8,128)S(1)}, f32[3,32,320]{2,1,0:T(8,128)S(1)}, u32[]{:S(2)}, u32[]{:S(2)}) collective-permute-start(f32[3,32,320]{2,1,0:T(8,128)S(1)} %get-tuple-element.43), channel_id=1, source_target_pairs={{16,0},{32,16},{48,32},{64,48},{80,64},{96,80},{112,96},{17,1},{33... | collective-permute-start | bytes 368648 | tf_op jit(solution)/shard_map/ppermute | solution.py:19
  41.3 9.2 %collective-permute-start.3 = (f32[3,24,320]{2,1,0:T(8,128)S(1)}, f32[3,24,320]{2,1,0:T(8,128)S(1)}, u32[]{:S(2)}, u32[]{:S(2)}) collective-permute-start(f32[3,24,320]{2,1,0:T(8,128)S(1)} %get-tuple-element.44), channel_id=1, source_target_pairs={{1,0},{2,1},{3,2},{4,3},{5,4},{6,5},{7,6},{8,7},{9,8},{10,9},{11,1... | collective-permute-start | bytes 276488 | tf_op jit(solution)/shard_map/ppermute | solution.py:19
  58.0 10.6 %collective-permute-start.4 = (f32[4,32,320]{2,1,0:T(8,128)S(1)}, f32[4,32,320]{2,1,0:T(8,128)S(1)}, u32[]{:S(2)}, u32[]{:S(2)}) collective-permute-start(f32[4,32,320]{2,1,0:T(8,128)S(1)} %get-tuple-element.52), channel_id=1, source_target_pairs={{0,16},{16,32},{32,48},{48,64},{64,80},{80,96},{96,112},{1,17},{17... | collective-permute-start | bytes 491528 | tf_op jit(solution)/shard_map/ppermute | solution.py:19
  60.9 7.8 %collective-permute-start.5 = (f32[4,24,320]{2,1,0:T(8,128)S(1)}, f32[4,24,320]{2,1,0:T(8,128)S(1)}, u32[]{:S(2)}, u32[]{:S(2)}) collective-permute-start(f32[4,24,320]{2,1,0:T(8,128)S(1)} %get-tuple-element.53), channel_id=1, source_target_pairs={{0,1},{1,2},{2,3},{3,4},{4,5},{5,6},{6,7},{7,8},{8,9},{9,10},{10,1... | collective-permute-start | bytes 368648 | tf_op jit(solution)/shard_map/ppermute | solution.py:19
  68.8 11.6 %collective-permute-start.6 = (f32[3,32,320]{2,1,0:T(8,128)S(1)}, f32[3,32,320]{2,1,0:T(8,128)S(1)}, u32[]{:S(2)}, u32[]{:S(2)}) collective-permute-start(f32[3,32,320]{2,1,0:T(8,128)S(1)} %get-tuple-element.61.refs_4_), channel_id=1, source_target_pairs={{16,0},{32,16},{48,32},{64,48},{80,64},{96,80},{112,96},{17,1},{33... | collective-permute-start | bytes 368648 | tf_op jit(solution)/shard_map/ppermute | solution.py:19
  72.1 8.2 %collective-permute-start.7 = (f32[3,24,320]{2,1,0:T(8,128)S(1)}, f32[3,24,320]{2,1,0:T(8,128)S(1)}, u32[]{:S(2)}, u32[]{:S(2)}) collective-permute-start(f32[3,24,320]{2,1,0:T(8,128)S(1)} %get-tuple-element.62.refs_5_), channel_id=1, source_target_pairs={{1,0},{2,1},{3,2},{4,3},{5,4},{6,5},{7,6},{8,7},{9,8},{10,9},{11,1... | collective-permute-start | bytes 276488 | tf_op jit(solution)/shard_map/ppermute | solution.py:19

commit v8 on v7

--- a/solution.py
+++ b/solution.py
@@ -449,9 +449,6 @@
                 values.append(decay * (stress[c, x + 1, here] + shear * (a + b)))
             for c in range(6):
                 stress[c, x + 1, here] = values[c]
-            if not with_source and r == ny // strip - 1:
-                for c, which in enumerate((3, 1, 5)):
-                    last_rows[c, pl.ds(x, 1)] = values[which][strip - 1 :]
             below = rolled
 
     def one_chunk(n, _):
@@ -518,6 +515,8 @@
         for c, which in enumerate((0, 3, 4)):
             last_plane[c] = stress[which, nx]
         last_plane[3] = cells[3, nx - 1]
+        for c, which in enumerate((3, 1, 5)):
+            last_rows[c] = stress[which, 1:, ny - 1]
         last_rows[3] = cells[3, :nx, ny - 1]
         partial_velocity(
             [stress[c, 1] for c in range(6)],

time: 83 us -> 83 us (level)
  no operation moved by 1% of the time
where the time goes in v8:
time: 83 us; the launch traced here: 82.5 us
  starting transfers between devices  43.3 us (52%)
  Pallas kernels  23 us (28%)
  waiting for transfers between devices  15.4 us (19%)
    ppermute x8, starting transfers between devices, neighbour(): return lax.ppermute(value, axis, pairs)  27.5 us
    ppermute x8, waiting for transfers between devices, neighbour(): return lax.ppermute(value, axis, pairs)  15.4 us
    all_to_all x1, starting transfers between devices, shards(): gathered = lax.all_to_all(pieces, ('gx', 'gy'), 0, 0, tiled=True)  10.4 us
    pallas_call x3, Pallas kernels, second_step(): pl.pallas_call(functools.partial(step_kernel, kind), in_specs=in_specs, o...  7.81 us
    pallas_call x1, Pallas kernels, first_step(): pl.pallas_call(functools.partial(step_kernel, 'first'), in_specs=[pl.Bloc...  7.52 us
    all_to_all x1, starting transfers between devices, shards(): box = lax.all_to_all(shares, 'gx', 0, 0, tiled=True)  5.43 us
    pallas_call x1, Pallas kernels, sections(): pl.pallas_call(functools.partial(sections_kernel, size_x, size_y, columns...  4.11 us
    pallas_call x1, Pallas kernels, contract(): pl.pallas_call(functools.partial(contract_kernel, own, part, nx), in_spec...  1.97 us
  transfers between devices with their start and end apart: 10, of which 4 were waited for; matrix products, arithmetic and copies ran while one was open for 0% of the time, Pallas kernels for 9%

profile of v8, /device:TPU:57, one launch (start us, length us, event | category | flops | bytes accessed | tf_op | source)
XLA Modules:
  0.0 82.5 jit_solution(9304184778895048383)
XLA Ops:
  0.6 0.0 copy-start.1
  0.6 0.0 copy-start
  0.7 4.1 %sections.1 = (f32[1536,128]{1,0:T(8,128)}, f32[3,32,320]{2,1,0:T(8,128)S(1)}, f32[3,24,320]{2,1,0:T(8,128)S(1)}, f32[3,32,320]{2,1,0:T(8,128)S(1)}, f32[3,24,32...) custom-call(f32[3,384,384]{2,1,0:T(8,128)} %refs_0_.2, f32[96,384]{1,0:T(8,128)} %refs_1_.2, ...), custom_call_target="tpu_custom_call" | custom-call | tf_op jit(solution)/shard_map/sections/pallas_call | solution.py:185
  4.8 10.4 %all-to-all-start = ((f32[384,4,128]{2,1,0:T(4,128)}), f32[384,4,128]{2,1,0:T(4,128)S(1)}, u32[]{:S(2)}, u32[]{:S(2)}) async-start(f32[384,4,128]{2,1,0:T(4,128)} %bitcast), calls=%async_computation | async-start | bytes 1572864 | tf_op jit(solution)/shard_map/all_to_all | solution.py:620
  15.2 4.6 %collective-permute-start = (f32[3,32,320]{2,1,0:T(8,128)S(1)}, f32[3,32,320]{2,1,0:T(8,128)S(1)}, u32[]{:S(2)}, u32[]{:S(2)}) collective-permute-start(f32[3,32,320]{2,1,0:T(8,128)S(1)} %get-tuple-element.35), channel_id=1, source_target_pairs={{0,16},{16,32},{32,48},{48,64},{64,80},{80,96},{96,112},{1,17},{17... | collective-permute-start | bytes 368648 | tf_op jit(solution)/shard_map/ppermute | solution.py:19
  19.8 2.5 %collective-permute-start.1 = (f32[3,24,320]{2,1,0:T(8,128)S(1)}, f32[3,24,320]{2,1,0:T(8,128)S(1)}, u32[]{:S(2)}, u32[]{:S(2)}) collective-permute-start(f32[3,24,320]{2,1,0:T(8,128)S(1)} %get-tuple-element.36), channel_id=1, source_target_pairs={{0,1},{1,2},{2,3},{3,4},{4,5},{5,6},{6,7},{7,8},{8,9},{9,10},{10,1... | collective-permute-start | bytes 276488 | tf_op jit(solution)/shard_map/ppermute | solution.py:19
  22.3 5.4 %collective-permute-done.1.refs_5_.refs_7_ = f32[3,24,320]{2,1,0:T(8,128)S(1)} collective-permute-done((f32[3,24,320]{2,1,0:T(8,128)S(1)}, f32[3,24,320]{2,1,0:T(8,128)S(1)}, u32[]{:S(2)}, u32[]{:S(2)}) %collective-permute-start.1) | collective-permute-done | bytes 92192 | tf_op jit(solution)/shard_map/ppermute | solution.py:19
  27.8 1.5 %collective-permute-done.refs_4_.refs_6_ = f32[3,32,320]{2,1,0:T(8,128)S(1)} collective-permute-done((f32[3,32,320]{2,1,0:T(8,128)S(1)}, f32[3,32,320]{2,1,0:T(8,128)S(1)}, u32[]{:S(2)}, u32[]{:S(2)}) %collective-permute-start) | collective-permute-done | bytes 122912 | tf_op jit(solution)/shard_map/ppermute | solution.py:19
  29.3 0.0 all-to-all-done
  29.3 0.0 copy-done.1
  29.3 0.0 copy-done
  29.3 2.0 %contract.1 = (f32[8,104,128]{2,1,0:T(8,128)}, f32[3,32,320]{2,1,0:T(8,128)S(1)}, f32[3,24,320]{2,1,0:T(8,128)S(1)}) custom-call(s32[3]{0:T(128)S(1)} %copy-done.1, f32[64,384]{1,0:T(8,128)S(1)} %copy-done, f32[1536,128]{1,0:T(8,128)S(1)} %bitcast.2, f32[3,32,320]{2,1,0:T(8,128)S(1)} %get-tuple-element.38.refs_0_, ...), custom_call_target="tpu_custom_call" | custom-call | tf_op jit(solution)/shard_map/contract/pallas_call | solution.py:241
  31.3 5.4 %all-to-all-start.1 = ((f32[8,104,128]{2,1,0:T(8,128)}), f32[8,104,128]{2,1,0:T(8,128)S(1)}, u32[]{:S(2)}, u32[]{:S(2)}) async-start(f32[8,104,128]{2,1,0:T(8,128)} %get-tuple-element.42), calls=%async_computation.1 | async-start | bytes 851968 | tf_op jit(solution)/shard_map/all_to_all | solution.py:628
  36.7 4.6 %collective-permute-start.2 = (f32[3,32,320]{2,1,0:T(8,128)S(1)}, f32[3,32,320]{2,1,0:T(8,128)S(1)}, u32[]{:S(2)}, u32[]{:S(2)}) collective-permute-start(f32[3,32,320]{2,1,0:T(8,128)S(1)} %get-tuple-element.43), channel_id=1, source_target_pairs={{16,0},{32,16},{48,32},{64,48},{80,64},{96,80},{112,96},{17,1},{33... | collective-permute-start | bytes 368648 | tf_op jit(solution)/shard_map/ppermute | solution.py:19
  41.3 3.4 %collective-permute-start.3 = (f32[3,24,320]{2,1,0:T(8,128)S(1)}, f32[3,24,320]{2,1,0:T(8,128)S(1)}, u32[]{:S(2)}, u32[]{:S(2)}) collective-permute-start(f32[3,24,320]{2,1,0:T(8,128)S(1)} %get-tuple-element.44), channel_id=1, source_target_pairs={{1,0},{2,1},{3,2},{4,3},{5,4},{6,5},{7,6},{8,7},{9,8},{10,9},{11,1... | collective-permute-start | bytes 276488 | tf_op jit(solution)/shard_map/ppermute | solution.py:19
  44.8 5.7 %collective-permute-done.3.refs_9_ = f32[3,24,320]{2,1,0:T(8,128)S(1)} collective-permute-done((f32[3,24,320]{2,1,0:T(8,128)S(1)}, f32[3,24,320]{2,1,0:T(8,128)S(1)}, u32[]{:S(2)}, u32[]{:S(2)}) %collective-permute-start.3) | collective-permute-done | bytes 92192 | tf_op jit(solution)/shard_map/ppermute | solution.py:19
  50.5 0.0 collective-permute-done.2.refs_8_
  50.5 0.0 all-to-all-done.1.box
  50.5 7.5 %first_step.1 = (f32[6,25,32,320]{3,2,1,0:T(8,128)S(1)}, f32[3,25,32,320]{3,2,1,0:T(8,128)S(1)}, f32[4,25,32,320]{3,2,1,0:T(8,128)S(1)}, f32[4,32,320]{2,1,0:T(8...) custom-call(f32[6,24,32,320]{3,2,1,0:T(8,128)} %refs_0_.3, ...), custom_call_target="tpu_custom_call" | custom-call | flops 24576000 | bytes 12779520 | tf_op jit(solution)/shard_map/first_step/pallas_call | solution.py:548
  58.0 2.8 %collective-permute-start.4 = (f32[4,32,320]{2,1,0:T(8,128)S(1)}, f32[4,32,320]{2,1,0:T(8,128)S(1)}, u32[]{:S(2)}, u32[]{:S(2)}) collective-permute-start(f32[4,32,320]{2,1,0:T(8,128)S(1)} %get-tuple-element.52), channel_id=1, source_target_pairs={{0,16},{16,32},{32,48},{48,64},{64,80},{80,96},{96,112},{1,17},{17... | collective-permute-start | bytes 491528 | tf_op jit(solution)/shard_map/ppermute | solution.py:19
  60.8 4.2 %collective-permute-start.5 = (f32[4,24,320]{2,1,0:T(8,128)S(1)}, f32[4,24,320]{2,1,0:T(8,128)S(1)}, u32[]{:S(2)}, u32[]{:S(2)}) collective-permute-start(f32[4,24,320]{2,1,0:T(8,128)S(1)} %get-tuple-element.53), channel_id=1, source_target_pairs={{0,1},{1,2},{2,3},{3,4},{4,5},{5,6},{6,7},{7,8},{8,9},{9,10},{10,1... | collective-permute-start | bytes 368648 | tf_op jit(solution)/shard_map/ppermute | solution.py:19
  65.0 1.5 %place.1 = (f32[25,32,320]{2,1,0:T(8,128)S(1)}, f32[32,320]{1,0:T(8,128)S(1)}, f32[24,320]{1,0:T(8,128)S(1)}) custom-call(s32[3]{0:T(128)S(1)} %copy-done.1, f32[8,104,128]{2,1,0:T(8,128)S(1)} %all-to-all-done.1.box, f32[4,25,32,320]{3,2,1,0:T(8,128)S(1)} %get-tuple-element.49.cells.refs_2_), custom_call_target="tpu_custom_call" | custom-call | tf_op jit(solution)/shard_map/place/pallas_call | solution.py:294
  66.5 2.1 %second_velocity.1.refs_1_ = f32[3,25,32,320]{3,2,1,0:T(8,128)S(1)} custom-call(f32[6,25,32,320]{3,2,1,0:T(8,128)S(1)} %get-tuple-element.47.refs_0_, f32[3,25,32,320]{3,2,1,0:T(8,128)S(1)} %get-tuple-element.48.refs_1_, f32[4,25,32,320]{3,2,1,0:T(8,128)S(1)} %get-tuple-element.49.cells.refs_2_, ...), custom_call_target="tpu_custom_call", output_to_operand_aliasing={{}: (1, {})} | custom-call | flops 24576000 | bytes 2949120 | tf_op jit(solution)/shard_map/second_velocity/pallas_call | solution.py:580
  68.6 0.0 collective-permute-done.5.refs_5_
  68.6 0.0 collective-permute-done.4.refs_4_
  68.6 0.1 second_edges.1
  68.7 3.4 %collective-permute-start.6 = (f32[3,32,320]{2,1,0:T(8,128)S(1)}, f32[3,32,320]{2,1,0:T(8,128)S(1)}, u32[]{:S(2)}, u32[]{:S(2)}) collective-permute-start(f32[3,32,320]{2,1,0:T(8,128)S(1)} %get-tuple-element.61.refs_4_), channel_id=1, source_target_pairs={{16,0},{32,16},{48,32},{64,48},{80,64},{96,80},{112,96},{17,1},{33... | collective-permute-start | bytes 368648 | tf_op jit(solution)/shard_map/ppermute | solution.py:19
  72.1 1.9 %collective-permute-start.7 = (f32[3,24,320]{2,1,0:T(8,128)S(1)}, f32[3,24,320]{2,1,0:T(8,128)S(1)}, u32[]{:S(2)}, u32[]{:S(2)}) collective-permute-start(f32[3,24,320]{2,1,0:T(8,128)S(1)} %get-tuple-element.62.refs_5_), channel_id=1, source_target_pairs={{1,0},{2,1},{3,2},{4,3},{5,4},{6,5},{7,6},{8,7},{9,8},{10,9},{11,1... | collective-permute-start | bytes 276488 | tf_op jit(solution)/shard_map/ppermute | solution.py:19
  74.0 3.6 %second_inner.1 = (f32[6,24,32,320]{3,2,1,0:T(8,128)}, f32[6,25,32,320]{3,2,1,0:T(8,128)S(1)}, f32[3,25,32,320]{3,2,1,0:T(8,128)S(1)}, f32[3,24,32,320]{3,2,1,0:T(8,128)}) custom-call(f32[6,25,32,320]{3,2,1,0:T(8,128)S(1)} %get-tuple-element.47.refs_0_, f32[3,25,32,320]{3,2,1,0:T(8,128)S(1)} %second_velocity.1.refs_1_, ...), custom_call_target="tpu_custom_call", output_to_operand_aliasing={{1}: (0, {}), {2}: (1, {})} | custom-call | flops 24576000 | bytes 2949120 | tf_op jit(solution)/shard_map/second_inner/pallas_call | solution.py:580
  77.6 2.7 %collective-permute-done.7.refs_5_ = f32[3,24,320]{2,1,0:T(8,128)S(1)} collective-permute-done((f32[3,24,320]{2,1,0:T(8,128)S(1)}, f32[3,24,320]{2,1,0:T(8,128)S(1)}, u32[]{:S(2)}, u32[]{:S(2)}) %collective-permute-start.7) | collective-permute-done | bytes 92192 | tf_op jit(solution)/shard_map/ppermute | solution.py:19
  80.3 0.0 collective-permute-done.6.refs_4_
  80.3 2.2 %second_outer.1 = (f32[6,24,32,320]{3,2,1,0:T(8,128)}, f32[6,25,32,320]{3,2,1,0:T(8,128)S(1)}, f32[3,25,32,320]{3,2,1,0:T(8,128)S(1)}) custom-call(f32[6,25,32,320]{3,2,1,0:T(8,128)S(1)} %get-tuple-element.64.refs_0_, f32[3,25,32,320]{3,2,1,0:T(8,128)S(1)} %get-tuple-element.65.refs_1_, ...), custom_call_target="tpu_custom_call", output_to_operand_aliasing={{1}: (0, {}), {2}: (1, {}), {0}: (6, {})} | custom-call | flops 24576000 | bytes 2949120 | tf_op jit(solution)/shard_map/second_outer/pallas_call | solution.py:580
Async XLA Ops:
  0.6 28.7 %copy-start.1 = (s32[3]{0:T(128)S(1)}, s32[3]{0:T(128)}, u32[]{:S(2)}) copy-start(s32[3]{0:T(128)} %anchor.3) | copy-start | bytes 40
  0.6 28.7 %copy-start = (f32[64,384]{1,0:T(8,128)S(1)}, f32[64,384]{1,0:T(8,128)}, u32[]{:S(2)}) copy-start(f32[64,384]{1,0:T(8,128)} %weight_x.1) | copy-start | bytes 294916
  4.8 24.5 %all-to-all-start = ((f32[384,4,128]{2,1,0:T(4,128)}), f32[384,4,128]{2,1,0:T(4,128)S(1)}, u32[]{:S(2)}, u32[]{:S(2)}) async-start(f32[384,4,128]{2,1,0:T(4,128)} %bitcast), calls=%async_computation | async-start | bytes 1572864 | tf_op jit(solution)/shard_map/all_to_all | solution.py:620
  15.2 14.1 %collective-permute-start = (f32[3,32,320]{2,1,0:T(8,128)S(1)}, f32[3,32,320]{2,1,0:T(8,128)S(1)}, u32[]{:S(2)}, u32[]{:S(2)}) collective-permute-start(f32[3,32,320]{2,1,0:T(8,128)S(1)} %get-tuple-element.35), channel_id=1, source_target_pairs={{0,16},{16,32},{32,48},{48,64},{64,80},{80,96},{96,112},{1,17},{17... | collective-permute-start | bytes 368648 | tf_op jit(solution)/shard_map/ppermute | solution.py:19
  19.8 8.0 %collective-permute-start.1 = (f32[3,24,320]{2,1,0:T(8,128)S(1)}, f32[3,24,320]{2,1,0:T(8,128)S(1)}, u32[]{:S(2)}, u32[]{:S(2)}) collective-permute-start(f32[3,24,320]{2,1,0:T(8,128)S(1)} %get-tuple-element.36), channel_id=1, source_target_pairs={{0,1},{1,2},{2,3},{3,4},{4,5},{5,6},{6,7},{7,8},{8,9},{9,10},{10,1... | collective-permute-start | bytes 276488 | tf_op jit(solution)/shard_map/ppermute | solution.py:19
  31.3 19.2 %all-to-all-start.1 = ((f32[8,104,128]{2,1,0:T(8,128)}), f32[8,104,128]{2,1,0:T(8,128)S(1)}, u32[]{:S(2)}, u32[]{:S(2)}) async-start(f32[8,104,128]{2,1,0:T(8,128)} %get-tuple-element.42), calls=%async_computation.1 | async-start | bytes 851968 | tf_op jit(solution)/shard_map/all_to_all | solution.py:628
  36.7 13.8 %collective-permute-start.2 = (f32[3,32,320]{2,1,0:T(8,128)S(1)}, f32[3,32,320]{2,1,0:T(8,128)S(1)}, u32[]{:S(2)}, u32[]{:S(2)}) collective-permute-start(f32[3,32,320]{2,1,0:T(8,128)S(1)} %get-tuple-element.43), channel_id=1, source_target_pairs={{16,0},{32,16},{48,32},{64,48},{80,64},{96,80},{112,96},{17,1},{33... | collective-permute-start | bytes 368648 | tf_op jit(solution)/shard_map/ppermute | solution.py:19
  41.3 9.2 %collective-permute-start.3 = (f32[3,24,320]{2,1,0:T(8,128)S(1)}, f32[3,24,320]{2,1,0:T(8,128)S(1)}, u32[]{:S(2)}, u32[]{:S(2)}) collective-permute-start(f32[3,24,320]{2,1,0:T(8,128)S(1)} %get-tuple-element.44), channel_id=1, source_target_pairs={{1,0},{2,1},{3,2},{4,3},{5,4},{6,5},{7,6},{8,7},{9,8},{10,9},{11,1... | collective-permute-start | bytes 276488 | tf_op jit(solution)/shard_map/ppermute | solution.py:19
  58.0 10.6 %collective-permute-start.4 = (f32[4,32,320]{2,1,0:T(8,128)S(1)}, f32[4,32,320]{2,1,0:T(8,128)S(1)}, u32[]{:S(2)}, u32[]{:S(2)}) collective-permute-start(f32[4,32,320]{2,1,0:T(8,128)S(1)} %get-tuple-element.52), channel_id=1, source_target_pairs={{0,16},{16,32},{32,48},{48,64},{64,80},{80,96},{96,112},{1,17},{17... | collective-permute-start | bytes 491528 | tf_op jit(solution)/shard_map/ppermute | solution.py:19
  60.8 7.8 %collective-permute-start.5 = (f32[4,24,320]{2,1,0:T(8,128)S(1)}, f32[4,24,320]{2,1,0:T(8,128)S(1)}, u32[]{:S(2)}, u32[]{:S(2)}) collective-permute-start(f32[4,24,320]{2,1,0:T(8,128)S(1)} %get-tuple-element.53), channel_id=1, source_target_pairs={{0,1},{1,2},{2,3},{3,4},{4,5},{5,6},{6,7},{7,8},{8,9},{9,10},{10,1... | collective-permute-start | bytes 368648 | tf_op jit(solution)/shard_map/ppermute | solution.py:19
  68.7 11.6 %collective-permute-start.6 = (f32[3,32,320]{2,1,0:T(8,128)S(1)}, f32[3,32,320]{2,1,0:T(8,128)S(1)}, u32[]{:S(2)}, u32[]{:S(2)}) collective-permute-start(f32[3,32,320]{2,1,0:T(8,128)S(1)} %get-tuple-element.61.refs_4_), channel_id=1, source_target_pairs={{16,0},{32,16},{48,32},{64,48},{80,64},{96,80},{112,96},{17,1},{33... | collective-permute-start | bytes 368648 | tf_op jit(solution)/shard_map/ppermute | solution.py:19
  72.1 8.2 %collective-permute-start.7 = (f32[3,24,320]{2,1,0:T(8,128)S(1)}, f32[3,24,320]{2,1,0:T(8,128)S(1)}, u32[]{:S(2)}, u32[]{:S(2)}) collective-permute-start(f32[3,24,320]{2,1,0:T(8,128)S(1)} %get-tuple-element.62.refs_5_), channel_id=1, source_target_pairs={{1,0},{2,1},{3,2},{4,3},{5,4},{6,5},{7,6},{8,7},{9,8},{10,9},{11,1... | collective-permute-start | bytes 276488 | tf_op jit(solution)/shard_map/ppermute | solution.py:19
